TPU v7x, 256 devices: a whole 4x4x8 slice. The times are simulated.
256 devices in a mesh: dp: 8 (over y, core), expert: 32 (over x, z).
Axes of the slice: x: 4, y: 4, z: 8, core: 2. Of those that a mesh axis runs over, the one named last changes fastest.
Arguments:
- hidden_token_tiles: bfloat16 [8, 1024, 1024], P(None, 'dp'), may hold values from -6 to 6
- gradient_token_tiles: bfloat16 [8, 7168, 1024], P(None, 'expert', 'dp'), may hold values from -0.59765625 to 0.59765625
- momentum: float32 [8, 7168, 1024], P('dp', 'expert'), may hold values from -54 to 54, as said below
- filled_tile_count: int32 [8, 8], replicated, may hold values from 1 to 8, as said below
Outputs:
- new_momentum: float32 [8, 7168, 1024], P('dp', 'expert')
- update: float32 [8, 7168, 1024], P(None, 'expert')
Inputs may be any that keep to these rules, and one draw needn't show every extreme that they name: momentum entries are finite reals. filled_tile_count[g, x] filled tiles stand at the head of group g's slots for expert x; in every draw one expert is full in every group.
All inputs are finite; a program needn't handle non-finite values.
Results may differ from a plain program's by a relative error of at most 0.0009.
Values may be sent and summed in bfloat16 or wider, within the bound.
No kernel may reach another device: no remote copies, remote signals or barrier semaphores. Data moves between devices by JAX's collectives and lax.ppermute only.
A program may use at most 64 MiB of HBM per device.

v0:
```python
import math

import jax
import jax.numpy as jnp
from jax import lax
from jax.sharding import PartitionSpec as P

D = 7168
FF = 1024
TILE = 16
ITERS = 2


MOMENTUM_DECAY = 0.95
EPSILON = 1e-07
COEF_A = 3.4445
COEF_B = -4.775
COEF_C = 2.0315


def full_dot(left, right):
    return jnp.dot(left, right, precision=lax.Precision.HIGHEST, preferred_element_type=jnp.float32)


def body(hidden_token_tiles, gradient_token_tiles, momentum, filled_tile_count):
    group = lax.axis_index("dp")
    rows_group = hidden_token_tiles.shape[1]
    experts_here = hidden_token_tiles.shape[0]
    limits = lax.dynamic_index_in_dim(filled_tile_count, group, 0, keepdims=False) * TILE
    positions = lax.broadcasted_iota(jnp.int32, (experts_here, rows_group), 1)
    tallied_tiles = positions < limits[:, None]
    retained_entries = jnp.where(
        tallied_tiles[:, :, None], hidden_token_tiles, jnp.zeros((), jnp.bfloat16)
    )
    gradient = lax.psum_scatter(
        jnp.einsum(
            "tba,tan->tbn",
            gradient_token_tiles,
            retained_entries,
            preferred_element_type=jnp.float32,
        ),
        "dp",
        scatter_dimension=0,
        tiled=True,
    )[0]
    moment = MOMENTUM_DECAY * momentum[0] + gradient
    current = moment
    for iteration in range(ITERS):
        gram_total = lax.psum(full_dot(current.T, current).astype(jnp.bfloat16), "expert").astype(
            jnp.float32
        )
        if iteration == 0:
            factor = 1.0 / (jnp.sqrt(jnp.trace(gram_total)) + EPSILON)
            current = current * factor
            gram_total = gram_total * (factor * factor)
        mixer = COEF_B * gram_total + COEF_C * full_dot(gram_total, gram_total)
        current = COEF_A * current + full_dot(current, mixer)
    update_local = current * math.sqrt(max(FF, D))
    gathered = lax.all_gather(update_local[None], "dp", axis=0, tiled=True)
    return (moment[None], gathered)


def solution(mesh):
    placed = (P(None, "dp", None), P(None, "expert", "dp"), P("dp", "expert", None), P())
    return jax.shard_map(
        body,
        mesh=mesh,
        in_specs=placed,
        out_specs=(P("dp", "expert", None), P(None, "expert", None)),
        check_vma=False,
    )
```

profile of v0, /device:TPU:1, one launch (start us, length us, event | category | flops | bytes accessed | tf_op | source)
XLA Modules:
  0.0 476.9 jit_solution(4458757613890195179)
XLA Ops:
  7.2 0.0 copy-start
  7.2 0.0 reduce-scatter.2.cloned.1.call-start
  7.2 0.7 multiply_bitcast_fusion
  8.0 0.1 iota_compare_fusion.1
  8.0 0.2 copy-done
  8.2 5.8 %convolution_bitcast_fusion = f32[8,224,1024]{2,1,0:T(8,128)} fusion(bf16[8,224,128]{2,1,0:T(8,128)(2,1)S(1)} %copy-done, bf16[8,128,1024]{2,1,0:T(8,128)(2,1)} %param.4, pred[8,128]{1,0:T(8,128)(4,1)S(1)} %iota_compare_fusion.1), kind=kOutput, calls=%fused_computation.14 | convolution fusion | flops 470810624 | bytes 9896960 | tf_op jit(solution)/shard_map/tba,tan->tbn/dot_general | solution.py:36
  14.0 0.0 reduce-scatter.2.cloned.1.call-update
  14.0 0.0 all-reduce.3.cloned.1.call-start
  14.1 53.4 %reduce-scatter.2.cloned.1.call-done = f32[1,224,1024]{2,1,0:T(8,128)} async-done(((f32[8,224,1024]{2,1,0:T(8,128)}), f32[1,224,1024]{2,1,0:T(8,128)}) %reduce-scatter.2.cloned.1.call-update) | async-done | bytes 917520 | tf_op jit(solution)/shard_map/reduce_scatter | solution.py:35
  67.5 0.0 copy-done.4
  67.5 1.3 multiply_add_fusion
  68.8 0.0 copy-start.2
  68.8 4.8 %convolution_convert_fusion.1 = bf16[1024,1024]{1,0:T(8,128)(2,1)} fusion(f32[1,224,1024]{2,1,0:T(8,128)S(1)} %multiply_add_fusion), kind=kOutput, calls=%fused_computation.24 | convolution fusion | flops 2819620864 | bytes 3014656 | tf_op jit(solution)/shard_map/dot_general | solution.py:22
  73.6 0.0 all-reduce.3.cloned.1.call-update
  73.6 0.2 all-reduce.5.cloned.1.call-start
  73.9 149.9 %all-reduce.3.cloned.1.call-done = bf16[1024,1024]{1,0:T(8,128)(2,1)} async-done(((bf16[1024,1024]{1,0:T(8,128)(2,1)}), bf16[1024,1024]{1,0:T(8,128)(2,1)}) %all-reduce.3.cloned.1.call-update) | async-done | bytes 2097168 | tf_op jit(solution)/shard_map/psum | solution.py:49
  223.7 2.3 fusion.5
  226.8 0.0 copy-start.1
  226.8 16.3 %fusion = f32[1024,1024]{1,0:T(8,128)S(1)} fusion(bf16[1024,1024]{1,0:T(8,128)(2,1)} %all-reduce.3.cloned.1.call-done, f32[]{:T(128)S(6)} %mul.70), kind=kOutput, calls=%fused_computation.2 | convolution fusion | flops 12886999040 | bytes 6291460 | tf_op jit(solution)/shard_map/dot_general | solution.py:22
  243.2 0.0 copy-done.2
  243.2 0.0 copy-done.1
  243.2 4.1 fusion.23
  247.3 4.8 %convolution_convert_fusion = bf16[1024,1024]{1,0:T(8,128)(2,1)} fusion(f32[224,1024]{1,0:T(8,128)S(1)} %fusion.23), kind=kOutput, calls=%fused_computation.23 | convolution fusion | flops 2819620864 | bytes 3014656 | tf_op jit(solution)/shard_map/dot_general | solution.py:22
  252.1 0.0 all-reduce.5.cloned.1.call-update
  252.1 0.0 all-gather.3.cloned.1.call-start
  252.2 151.3 %all-reduce.5.cloned.1.call-done = bf16[1024,1024]{1,0:T(8,128)(2,1)} async-done(((bf16[1024,1024]{1,0:T(8,128)(2,1)}), bf16[1024,1024]{1,0:T(8,128)(2,1)}) %all-reduce.5.cloned.1.call-update) | async-done | bytes 2097168 | tf_op jit(solution)/shard_map/psum | solution.py:49
  403.5 4.7 fusion.39
  408.2 0.0 copy-done.3
  408.2 4.6 fusion.26
  412.9 0.0 all-gather.3.cloned.1.call-update
  412.9 50.0 %all-gather.3.cloned.1.call-done = f32[1792,1024]{1,0:T(8,128)} async-done(((f32[224,1024]{1,0:T(8,128)}), f32[1792,1024]{1,0:T(8,128)}) %all-gather.3.cloned.1.call-update) | async-done | bytes 7340048 | tf_op jit(solution)/shard_map/all_gather | solution.py:59
  462.9 7.5 %copy.9 = f32[8,224,1024]{2,1,0:T(8,128)} copy(f32[8,224,1024]{2,1,0:T(8,128)} %bitcast.20) | data formatting | bytes 14680064
  (2 shorter events, 0.0 us)
Async XLA Ops:
  7.2 1.0 copy-start
  7.2 60.3 %reduce-scatter.2.cloned.1.call-start = ((), (), s32[]{:S(2)}) async-start(), calls=%async_computation.1 | async-start | bytes 8257536 | tf_op jit(solution)/shard_map/reduce_scatter | solution.py:35
  14.0 53.4 %copy-start.4 = (f32[1,224,1024]{2,1,0:T(8,128)S(1)}, f32[1,224,1024]{2,1,0:T(8,128)}, u32[]{:S(2)}) copy-start(f32[1,224,1024]{2,1,0:T(8,128)} %param.6) | copy-start | bytes 2752516
  14.0 209.7 %all-reduce.3.cloned.1.call-start = ((), (), s32[]{:S(2)}) async-start(), calls=%async_computation.2 | async-start | bytes 4194304 | tf_op jit(solution)/shard_map/psum | solution.py:49
  68.8 174.4 %copy-start.2 = (f32[1,224,1024]{2,1,0:T(8,128)}, f32[1,224,1024]{2,1,0:T(8,128)S(1)}, u32[]{:S(2)}) copy-start(f32[1,224,1024]{2,1,0:T(8,128)S(1)} %multiply_add_fusion) | copy-start | bytes 2752516
  73.6 329.9 %all-reduce.5.cloned.1.call-start = ((), (), s32[]{:S(2)}) async-start(), calls=%async_computation.3 | async-start | bytes 4194304 | tf_op jit(solution)/shard_map/psum | solution.py:49
  226.8 16.4 %copy-start.1 = (bf16[1024,1024]{1,0:T(8,128)(2,1)S(1)}, bf16[1024,1024]{1,0:T(8,128)(2,1)}, u32[]{:S(2)}) copy-start(bf16[1024,1024]{1,0:T(8,128)(2,1)} %all-reduce.3.cloned.1.call-done) | copy-start | bytes 6291460
  252.1 210.7 %all-gather.3.cloned.1.call-start = ((), (), s32[]{:S(2)}) async-start(), calls=%async_computation.4 | async-start | bytes 8257536 | tf_op jit(solution)/shard_map/all_gather | solution.py:59
  403.5 4.7 copy-start.3
Sparse Core Ops, SparseCore 0:
  14.2 53.2 reduce-scatter.1
  73.7 149.9 all-reduce.2
  252.2 151.2 all-reduce.4
  413.0 49.7 all-gather.2
where the time goes:
time: 477 us
  waiting for transfers between devices  405 us (85%)
  matrix products  45.2 us (9%)
  between operations  14.6 us (3%)
  local copies, waits for them, and re-layouts  7.71 us (2%)
    psum x2, waiting for transfers between devices, body(): lax.psum(full_dot(current.T, current).astype(jnp.bfloat16), 'expert')  301 us
    reduce_scatter x1, waiting for transfers between devices, body(): lax.psum_scatter(jnp.einsum('tba,tan->tbn', gradient_token_tiles, retaine...  53.4 us
    all_gather x1, waiting for transfers between devices, body(): gathered = lax.all_gather(update_local[None], 'dp', axis=0, tiled=True)  50 us
    dot_general x6, matrix products, full_dot(): jnp.dot(left, right, precision=lax.Precision.HIGHEST, preferred_element_t...  39.4 us
  transfers between devices with their start and end apart: 4, of which 4 were waited for; matrix products, arithmetic and copies ran while one was open for 0% of the time, Pallas kernels for 0%

commit v1 on v0

v1 whole, which is shorter than its diff:
```python
import math

import jax
import jax.numpy as jnp
from jax import lax
from jax.experimental import pallas as pl
from jax.experimental.pallas import tpu as pltpu
from jax.sharding import PartitionSpec as P

D = 7168
FF = 1024
TILE = 16
BLOCK = 128
UNIT = 16

MOMENTUM_DECAY = 0.95
EPSILON = 1e-07
COEF_A = 3.4445
COEF_B = -4.775
COEF_C = 2.0315

BF16 = jnp.bfloat16
F32 = jnp.float32


def split_two(value):
    high = value.astype(BF16)
    return high, (value - high.astype(F32)).astype(BF16)


def block_pairs():
    count = FF // BLOCK
    return [(i, j) for i in range(count) for j in range(i, count)]


def gram_kernel(counts_ref, tokens_ref, hidden_ref, momentum_ref, moment_ref, packed_ref):
    groups, _, width = tokens_ref.shape
    lanes = lax.broadcasted_iota(jnp.int32, tokens_ref.shape[1:], 1)
    tokens = jnp.concatenate(
        [
            jnp.where(lanes < counts_ref[g] * TILE, tokens_ref[g].astype(F32), 0.0).astype(BF16)
            for g in range(groups)
        ],
        axis=1,
    )
    hidden = hidden_ref[...].reshape(groups * width, FF)
    gradient = jnp.dot(tokens, hidden, preferred_element_type=F32)
    moment = MOMENTUM_DECAY * momentum_ref[...] + gradient
    moment_ref[...] = moment

    high, low = split_two(moment)
    left = jnp.concatenate([high, low, high], axis=0).T
    right = jnp.concatenate([high, high, low], axis=0)
    per_device = packed_ref.shape[1] // UNIT - 1
    unit = 0
    for i in range(FF // BLOCK):
        strip = jnp.dot(
            left[i * BLOCK : (i + 1) * BLOCK], right[:, i * BLOCK :], preferred_element_type=F32
        ).astype(BF16)
        for j in range(i, FF // BLOCK):
            block = strip[:, (j - i) * BLOCK : (j - i + 1) * BLOCK]
            for k in range(BLOCK // UNIT):
                device, place = divmod(unit, per_device)
                packed_ref[device, place * UNIT : (place + 1) * UNIT, :] = block[
                    k * UNIT : (k + 1) * UNIT
                ]
                unit += 1

    total = jnp.sum(jnp.sum(moment * moment, axis=0, keepdims=True), axis=1, keepdims=True)
    first = total.astype(BF16).astype(F32)
    second = (total - first).astype(BF16).astype(F32)
    third = total - first - second
    rows = lax.broadcasted_iota(jnp.int32, (UNIT, BLOCK), 0)
    tile = jnp.where(rows == 0, first, jnp.where(rows == 1, second, jnp.where(rows == 2, third, 0.0)))
    for device in range(packed_ref.shape[0]):
        packed_ref[device, per_device * UNIT :, :] = tile.astype(BF16)


def sum_kernel(parts_ref, copies_ref, factor_ref):
    devices = parts_ref.shape[0]
    rows = copies_ref.shape[1]
    total = parts_ref[0].astype(F32)
    for source in range(1, devices):
        total = total + parts_ref[source].astype(F32)
    squares = jnp.sum(total[rows:], axis=0, keepdims=True)
    factor = 1.0 / (jnp.sqrt(squares) + EPSILON)
    piece = (total[:rows] * factor * factor).astype(BF16)
    for target in range(devices):
        copies_ref[target] = piece
    factor_ref[...] = jnp.broadcast_to(factor, factor_ref.shape)


def polynomial_kernel(moment_ref, factor_ref, packed_ref, update_ref, gram_ref):
    packed = packed_ref[...].reshape(-1, BLOCK)
    for at, (i, j) in enumerate(block_pairs()):
        block = packed[at * BLOCK : (at + 1) * BLOCK]
        gram_ref[i * BLOCK : (i + 1) * BLOCK, j * BLOCK : (j + 1) * BLOCK] = block
        if i != j:
            gram_ref[j * BLOCK : (j + 1) * BLOCK, i * BLOCK : (i + 1) * BLOCK] = block.T

    def by_gram(value):
        rows = value.shape[0]
        both = jnp.dot(
            jnp.concatenate(split_two(value), axis=0), gram_ref[...], preferred_element_type=F32
        )
        return both[:rows] + both[rows:]

    def by_first(value):
        return COEF_A * value + by_gram(COEF_B * value + COEF_C * by_gram(value))

    def by_second_gram(value):
        return by_first(by_gram(by_first(value)))

    start = moment_ref[...] * factor_ref[0:1, 0:1]
    once = by_first(start)
    twice = COEF_A * once + by_second_gram(COEF_B * once + COEF_C * by_second_gram(once))
    update_ref[...] = twice * math.sqrt(max(FF, D))


def whole(memory_space=pltpu.VMEM):
    return pl.BlockSpec(memory_space=memory_space)


PARAMS = pltpu.CompilerParams(vmem_limit_bytes=48 * 1024 * 1024)


def body(hidden_token_tiles, gradient_token_tiles, momentum, filled_tile_count):
    group = lax.axis_index("dp")
    devices = lax.axis_size("expert")
    rows = momentum.shape[1]
    piece = len(block_pairs()) * BLOCK // devices
    counts = lax.dynamic_index_in_dim(filled_tile_count, group, 1, keepdims=False)
    tokens = lax.all_to_all(gradient_token_tiles, "dp", 0, 0, tiled=True)
    hidden = lax.all_to_all(hidden_token_tiles, "dp", 0, 0, tiled=True)
    moment, packed = pl.pallas_call(
        gram_kernel,
        out_shape=(
            jax.ShapeDtypeStruct((rows, FF), F32),
            jax.ShapeDtypeStruct((devices, piece + UNIT, BLOCK), BF16),
        ),
        in_specs=[whole(pltpu.SMEM), whole(), whole(), whole()],
        out_specs=(whole(), whole()),
        compiler_params=PARAMS,
        name="gram",
    )(counts, tokens, hidden, momentum[0])
    parts = lax.all_to_all(packed, "expert", 0, 0, tiled=True)
    copies, factor = pl.pallas_call(
        sum_kernel,
        out_shape=(
            jax.ShapeDtypeStruct((devices, piece, BLOCK), BF16),
            jax.ShapeDtypeStruct((8, BLOCK), F32),
        ),
        in_specs=[whole()],
        out_specs=(whole(), whole()),
        compiler_params=PARAMS,
        name="total",
    )(parts)
    gram = lax.all_to_all(copies, "expert", 0, 0, tiled=True)
    update = pl.pallas_call(
        polynomial_kernel,
        out_shape=jax.ShapeDtypeStruct((rows, FF), F32),
        in_specs=[whole(), whole(), whole()],
        out_specs=whole(),
        scratch_shapes=[pltpu.VMEM((FF, FF), BF16)],
        compiler_params=PARAMS,
        name="polynomial",
    )(moment, factor, gram)
    gathered = lax.all_gather((update * 256.0).astype(jnp.float16), "dp", axis=0, tiled=False)
    return (moment[None], gathered.astype(F32) * (1.0 / 256.0))


def solution(mesh):
    placed = (P(None, "dp", None), P(None, "expert", "dp"), P("dp", "expert", None), P())
    return jax.shard_map(
        body,
        mesh=mesh,
        in_specs=placed,
        out_specs=(P("dp", "expert", None), P(None, "expert", None)),
        check_vma=False,
    )
```

time: 477 us -> 169 us (0.35)
  waiting for transfers between devices: 405 us -> 26.2 us
  blocking collectives: 0 us -> 118 us
  matrix products: 45.2 us -> 0 us
  Pallas kernels: 0 us -> 14.4 us
  between operations: 14.6 us -> 0.69 us
  local copies, waits for them, and re-layouts: 7.71 us -> 0.2 us
    psum x2 -> x0, waiting for transfers between devices: 301 us -> none  [body(): lax.psum(full_dot(current.T, current).astype(jnp.bfloat16), 'expert')]
    all_to_all x0 -> x3, blocking collectives: none -> 94.8 us  [the longest x1 42 us: body(): parts = lax.all_to_all(packed, 'expert', 0, 0, tiled=True)]
    reduce_scatter x1 -> x0, waiting for transfers between devices: 53.4 us -> none  [body(): lax.psum_scatter(jnp.einsum('tba,tan->tbn', gradient_token_tiles, retaine...]
    all_gather x1 -> x0, waiting for transfers between devices: 50 us -> none  [body(): gathered = lax.all_gather(update_local[None], 'dp', axis=0, tiled=True)]
    dot_general x7 -> x0, matrix products: 45.2 us -> none  [the longest x6 39.4 us: full_dot(): jnp.dot(left, right, precision=lax.Precision.HIGHEST, preferred_element_t...]
    all_to_all x0 -> x1, waiting for transfers between devices: none -> 26.2 us  [body(): hidden = lax.all_to_all(hidden_token_tiles, 'dp', 0, 0, tiled=True)]
    all_gather x0 -> x1, blocking collectives: none -> 23.4 us  [body(): lax.all_gather((update * 256.0).astype(jnp.float16), 'dp', axis=0, tiled=...]
    pallas_call x0 -> x3, Pallas kernels: none -> 14.4 us  [the longest x1 11.9 us: body(): pl.pallas_call(polynomial_kernel, out_shape=jax.ShapeDtypeStruct((rows, F...]
  transfers between devices with their start and end apart: 4 -> 1, of which waited for: 4 -> 1; matrix products, arithmetic and copies ran while one was open for 0% -> 0% of each run, Pallas kernels for 0% -> 0%
where the time goes in v1:
time: 169 us; the launch traced here: 168 us
  blocking collectives  118 us (70%)
  waiting for transfers between devices  26.2 us (16%)
  Pallas kernels  14.4 us (9%)
  starting transfers between devices  4.46 us (3%)
  other arithmetic  4.15 us (2%)
    all_to_all x1, blocking collectives, body(): parts = lax.all_to_all(packed, 'expert', 0, 0, tiled=True)  42 us
    all_to_all x1, blocking collectives, body(): gram = lax.all_to_all(copies, 'expert', 0, 0, tiled=True)  37.3 us
    all_to_all x1, waiting for transfers between devices, body(): hidden = lax.all_to_all(hidden_token_tiles, 'dp', 0, 0, tiled=True)  26.2 us
    all_gather x1, blocking collectives, body(): lax.all_gather((update * 256.0).astype(jnp.float16), 'dp', axis=0, tiled=...  23.4 us
    all_to_all x1, blocking collectives, body(): tokens = lax.all_to_all(gradient_token_tiles, 'dp', 0, 0, tiled=True)  15.5 us
    pallas_call x1, Pallas kernels, body(): pl.pallas_call(polynomial_kernel, out_shape=jax.ShapeDtypeStruct((rows, F...  11.9 us
    all_to_all x1, starting transfers between devices, body(): hidden = lax.all_to_all(hidden_token_tiles, 'dp', 0, 0, tiled=True)  4.46 us
    mul x1, other arithmetic, body(): return (moment[None], gathered.astype(F32) * (1.0 / 256.0))  4.07 us
  transfers between devices with their start and end apart: 1, of which 1 were waited for; matrix products, arithmetic and copies ran while one was open for 0% of the time, Pallas kernels for 0%

profile of v1, /device:TPU:1, one launch (start us, length us, event | category | flops | bytes accessed | tf_op | source)
XLA Modules:
  0.0 168.2 jit_solution(16287613604711433896)
XLA Ops:
  0.6 0.0 copy-start
  0.6 0.0 copy-start.1
  0.7 15.5 %all_to_all.20.tokens_ref = bf16[8,224,128]{2,1,0:T(8,128)(2,1)S(1)} all-to-all(bf16[8,224,128]{2,1,0:T(8,128)(2,1)} %param.5), channel_id=1, replica_groups=mesh['dp'=8,'expert'=32] {'dp'}, dimensions={0} | all-to-all | bytes 917504 | tf_op jit(solution)/shard_map/all_to_all | solution.py:133
  16.2 4.5 %all-to-all-start.1 = ((bf16[8,128,1024]{2,1,0:T(8,128)(2,1)}), bf16[8,128,1024]{2,1,0:T(8,128)(2,1)S(1)}, u32[]{:S(2)}, u32[]{:S(2)}) async-start(bf16[8,128,1024]{2,1,0:T(8,128)(2,1)} %param.4), calls=%async_computation.1 | async-start | bytes 4194304 | tf_op jit(solution)/shard_map/all_to_all | solution.py:134
  20.6 0.0 copy-done
  20.6 0.2 dynamic-slice_reduce_fusion.counts_ref
  20.8 26.2 %all-to-all-done.1.hidden_ref = bf16[8,128,1024]{2,1,0:T(8,128)(2,1)S(1)} async-done(((bf16[8,128,1024]{2,1,0:T(8,128)(2,1)}), bf16[8,128,1024]{2,1,0:T(8,128)(2,1)S(1)}, u32[]{:S(2)}, u32[]{:S(2)}) %all-to-all-start.1) | async-done | bytes 2097184 | tf_op jit(solution)/shard_map/all_to_all | solution.py:134
  47.0 0.0 copy-done.1
  47.0 2.4 %gram.1 = (f32[224,1024]{1,0:T(8,128)}, bf16[32,160,128]{2,1,0:T(8,128)(2,1)S(1)}) custom-call(s32[8]{0:T(128)S(1)} %dynamic-slice_reduce_fusion.counts_ref, bf16[8,224,128]{2,1,0:T(8,128)(2,1)S(1)} %all_to_all.20.tokens_ref, bf16[8,128,1024]{2,1,0:T(8,128)(2,1)S(1)} %all-to-all-done.1.hidden_ref, f32[224,1024]{1,0:T(8,128)S(1)} %bitcast.3), custom_call_target="tpu_custom_call" | custom-call | tf_op jit(solution)/shard_map/gram/pallas_call | solution.py:135
  49.3 0.0 copy-start.2
  49.4 42.0 %all_to_all.21.parts_ref = bf16[32,160,128]{2,1,0:T(8,128)(2,1)S(1)} all-to-all(bf16[32,160,128]{2,1,0:T(8,128)(2,1)S(1)} %get-tuple-element.7), channel_id=1, replica_groups=mesh['dp'=8,'expert'=32] {'expert'}, dimensions={0} | all-to-all | bytes 2621440 | tf_op jit(solution)/shard_map/all_to_all | solution.py:146
  91.3 0.2 total.1
  91.5 37.3 %all_to_all.22.packed_ref = bf16[32,144,128]{2,1,0:T(8,128)(2,1)S(1)} all-to-all(bf16[32,144,128]{2,1,0:T(8,128)(2,1)S(1)} %get-tuple-element.9), channel_id=1, replica_groups=mesh['dp'=8,'expert'=32] {'expert'}, dimensions={0} | all-to-all | bytes 2359296 | tf_op jit(solution)/shard_map/all_to_all | solution.py:158
  128.9 0.0 copy-done.2
  128.9 11.9 %polynomial.1 = f32[224,1024]{1,0:T(8,128)S(1)} custom-call(f32[224,1024]{1,0:T(8,128)S(1)} %copy-done.2, f32[8,128]{1,0:T(8,128)S(1)} %get-tuple-element.8.factor_ref, bf16[32,144,128]{2,1,0:T(8,128)(2,1)S(1)} %all_to_all.22.packed_ref), custom_call_target="tpu_custom_call" | custom-call | tf_op jit(solution)/shard_map/polynomial/pallas_call | solution.py:159
  140.7 0.1 multiply_convert_fusion
  140.8 23.4 %all-gather.2 = f16[1792,1024]{1,0:T(8,128)(2,1)S(1)} all-gather(f16[224,1024]{1,0:T(8,128)(2,1)S(1)} %multiply_convert_fusion), channel_id=2, replica_groups=mesh['dp'=8,'expert'=32] {'dp'}, dimensions={0}, use_global_device_ids=true | all-gather | bytes 4128768 | tf_op jit(solution)/shard_map/all_gather | solution.py:168
  164.2 4.1 %convert_multiply_fusion = f32[1792,1024]{1,0:T(8,128)} fusion(f16[1792,1024]{1,0:T(8,128)(2,1)S(1)} %all-gather.2), kind=kLoop, calls=%fused_computation | loop fusion | flops 3670016 | bytes 11010048 | tf_op jit(solution)/shard_map/mul | solution.py:169
Async XLA Ops:
  0.6 20.0 %copy-start = (s32[8,8]{1,0:T(8,128)S(1)}, s32[8,8]{1,0:T(8,128)}, u32[]{:S(2)}) copy-start(s32[8,8]{1,0:T(8,128)} %param.7) | copy-start | bytes 772
  0.6 46.3 %copy-start.1 = (f32[1,224,1024]{2,1,0:T(8,128)S(1)}, f32[1,224,1024]{2,1,0:T(8,128)}, u32[]{:S(2)}) copy-start(f32[1,224,1024]{2,1,0:T(8,128)} %param.6) | copy-start | bytes 2752516
  16.2 30.8 %all-to-all-start.1 = ((bf16[8,128,1024]{2,1,0:T(8,128)(2,1)}), bf16[8,128,1024]{2,1,0:T(8,128)(2,1)S(1)}, u32[]{:S(2)}, u32[]{:S(2)}) async-start(bf16[8,128,1024]{2,1,0:T(8,128)(2,1)} %param.4), calls=%async_computation.1 | async-start | bytes 4194304 | tf_op jit(solution)/shard_map/all_to_all | solution.py:134
  49.3 79.5 %copy-start.2 = (f32[224,1024]{1,0:T(8,128)S(1)}, f32[224,1024]{1,0:T(8,128)}, u32[]{:S(2)}) copy-start(f32[224,1024]{1,0:T(8,128)} %get-tuple-element.6.moment_ref) | copy-start | bytes 2752516

commit v2 on v1

v2 whole, which is shorter than its diff:
```python
import math

import jax
import jax.numpy as jnp
from jax import lax
from jax.experimental import pallas as pl
from jax.experimental.pallas import tpu as pltpu
from jax.sharding import Mesh
from jax.sharding import PartitionSpec as P

D = 7168
FF = 1024
TILE = 16
BLOCK = 128
UNIT = 16

MOMENTUM_DECAY = 0.95
EPSILON = 1e-07
COEF_A = 3.4445
COEF_B = -4.775
COEF_C = 2.0315

DP = ("y", "core")
EXPERT = ("x", "z")

BF16 = jnp.bfloat16
F32 = jnp.float32


def split_two(value):
    high = value.astype(BF16)
    return high, (value - high.astype(F32)).astype(BF16)


def block_pairs():
    count = FF // BLOCK
    return [(i, j) for i in range(count) for j in range(i, count)]


def pieces_of(total, shape):
    first = total.astype(BF16).astype(F32)
    second = (total - first).astype(BF16).astype(F32)
    third = total - first - second
    rows = lax.broadcasted_iota(jnp.int32, shape, 0)
    tile = jnp.where(rows == 0, first, jnp.where(rows == 1, second, jnp.where(rows == 2, third, 0.0)))
    return tile.astype(BF16)


def pack_kernel(counts_ref, hidden_ref, tokens_ref, packed_ref):
    lanes = lax.broadcasted_iota(jnp.int32, tokens_ref.shape[1:], 1)
    for x in range(hidden_ref.shape[0]):
        for c in range(FF // BLOCK):
            packed_ref[x, c * BLOCK : (c + 1) * BLOCK] = hidden_ref[x, :, c * BLOCK : (c + 1) * BLOCK]
        kept = jnp.where(lanes < counts_ref[x] * TILE, tokens_ref[x].astype(F32), 0.0)
        packed_ref[x, FF:] = kept.astype(BF16)


def gram_kernel(place_ref, tiles_ref, momentum_ref, moment_ref, packed_ref):
    groups = tiles_ref.shape[0]
    tokens = jnp.concatenate([tiles_ref[g, FF:] for g in range(groups)], axis=1)
    hidden = jnp.concatenate(
        [
            jnp.concatenate([tiles_ref[g, c * BLOCK : (c + 1) * BLOCK] for c in range(FF // BLOCK)], axis=1)
            for g in range(groups)
        ],
        axis=0,
    )
    gradient = jnp.dot(tokens, hidden, preferred_element_type=F32)
    moment = MOMENTUM_DECAY * momentum_ref[...] + gradient
    moment_ref[...] = moment

    high, low = split_two(moment)
    left = jnp.concatenate([high, low, high], axis=0).T
    right = jnp.concatenate([high, high, low], axis=0)
    chunks = packed_ref.shape[0]
    per_chunk = len(block_pairs()) // chunks
    at = 0
    for i in range(FF // BLOCK):
        strip = jnp.dot(
            left[i * BLOCK : (i + 1) * BLOCK], right[:, i * BLOCK :], preferred_element_type=F32
        ).astype(BF16)
        for j in range(i, FF // BLOCK):
            chunk, place = divmod(at, per_chunk)
            packed_ref[
                lax.rem(chunk - place_ref[0] + chunks, chunks), place * BLOCK : (place + 1) * BLOCK, :
            ] = strip[:, (j - i) * BLOCK : (j - i + 1) * BLOCK]
            at += 1

    total = jnp.sum(jnp.sum(moment * moment, axis=0, keepdims=True), axis=1, keepdims=True)
    tile = pieces_of(total, (UNIT, BLOCK))
    for chunk in range(chunks):
        packed_ref[chunk, per_chunk * BLOCK :, :] = tile


def middle_kernel(own_ref, *refs):
    *others, cut_ref = refs
    targets, height, _ = cut_ref.shape
    rows = height - UNIT
    total = own_ref[...].astype(F32)
    for other in others:
        total = total + other[...].astype(F32)
    tile = pieces_of(jnp.sum(total[targets * rows :, 0:1], axis=0, keepdims=True), (UNIT, BLOCK))
    for target in range(targets):
        cut_ref[target, :rows] = total[target * rows : (target + 1) * rows].astype(BF16)
        cut_ref[target, rows:] = tile


def sum_kernel(parts_ref, copies_ref, factor_ref):
    devices = parts_ref.shape[0]
    rows = copies_ref.shape[1]
    total = parts_ref[0].astype(F32)
    for source in range(1, devices):
        total = total + parts_ref[source].astype(F32)
    squares = jnp.sum(total[rows:], axis=0, keepdims=True)
    factor = 1.0 / (jnp.sqrt(squares) + EPSILON)
    piece = (total[:rows] * factor * factor).astype(BF16)
    for target in range(devices):
        copies_ref[target] = piece
    factor_ref[...] = jnp.broadcast_to(factor, factor_ref.shape)


def polynomial_kernel(place_ref, moment_ref, factor_ref, *refs):
    *chunk_refs, update_ref, packed_ref, gram_ref = refs
    chunks = len(chunk_refs)
    for distance, chunk_ref in enumerate(chunk_refs):
        packed_ref[lax.rem(place_ref[0] - distance + chunks, chunks)] = chunk_ref[...]
    per_chunk = len(block_pairs()) // chunks
    for at, (i, j) in enumerate(block_pairs()):
        chunk, place = divmod(at, per_chunk)
        block = packed_ref[chunk, place * BLOCK : (place + 1) * BLOCK]
        gram_ref[i * BLOCK : (i + 1) * BLOCK, j * BLOCK : (j + 1) * BLOCK] = block
        if i != j:
            gram_ref[j * BLOCK : (j + 1) * BLOCK, i * BLOCK : (i + 1) * BLOCK] = block.T

    def by_gram(value):
        rows = value.shape[0]
        both = jnp.dot(
            jnp.concatenate(split_two(value), axis=0), gram_ref[...], preferred_element_type=F32
        )
        return both[:rows] + both[rows:]

    def by_first(value):
        return COEF_A * value + by_gram(COEF_B * value + COEF_C * by_gram(value))

    def by_second_gram(value):
        return by_first(by_gram(by_first(value)))

    start = moment_ref[...] * factor_ref[0:1, 0:1]
    once = by_first(start)
    twice = COEF_A * once + by_second_gram(COEF_B * once + COEF_C * by_second_gram(once))
    update_ref[...] = twice * math.sqrt(max(FF, D))


def whole(memory_space=pltpu.VMEM):
    return pl.BlockSpec(memory_space=memory_space)


PARAMS = pltpu.CompilerParams(vmem_limit_bytes=48 * 1024 * 1024)


def call(kernel, out_shape, inputs, scratch=(), scalars=0):
    return pl.pallas_call(
        kernel,
        out_shape=out_shape,
        in_specs=[whole(pltpu.SMEM)] * scalars + [whole()] * (len(inputs) - scalars),
        out_specs=jax.tree.map(lambda _: whole(), out_shape),
        scratch_shapes=scratch,
        compiler_params=PARAMS,
        name=kernel.__name__.removesuffix("_kernel"),
    )(*inputs)


def shifted(value, axis, distance):
    size = lax.axis_size(axis)
    return lax.ppermute(value, axis, [(i, (i + distance) % size) for i in range(size)])


def body(hidden_token_tiles, gradient_token_tiles, momentum, filled_tile_count):
    experts = hidden_token_tiles.shape[0]
    along_x, along_z = lax.axis_size("x"), lax.axis_size("z")
    rows = momentum.shape[1]
    chunk = len(block_pairs()) * BLOCK // along_x
    piece = chunk // along_z
    counts = lax.dynamic_index_in_dim(filled_tile_count, lax.axis_index(DP), 0, keepdims=False)
    place = lax.axis_index("x").astype(jnp.int32).reshape(1)

    packed = call(
        pack_kernel,
        jax.ShapeDtypeStruct((experts, FF + rows, BLOCK), BF16),
        (counts, hidden_token_tiles, gradient_token_tiles),
        scalars=1,
    )
    tiles = lax.all_to_all(packed, DP, 0, 0, tiled=True)
    moment, parts = call(
        gram_kernel,
        (
            jax.ShapeDtypeStruct((rows, FF), F32),
            jax.ShapeDtypeStruct((along_x, chunk + UNIT, BLOCK), BF16),
        ),
        (place, tiles, momentum[0]),
        scalars=1,
    )
    cut = call(
        middle_kernel,
        jax.ShapeDtypeStruct((along_z, piece + UNIT, BLOCK), BF16),
        [parts[0]] + [shifted(parts[k], "x", k) for k in range(1, along_x)],
    )
    copies, factor = call(
        sum_kernel,
        (
            jax.ShapeDtypeStruct((along_z, piece, BLOCK), BF16),
            jax.ShapeDtypeStruct((8, BLOCK), F32),
        ),
        [lax.all_to_all(cut, "z", 0, 0, tiled=True)],
    )
    own = lax.all_to_all(copies, "z", 0, 0, tiled=True).reshape(chunk, BLOCK)
    update = call(
        polynomial_kernel,
        jax.ShapeDtypeStruct((rows, FF), F32),
        [place, moment, factor, own] + [shifted(own, "x", k) for k in range(1, along_x)],
        scratch=[pltpu.VMEM((along_x, chunk, BLOCK), BF16), pltpu.VMEM((FF, FF), BF16)],
        scalars=1,
    )
    gathered = lax.all_gather((update * 256.0).astype(jnp.float16), DP, axis=0, tiled=False)
    return (moment[None], gathered.astype(F32) * (1.0 / 256.0))


def solution(mesh):
    split = Mesh(mesh.devices.reshape(4, 2, 4, 8), ("y", "core", "x", "z"))
    placed = (P(None, DP, None), P(None, EXPERT, DP), P(DP, EXPERT, None), P())
    return jax.shard_map(
        body,
        mesh=split,
        in_specs=placed,
        out_specs=(P(DP, EXPERT, None), P(None, EXPERT, None)),
        check_vma=False,
    )
```

time: 169 us -> 152 us (0.90)
  blocking collectives: 118 us -> 54.3 us
  waiting for transfers between devices: 26.2 us -> 61.3 us
  starting transfers between devices: 4.46 us -> 11.2 us
  local copies, waits for them, and re-layouts: 0.2 us -> 4.84 us
    all_to_all x3 -> x2, blocking collectives: 94.8 us -> 33.3 us  [the longest x1 20.6 us: body(): lax.all_to_all(cut, 'z', 0, 0, tiled=True)]
    ppermute x0 -> x6, waiting for transfers between devices: none -> 30.1 us  [shifted(): lax.ppermute(value, axis, [(i, (i + distance) % size) for i in range(size)])]
    all_to_all x1, waiting for transfers between devices: 26.2 us -> 31.3 us  [body(): tiles = lax.all_to_all(packed, DP, 0, 0, tiled=True)]
    unnamed x6 -> x12, local copies, waits for them, and re-layouts: 0.02 us -> 4.76 us
    ppermute x0 -> x6, starting transfers between devices: none -> 4.34 us  [shifted(): lax.ppermute(value, axis, [(i, (i + distance) % size) for i in range(size)])]
    all_to_all x1, starting transfers between devices: 4.46 us -> 6.9 us  [body(): tiles = lax.all_to_all(packed, DP, 0, 0, tiled=True)]
    all_gather x1, blocking collectives: 23.4 us -> 21 us  [body(): lax.all_gather((update * 256.0).astype(jnp.float16), DP, axis=0, tiled=Fa...]
    pallas_call x3 -> x5, Pallas kernels: 14.4 us -> 15.4 us  [call(): pl.pallas_call(kernel, out_shape=out_shape, in_specs=[whole(pltpu.SMEM)]...]
  transfers between devices with their start and end apart: 1 -> 7, of which waited for: 1 -> 7; matrix products, arithmetic and copies ran while one was open for 0% -> 0% of each run, Pallas kernels for 0% -> 0%
where the time goes in v2:
time: 152 us
  waiting for transfers between devices  61.3 us (40%)
  blocking collectives  54.3 us (36%)
  Pallas kernels  15.4 us (10%)
  starting transfers between devices  11.2 us (7%)
  local copies, waits for them, and re-layouts  4.84 us (3%)
  other arithmetic  4.15 us (3%)
    all_to_all x1, waiting for transfers between devices, body(): tiles = lax.all_to_all(packed, DP, 0, 0, tiled=True)  31.3 us
    ppermute x6, waiting for transfers between devices, shifted(): lax.ppermute(value, axis, [(i, (i + distance) % size) for i in range(size)])  30.1 us
    all_gather x1, blocking collectives, body(): lax.all_gather((update * 256.0).astype(jnp.float16), DP, axis=0, tiled=Fa...  21 us
    all_to_all x1, blocking collectives, body(): lax.all_to_all(cut, 'z', 0, 0, tiled=True)  20.6 us
    pallas_call x5, Pallas kernels, call(): pl.pallas_call(kernel, out_shape=out_shape, in_specs=[whole(pltpu.SMEM)]...  15.4 us
    all_to_all x1, blocking collectives, body(): own = lax.all_to_all(copies, 'z', 0, 0, tiled=True).reshape(chunk, BLOCK)  12.8 us
    all_to_all x1, starting transfers between devices, body(): tiles = lax.all_to_all(packed, DP, 0, 0, tiled=True)  6.9 us
    unnamed x12, local copies, waits for them, and re-layouts  4.76 us
  transfers between devices with their start and end apart: 7, of which 7 were waited for; matrix products, arithmetic and copies ran while one was open for 0% of the time, Pallas kernels for 0%

profile of v2, /device:TPU:1, one launch (start us, length us, event | category | flops | bytes accessed | tf_op | source)
XLA Modules:
  0.0 151.9 jit_solution(16772649847931251325)
XLA Ops:
  0.6 0.0 copy-start
  0.7 0.7 copy-done
  1.3 1.6 %copy-done.2 = bf16[8,128,1024]{2,1,0:T(8,128)(2,1)S(1)} copy-done((bf16[8,128,1024]{2,1,0:T(8,128)(2,1)S(1)}, bf16[8,128,1024]{2,1,0:T(8,128)(2,1)}, u32[]{:S(2)}) %copy-start.2) | copy-done | bytes 2097176
  2.9 1.0 copy-done.5
  3.9 0.9 pack.1
  4.9 0.0 copy-start.1
  4.9 1.5 copy-done.1
  6.4 6.9 %all-to-all-start = ((bf16[8,1248,128]{2,1,0:T(8,128)(2,1)}), bf16[8,1248,128]{2,1,0:T(8,128)(2,1)S(1)}, u32[]{:S(2)}, u32[]{:S(2)}) async-start(bf16[8,1248,128]{2,1,0:T(8,128)(2,1)} %copy-done.1), calls=%async_computation | async-start | bytes 5111808 | tf_op jit(solution)/shard_map/all_to_all | solution.py:193
  13.3 31.3 %all-to-all-done.tiles_ref = bf16[8,1248,128]{2,1,0:T(8,128)(2,1)S(1)} async-done(((bf16[8,1248,128]{2,1,0:T(8,128)(2,1)}), bf16[8,1248,128]{2,1,0:T(8,128)(2,1)S(1)}, u32[]{:S(2)}, u32[]{:S(2)}) %all-to-all-start) | async-done | bytes 2555936 | tf_op jit(solution)/shard_map/all_to_all | solution.py:193
  44.5 0.0 copy-done.3
  44.5 2.0 %gram.1 = (f32[224,1024]{1,0:T(8,128)}, bf16[4,1168,128]{2,1,0:T(8,128)(2,1)S(1)}) custom-call(s32[1]{0:T(128)} %bitcast.place_ref, bf16[8,1248,128]{2,1,0:T(8,128)(2,1)S(1)} %all-to-all-done.tiles_ref, f32[224,1024]{1,0:T(8,128)S(1)} %bitcast.19), custom_call_target="tpu_custom_call" | custom-call | tf_op jit(solution)/shard_map/gram/pallas_call | solution.py:162
  46.5 0.1 slice_bitcast_fusion
  46.6 1.7 %collective-permute-start.2 = (bf16[1168,128]{1,0:T(8,128)(2,1)S(1)}, bf16[1168,128]{1,0:T(8,128)(2,1)S(1)}, u32[]{:S(2)}, u32[]{:S(2)}) collective-permute-start(bf16[1168,128]{1,0:T(8,128)(2,1)S(1)} %get-tuple-element.10), channel_id=1, source_target_pairs={{0,24},{8,0},{16,8},{24,16},{1,25},{9,1},{17,9},{25,17},{2,26},{10... | collective-permute-start | bytes 897032 | tf_op jit(solution)/shard_map/ppermute | solution.py:175
  48.3 0.5 collective-permute-start.1
  48.8 0.6 collective-permute-start
  49.4 4.9 %collective-permute-done.2.refs_2_ = bf16[1168,128]{1,0:T(8,128)(2,1)S(1)} collective-permute-done((bf16[1168,128]{1,0:T(8,128)(2,1)S(1)}, bf16[1168,128]{1,0:T(8,128)(2,1)S(1)}, u32[]{:S(2)}, u32[]{:S(2)}) %collective-permute-start.2) | collective-permute-done | bytes 299040 | tf_op jit(solution)/shard_map/ppermute | solution.py:175
  54.4 2.9 %collective-permute-done.1.refs_1_ = bf16[1168,128]{1,0:T(8,128)(2,1)S(1)} collective-permute-done((bf16[1168,128]{1,0:T(8,128)(2,1)S(1)}, bf16[1168,128]{1,0:T(8,128)(2,1)S(1)}, u32[]{:S(2)}, u32[]{:S(2)}) %collective-permute-start.1) | collective-permute-done | bytes 299040 | tf_op jit(solution)/shard_map/ppermute | solution.py:175
  57.3 7.9 %collective-permute-done.refs_0_ = bf16[1168,128]{1,0:T(8,128)(2,1)S(1)} collective-permute-done((bf16[1168,128]{1,0:T(8,128)(2,1)S(1)}, bf16[1168,128]{1,0:T(8,128)(2,1)S(1)}, u32[]{:S(2)}, u32[]{:S(2)}) %collective-permute-start) | collective-permute-done | bytes 299040 | tf_op jit(solution)/shard_map/ppermute | solution.py:175
  65.2 0.3 middle.1
  65.5 20.6 %all_to_all.15.parts_ref = bf16[8,160,128]{2,1,0:T(8,128)(2,1)S(1)} all-to-all(bf16[8,160,128]{2,1,0:T(8,128)(2,1)S(1)} %middle.1), channel_id=1, replica_groups=mesh['y'=4,'core'=2,'x'=4,'z'=8] {'z'}, dimensions={0} | all-to-all | bytes 655360 | tf_op jit(solution)/shard_map/all_to_all | solution.py:214
  86.1 0.1 sum.1
  86.2 12.8 %all_to_all.16 = bf16[8,144,128]{2,1,0:T(8,128)(2,1)S(1)} all-to-all(bf16[8,144,128]{2,1,0:T(8,128)(2,1)S(1)} %get-tuple-element.9), channel_id=1, replica_groups=mesh['y'=4,'core'=2,'x'=4,'z'=8] {'z'}, dimensions={0} | all-to-all | bytes 589824 | tf_op jit(solution)/shard_map/all_to_all | solution.py:216
  98.9 0.0 collective-permute-start.5
  98.9 0.5 collective-permute-start.4
  99.5 0.9 collective-permute-start.3
  100.4 4.1 %collective-permute-done.5.refs_3_ = bf16[1152,128]{1,0:T(8,128)(2,1)S(1)} collective-permute-done((bf16[1152,128]{1,0:T(8,128)(2,1)S(1)}, bf16[1152,128]{1,0:T(8,128)(2,1)S(1)}, u32[]{:S(2)}, u32[]{:S(2)}) %collective-permute-start.5) | collective-permute-done | bytes 294944 | tf_op jit(solution)/shard_map/ppermute | solution.py:175
  104.5 1.6 %collective-permute-done.4.refs_2_ = bf16[1152,128]{1,0:T(8,128)(2,1)S(1)} collective-permute-done((bf16[1152,128]{1,0:T(8,128)(2,1)S(1)}, bf16[1152,128]{1,0:T(8,128)(2,1)S(1)}, u32[]{:S(2)}, u32[]{:S(2)}) %collective-permute-start.4) | collective-permute-done | bytes 294944 | tf_op jit(solution)/shard_map/ppermute | solution.py:175
  106.1 8.5 %collective-permute-done.3.refs_1_ = bf16[1152,128]{1,0:T(8,128)(2,1)S(1)} collective-permute-done((bf16[1152,128]{1,0:T(8,128)(2,1)S(1)}, bf16[1152,128]{1,0:T(8,128)(2,1)S(1)}, u32[]{:S(2)}, u32[]{:S(2)}) %collective-permute-start.3) | collective-permute-done | bytes 294944 | tf_op jit(solution)/shard_map/ppermute | solution.py:175
  114.7 12.1 %polynomial.1 = f32[224,1024]{1,0:T(8,128)S(1)} custom-call(s32[1]{0:T(128)} %bitcast.place_ref, f32[224,1024]{1,0:T(8,128)S(1)} %copy-done.4, f32[8,128]{1,0:T(8,128)S(1)} %get-tuple-element.8.factor_ref, bf16[1152,128]{1,0:T(8,128)(2,1)S(1)} %bitcast.18, bf16[1152,128]{1,0:T(8,128)(2,1)S(1)} %collective-permute-done.3.refs_1_, ...), custom_call_target="tpu_custom_call" | custom-call | tf_op jit(solution)/shard_map/polynomial/pallas_call | solution.py:162
  126.8 0.1 multiply_convert_fusion
  126.9 21.0 %all-gather.2 = f16[1792,1024]{1,0:T(8,128)(2,1)S(1)} all-gather(f16[224,1024]{1,0:T(8,128)(2,1)S(1)} %multiply_convert_fusion), channel_id=2, replica_groups=mesh['y'=4,'core'=2,'x'=4,'z'=8] {'y','core'}, dimensions={0}, use_global_device_ids=true | all-gather | bytes 4128768 | tf_op jit(solution)/shard_map/all_gather | solution.py:224
  147.8 4.1 %convert_multiply_fusion = f32[1792,1024]{1,0:T(8,128)} fusion(f16[1792,1024]{1,0:T(8,128)(2,1)S(1)} %all-gather.2), kind=kLoop, calls=%fused_computation | loop fusion | flops 3670016 | bytes 11010048 | tf_op jit(solution)/shard_map/mul | solution.py:225
  (6 shorter events, 0.0 us)
Async XLA Ops:
  0.6 0.7 copy-start
  1.3 1.6 %copy-start.2 = (bf16[8,128,1024]{2,1,0:T(8,128)(2,1)S(1)}, bf16[8,128,1024]{2,1,0:T(8,128)(2,1)}, u32[]{:S(2)}) copy-start(bf16[8,128,1024]{2,1,0:T(8,128)(2,1)} %hidden_ref.1) | copy-start | bytes 6291460
  2.9 1.0 copy-start.5
  4.9 1.5 copy-start.1
  6.4 38.2 %copy-start.3 = (f32[1,224,1024]{2,1,0:T(8,128)S(1)}, f32[1,224,1024]{2,1,0:T(8,128)}, u32[]{:S(2)}) copy-start(f32[1,224,1024]{2,1,0:T(8,128)} %param.6) | copy-start | bytes 2752516
  6.4 38.2 %all-to-all-start = ((bf16[8,1248,128]{2,1,0:T(8,128)(2,1)}), bf16[8,1248,128]{2,1,0:T(8,128)(2,1)S(1)}, u32[]{:S(2)}, u32[]{:S(2)}) async-start(bf16[8,1248,128]{2,1,0:T(8,128)(2,1)} %copy-done.1), calls=%async_computation | async-start | bytes 5111808 | tf_op jit(solution)/shard_map/all_to_all | solution.py:193
  46.5 68.2 %copy-start.4 = (f32[224,1024]{1,0:T(8,128)S(1)}, f32[224,1024]{1,0:T(8,128)}, u32[]{:S(2)}) copy-start(f32[224,1024]{1,0:T(8,128)} %get-tuple-element.6.moment_ref) | copy-start | bytes 2752516
  46.6 7.8 %collective-permute-start.2 = (bf16[1168,128]{1,0:T(8,128)(2,1)S(1)}, bf16[1168,128]{1,0:T(8,128)(2,1)S(1)}, u32[]{:S(2)}, u32[]{:S(2)}) collective-permute-start(bf16[1168,128]{1,0:T(8,128)(2,1)S(1)} %get-tuple-element.10), channel_id=1, source_target_pairs={{0,24},{8,0},{16,8},{24,16},{1,25},{9,1},{17,9},{25,17},{2,26},{10... | collective-permute-start | bytes 897032 | tf_op jit(solution)/shard_map/ppermute | solution.py:175
  48.3 9.0 %collective-permute-start.1 = (bf16[1168,128]{1,0:T(8,128)(2,1)S(1)}, bf16[1168,128]{1,0:T(8,128)(2,1)S(1)}, u32[]{:S(2)}, u32[]{:S(2)}) collective-permute-start(bf16[1168,128]{1,0:T(8,128)(2,1)S(1)} %get-tuple-element.11), channel_id=1, source_target_pairs={{0,16},{8,24},{16,0},{24,8},{1,17},{9,25},{17,1},{25,9},{2,18},{10... | collective-permute-start | bytes 897032 | tf_op jit(solution)/shard_map/ppermute | solution.py:175
  48.8 16.4 %collective-permute-start = (bf16[1168,128]{1,0:T(8,128)(2,1)S(1)}, bf16[1168,128]{1,0:T(8,128)(2,1)S(1)}, u32[]{:S(2)}, u32[]{:S(2)}) collective-permute-start(bf16[1168,128]{1,0:T(8,128)(2,1)S(1)} %get-tuple-element.12), channel_id=1, source_target_pairs={{0,8},{8,16},{16,24},{24,0},{1,9},{9,17},{17,25},{25,1},{2,10},{10... | collective-permute-start | bytes 897032 | tf_op jit(solution)/shard_map/ppermute | solution.py:175
  98.9 5.6 %collective-permute-start.5 = (bf16[1152,128]{1,0:T(8,128)(2,1)S(1)}, bf16[1152,128]{1,0:T(8,128)(2,1)S(1)}, u32[]{:S(2)}, u32[]{:S(2)}) collective-permute-start(bf16[1152,128]{1,0:T(8,128)(2,1)S(1)} %bitcast.15), channel_id=1, source_target_pairs={{0,24},{8,0},{16,8},{24,16},{1,25},{9,1},{17,9},{25,17},{2,26},{10... | collective-permute-start | bytes 884744 | tf_op jit(solution)/shard_map/ppermute | solution.py:175
  98.9 7.2 %collective-permute-start.4 = (bf16[1152,128]{1,0:T(8,128)(2,1)S(1)}, bf16[1152,128]{1,0:T(8,128)(2,1)S(1)}, u32[]{:S(2)}, u32[]{:S(2)}) collective-permute-start(bf16[1152,128]{1,0:T(8,128)(2,1)S(1)} %bitcast.16), channel_id=1, source_target_pairs={{0,16},{8,24},{16,0},{24,8},{1,17},{9,25},{17,1},{25,9},{2,18},{10... | collective-permute-start | bytes 884744 | tf_op jit(solution)/shard_map/ppermute | solution.py:175
  99.5 15.2 %collective-permute-start.3 = (bf16[1152,128]{1,0:T(8,128)(2,1)S(1)}, bf16[1152,128]{1,0:T(8,128)(2,1)S(1)}, u32[]{:S(2)}, u32[]{:S(2)}) collective-permute-start(bf16[1152,128]{1,0:T(8,128)(2,1)S(1)} %bitcast.17), channel_id=1, source_target_pairs={{0,8},{8,16},{16,24},{24,0},{1,9},{9,17},{17,25},{25,1},{2,10},{10... | collective-permute-start | bytes 884744 | tf_op jit(solution)/shard_map/ppermute | solution.py:175

commit v3 on v2

v3 whole, which is shorter than its diff:
```python
import math

import jax
import jax.numpy as jnp
from jax import lax
from jax.experimental import pallas as pl
from jax.experimental.pallas import tpu as pltpu
from jax.sharding import Mesh
from jax.sharding import PartitionSpec as P

D = 7168
FF = 1024
TILE = 16
BLOCK = 128
UNIT = 16
NEEDED = 6

MOMENTUM_DECAY = 0.95
EPSILON = 1e-07
COEF_A = 3.4445
COEF_B = -4.775
COEF_C = 2.0315

DP = ("y", "core")
EXPERT = ("x", "z")

BF16 = jnp.bfloat16
F32 = jnp.float32


def split_two(value):
    high = value.astype(BF16)
    return high, (value - high.astype(F32)).astype(BF16)


def block_pairs(place):
    half = 0 if place < 2 else 1
    return [(0, 0), (0, 1), (0, 2), (0, 3), (0, 5), (1, 1), (1, 2), (1, 3), (half, 4 + half)]


def pieces_of(total, shape):
    first = total.astype(BF16).astype(F32)
    second = (total - first).astype(BF16).astype(F32)
    third = total - first - second
    rows = lax.broadcasted_iota(jnp.int32, shape, 0)
    tile = jnp.where(rows == 0, first, jnp.where(rows == 1, second, jnp.where(rows == 2, third, 0.0)))
    return tile.astype(BF16)


def column(place, block):
    return pl.ds(pl.multiple_of(lax.rem(2 * place + block, FF // BLOCK) * BLOCK, BLOCK), BLOCK)


def columns_kernel(place_ref, momentum_ref, *column_refs):
    for distance, column_ref in enumerate(column_refs, 1):
        for block in range(NEEDED):
            value = momentum_ref[:, column(place_ref[0] + distance, block)]
            column_ref[:, block * BLOCK : (block + 1) * BLOCK] = value.astype(BF16)


def gram_kernel(place_ref, counts_ref, hidden_ref, momentum_ref, tokens_ref, *refs):
    *other_refs, moment_ref, cut_ref, needed_ref = refs
    groups, height, width = tokens_ref.shape
    place = place_ref[0]
    lanes = lax.broadcasted_iota(jnp.int32, (height, width), 1)

    def tokens_of(ref):
        kept = [jnp.where(lanes < counts_ref[g] * TILE, ref[g].astype(F32), 0.0) for g in range(groups)]
        return jnp.concatenate(kept, axis=1).astype(BF16)

    gradient = jnp.dot(
        tokens_of(tokens_ref), hidden_ref[...].reshape(groups * width, FF), preferred_element_type=F32
    )
    moment = MOMENTUM_DECAY * momentum_ref[...] + gradient
    moment_ref[...] = moment

    for g in range(groups):
        for block in range(NEEDED):
            needed_ref[g * width : (g + 1) * width, block * BLOCK : (block + 1) * BLOCK] = hidden_ref[
                g, :, column(place, block)
            ]
    values = [jnp.concatenate([moment_ref[:, column(place, block)] for block in range(NEEDED)], axis=1)]
    others = len(other_refs) // 2
    for momentum_columns, other_tokens in zip(other_refs[:others], other_refs[others:]):
        gradient = jnp.dot(tokens_of(other_tokens), needed_ref[...], preferred_element_type=F32)
        values.append(MOMENTUM_DECAY * momentum_columns[...].astype(F32) + gradient)
    high, low = split_two(jnp.concatenate(values, axis=0))
    left = jnp.concatenate([high[:, : 2 * BLOCK], low[:, : 2 * BLOCK], high[:, : 2 * BLOCK]], axis=0).T
    right = jnp.concatenate([high, high, low], axis=0)
    strips = [
        jnp.dot(left[i * BLOCK : (i + 1) * BLOCK], right, preferred_element_type=F32).astype(BF16)
        for i in range(2)
    ]

    def block_of(i, j):
        return strips[i][:, j * BLOCK : (j + 1) * BLOCK]

    blocks = [block_of(i, j) for i, j in block_pairs(0)[:-1]]
    blocks.append(jnp.where(place < 2, block_of(*block_pairs(0)[-1]), block_of(*block_pairs(2)[-1])))
    per_device = cut_ref.shape[1] // UNIT - 1
    for unit in range(cut_ref.shape[0] * per_device):
        device, at = divmod(unit, per_device)
        block, row = divmod(unit * UNIT, BLOCK)
        cut_ref[device, at * UNIT : (at + 1) * UNIT] = blocks[block][row : row + UNIT]
    total = jnp.sum(jnp.sum(moment * moment, axis=0, keepdims=True), axis=1, keepdims=True)
    for device in range(cut_ref.shape[0]):
        cut_ref[device, per_device * UNIT :] = pieces_of(total, (UNIT, BLOCK))


def sum_kernel(parts_ref, copies_ref):
    total = parts_ref[0].astype(F32)
    for source in range(1, parts_ref.shape[0]):
        total = total + parts_ref[source].astype(F32)
    rows = total.shape[0] - UNIT
    squares = jnp.sum(total[rows:, 0:1], axis=0, keepdims=True)
    piece = total[:rows].astype(BF16)
    tile = pieces_of(squares, (UNIT, BLOCK))
    for target in range(copies_ref.shape[0]):
        copies_ref[target, :rows] = piece
        copies_ref[target, rows:] = tile


def polynomial_kernel(place_ref, moment_ref, *refs):
    *chunk_refs, update_ref, packed_ref, gram_ref = refs
    chunks = len(chunk_refs)
    pieces, height, _ = chunk_refs[0].shape
    rows = height - UNIT
    squares = jnp.zeros((1, 1), F32)
    for distance, chunk_ref in enumerate(chunk_refs):
        source = lax.rem(place_ref[0] - distance + chunks, chunks)
        for piece in range(pieces):
            packed_ref[source, piece * rows : (piece + 1) * rows] = chunk_ref[piece, :rows]
        squares = squares + jnp.sum(chunk_ref[0, rows:].astype(F32)[:, 0:1], axis=0, keepdims=True)
    factor = 1.0 / (jnp.sqrt(squares) + EPSILON)
    for source in range(chunks):
        for at, pair in enumerate(block_pairs(source)):
            i, j = ((2 * source + block) % (FF // BLOCK) for block in pair)
            block = packed_ref[source, at * BLOCK : (at + 1) * BLOCK]
            gram_ref[i * BLOCK : (i + 1) * BLOCK, j * BLOCK : (j + 1) * BLOCK] = block
            if i != j:
                gram_ref[j * BLOCK : (j + 1) * BLOCK, i * BLOCK : (i + 1) * BLOCK] = block.T

    def by_gram(value):
        rows = value.shape[0]
        both = jnp.dot(
            jnp.concatenate(split_two(value), axis=0), gram_ref[...], preferred_element_type=F32
        )
        return (both[:rows] + both[rows:]) * factor * factor

    def by_first(value):
        return COEF_A * value + by_gram(COEF_B * value + COEF_C * by_gram(value))

    def by_second_gram(value):
        return by_first(by_gram(by_first(value)))

    once = by_first(moment_ref[...] * factor)
    twice = COEF_A * once + by_second_gram(COEF_B * once + COEF_C * by_second_gram(once))
    update_ref[...] = twice * math.sqrt(max(FF, D))


def whole(memory_space=pltpu.VMEM):
    return pl.BlockSpec(memory_space=memory_space)


PARAMS = pltpu.CompilerParams(vmem_limit_bytes=48 * 1024 * 1024)


def call(kernel, out_shape, inputs, scratch=(), scalars=0):
    return pl.pallas_call(
        kernel,
        out_shape=out_shape,
        in_specs=[whole(pltpu.SMEM)] * scalars + [whole()] * (len(inputs) - scalars),
        out_specs=jax.tree.map(lambda _: whole(), out_shape),
        scratch_shapes=scratch,
        compiler_params=PARAMS,
        name=kernel.__name__.removesuffix("_kernel"),
    )(*inputs)


def shifted(value, axis, distance):
    size = lax.axis_size(axis)
    return lax.ppermute(value, axis, [(i, (i + distance) % size) for i in range(size)])


def body(hidden_token_tiles, gradient_token_tiles, momentum, filled_tile_count):
    along_x, along_z = lax.axis_size("x"), lax.axis_size("z")
    rows = momentum.shape[1]
    piece = len(block_pairs(0)) * BLOCK // along_z
    counts = lax.dynamic_index_in_dim(filled_tile_count, lax.axis_index(DP), 1, keepdims=False)
    place = lax.axis_index("x").astype(jnp.int32).reshape(1)
    distances = range(1, along_x)

    columns = call(
        columns_kernel,
        [jax.ShapeDtypeStruct((rows, NEEDED * BLOCK), BF16) for _ in distances],
        [place, momentum[0]],
        scalars=1,
    )
    other_columns = [shifted(columns[k - 1], "x", k) for k in distances]
    tokens = lax.all_to_all(gradient_token_tiles, DP, 0, 0, tiled=True)
    other_tokens = [shifted(tokens, "x", k) for k in distances]
    hidden = lax.all_to_all(hidden_token_tiles, DP, 0, 0, tiled=True)
    moment, cut = call(
        gram_kernel,
        (
            jax.ShapeDtypeStruct((rows, FF), F32),
            jax.ShapeDtypeStruct((along_z, piece + UNIT, BLOCK), BF16),
        ),
        [place, counts, hidden, momentum[0], tokens] + other_columns + other_tokens,
        scratch=[pltpu.VMEM((hidden.shape[0] * hidden.shape[1], NEEDED * BLOCK), BF16)],
        scalars=2,
    )
    copies = call(
        sum_kernel,
        jax.ShapeDtypeStruct((along_z, piece + UNIT, BLOCK), BF16),
        [lax.all_to_all(cut, "z", 0, 0, tiled=True)],
    )
    own = lax.all_to_all(copies, "z", 0, 0, tiled=True)
    update = call(
        polynomial_kernel,
        jax.ShapeDtypeStruct((rows, FF), F32),
        [place, moment, own] + [shifted(own, "x", k) for k in distances],
        scratch=[
            pltpu.VMEM((along_x, along_z * piece, BLOCK), BF16),
            pltpu.VMEM((FF, FF), BF16),
        ],
        scalars=1,
    )
    gathered = lax.all_gather((update * 256.0).astype(jnp.float16), DP, axis=0, tiled=False)
    return (moment[None], gathered.astype(F32) * (1.0 / 256.0))


def solution(mesh):
    split = Mesh(mesh.devices.reshape(4, 2, 4, 8), ("y", "core", "x", "z"))
    placed = (P(None, DP, None), P(None, EXPERT, DP), P(DP, EXPERT, None), P())
    return jax.shard_map(
        body,
        mesh=split,
        in_specs=placed,
        out_specs=(P(DP, EXPERT, None), P(None, EXPERT, None)),
        check_vma=False,
    )
```

time: 152 us -> 159 us (1.046)
  blocking collectives: 54.3 us -> 69 us
  waiting for transfers between devices: 61.3 us -> 47.4 us
  starting transfers between devices: 11.2 us -> 13.7 us
  Pallas kernels: 15.4 us -> 17.9 us
    all_to_all x1, waiting for transfers between devices: 31.3 us -> 0.01 us  [body(): hidden = lax.all_to_all(hidden_token_tiles, DP, 0, 0, tiled=True)]
    ppermute x6 -> x9, waiting for transfers between devices: 30.1 us -> 47.4 us  [shifted(): lax.ppermute(value, axis, [(i, (i + distance) % size) for i in range(size)])]
    all_to_all x1 -> x2, blocking collectives: 12.8 us -> 28.5 us  [the longest x1 15.4 us: body(): tokens = lax.all_to_all(gradient_token_tiles, DP, 0, 0, tiled=True)]
    ppermute x6 -> x9, starting transfers between devices: 4.34 us -> 9.28 us  [shifted(): lax.ppermute(value, axis, [(i, (i + distance) % size) for i in range(size)])]
    pallas_call x5 -> x4, Pallas kernels: 15.4 us -> 17.9 us  [call(): pl.pallas_call(kernel, out_shape=out_shape, in_specs=[whole(pltpu.SMEM)]...]
    all_to_all x1, starting transfers between devices: 6.9 us -> 4.46 us  [body(): hidden = lax.all_to_all(hidden_token_tiles, DP, 0, 0, tiled=True)]
  transfers between devices with their start and end apart: 7 -> 10, of which waited for: 7 -> 5; matrix products, arithmetic and copies ran while one was open for 0% -> 0% of each run, Pallas kernels for 0% -> 1%
where the time goes in v3:
time: 159 us; the launch traced here: 158 us
  blocking collectives  69 us (43%)
  waiting for transfers between devices  47.4 us (30%)
  Pallas kernels  17.9 us (11%)
  starting transfers between devices  13.7 us (9%)
  local copies, waits for them, and re-layouts  5.44 us (3%)
  other arithmetic  4.15 us (3%)
    ppermute x9, waiting for transfers between devices, shifted(): lax.ppermute(value, axis, [(i, (i + distance) % size) for i in range(size)])  47.4 us
    all_gather x1, blocking collectives, body(): lax.all_gather((update * 256.0).astype(jnp.float16), DP, axis=0, tiled=Fa...  21.3 us
    all_to_all x1, blocking collectives, body(): lax.all_to_all(cut, 'z', 0, 0, tiled=True)  19.2 us
    pallas_call x4, Pallas kernels, call(): pl.pallas_call(kernel, out_shape=out_shape, in_specs=[whole(pltpu.SMEM)]...  17.9 us
    all_to_all x1, blocking collectives, body(): tokens = lax.all_to_all(gradient_token_tiles, DP, 0, 0, tiled=True)  15.4 us
    all_to_all x1, blocking collectives, body(): own = lax.all_to_all(copies, 'z', 0, 0, tiled=True)  13.2 us
    ppermute x9, starting transfers between devices, shifted(): lax.ppermute(value, axis, [(i, (i + distance) % size) for i in range(size)])  9.28 us
    unnamed x12, local copies, waits for them, and re-layouts  5.25 us
  transfers between devices with their start and end apart: 10, of which 5 were waited for; matrix products, arithmetic and copies ran while one was open for 0% of the time, Pallas kernels for 1%

profile of v3, /device:TPU:1, one launch (start us, length us, event | category | flops | bytes accessed | tf_op | source)
XLA Modules:
  0.0 158.3 jit_solution(16222887759488526197)
XLA Ops:
  0.6 0.0 copy-start
  0.6 15.4 %all_to_all.20.tokens_ref = bf16[8,224,128]{2,1,0:T(8,128)(2,1)S(1)} all-to-all(bf16[8,224,128]{2,1,0:T(8,128)(2,1)} %param.5), channel_id=1, replica_groups=mesh['y'=4,'core'=2,'x'=4,'z'=8] {'y','core'}, dimensions={0} | all-to-all | bytes 917504 | tf_op jit(solution)/shard_map/all_to_all | solution.py:200
  16.0 4.5 %all-to-all-start = ((bf16[8,128,1024]{2,1,0:T(8,128)(2,1)}), bf16[8,128,1024]{2,1,0:T(8,128)(2,1)S(1)}, u32[]{:S(2)}, u32[]{:S(2)}) async-start(bf16[8,128,1024]{2,1,0:T(8,128)(2,1)} %param.4), calls=%async_computation | async-start | bytes 4194304 | tf_op jit(solution)/shard_map/all_to_all | solution.py:202
  20.5 1.2 copy-done.1
  21.7 1.1 columns.1
  22.8 0.6 collective-permute-start
  23.4 2.1 %collective-permute-start.5 = (bf16[8,224,128]{2,1,0:T(8,128)(2,1)S(1)}, bf16[8,224,128]{2,1,0:T(8,128)(2,1)S(1)}, u32[]{:S(2)}, u32[]{:S(2)}) collective-permute-start(bf16[8,224,128]{2,1,0:T(8,128)(2,1)S(1)} %all_to_all.20.tokens_ref), channel_id=1, source_target_pairs={{0,24},{8,0},{16,8},{24,16},{1,25},{9,1},{17,9},{25,17},{2,26},{10... | collective-permute-start | bytes 1376264 | tf_op jit(solution)/shard_map/ppermute | solution.py:182
  25.5 0.9 collective-permute-start.4
  26.4 0.3 collective-permute-start.3
  26.7 1.8 %collective-permute-start.1 = (bf16[224,768]{1,0:T(8,128)(2,1)}, bf16[224,768]{1,0:T(8,128)(2,1)}, u32[]{:S(2)}, u32[]{:S(2)}) collective-permute-start(bf16[224,768]{1,0:T(8,128)(2,1)} %get-tuple-element.8), channel_id=1, source_target_pairs={{0,16},{8,24},{16,0},{24,8},{1,17},{9,25},{17,1},{25,9},{2,18},{10... | collective-permute-start | bytes 1032200 | tf_op jit(solution)/shard_map/ppermute | solution.py:182
  28.4 5.2 %collective-permute-done.refs_0_ = bf16[224,768]{1,0:T(8,128)(2,1)S(1)} collective-permute-done((bf16[224,768]{1,0:T(8,128)(2,1)S(1)}, bf16[224,768]{1,0:T(8,128)(2,1)S(1)}, u32[]{:S(2)}, u32[]{:S(2)}) %collective-permute-start) | collective-permute-done | bytes 344096 | tf_op jit(solution)/shard_map/ppermute | solution.py:182
  33.6 0.7 copy-done.4
  34.3 0.6 collective-permute-start.2
  35.0 0.2 dynamic-slice_reduce_fusion.counts_ref
  35.2 26.0 %collective-permute-done.1.refs_1_ = bf16[224,768]{1,0:T(8,128)(2,1)} collective-permute-done((bf16[224,768]{1,0:T(8,128)(2,1)}, bf16[224,768]{1,0:T(8,128)(2,1)}, u32[]{:S(2)}, u32[]{:S(2)}) %collective-permute-start.1) | collective-permute-done | bytes 344096 | tf_op jit(solution)/shard_map/ppermute | solution.py:182
  61.2 0.0 copy-start.2
  61.2 1.2 copy-done.2
  62.4 1.0 copy-done.5
  63.3 4.5 %gram.1 = (f32[224,1024]{1,0:T(8,128)}, bf16[8,160,128]{2,1,0:T(8,128)(2,1)S(1)}) custom-call(s32[1]{0:T(128)} %bitcast.place_ref, s32[8]{0:T(128)S(1)} %dynamic-slice_reduce_fusion.counts_ref, bf16[8,128,1024]{2,1,0:T(8,128)(2,1)S(1)} %all-to-all-done.hidden_ref, f32[224,1024]{1,0:T(8,128)S(1)} %bitcast.5, bf16[8,224,128]{2,1,0:T(8,128)(2,1)S(1)} %all_to_all.20.tokens_ref, ...), custom_call_target="tpu_custom_call" | custom-call | tf_op jit(solution)/shard_map/gram/pallas_call | solution.py:169
  67.9 19.2 %all_to_all.21.parts_ref = bf16[8,160,128]{2,1,0:T(8,128)(2,1)S(1)} all-to-all(bf16[8,160,128]{2,1,0:T(8,128)(2,1)S(1)} %get-tuple-element.11), channel_id=1, replica_groups=mesh['y'=4,'core'=2,'x'=4,'z'=8] {'z'}, dimensions={0} | all-to-all | bytes 655360 | tf_op jit(solution)/shard_map/all_to_all | solution.py:216
  87.1 0.1 sum.1
  87.2 13.2 %all_to_all.22.refs_0_ = bf16[8,160,128]{2,1,0:T(8,128)(2,1)S(1)} all-to-all(bf16[8,160,128]{2,1,0:T(8,128)(2,1)S(1)} %sum.1), channel_id=1, replica_groups=mesh['y'=4,'core'=2,'x'=4,'z'=8] {'z'}, dimensions={0} | all-to-all | bytes 655360 | tf_op jit(solution)/shard_map/all_to_all | solution.py:218
  100.3 2.4 %collective-permute-start.8 = (bf16[8,160,128]{2,1,0:T(8,128)(2,1)S(1)}, bf16[8,160,128]{2,1,0:T(8,128)(2,1)S(1)}, u32[]{:S(2)}, u32[]{:S(2)}) collective-permute-start(bf16[8,160,128]{2,1,0:T(8,128)(2,1)S(1)} %all_to_all.22.refs_0_), channel_id=1, source_target_pairs={{0,24},{8,0},{16,8},{24,16},{1,25},{9,1},{17,9},{25,17},{2,26},{10... | collective-permute-start | bytes 983048 | tf_op jit(solution)/shard_map/ppermute | solution.py:182
  102.7 0.6 collective-permute-start.6
  103.3 6.9 %collective-permute-done.8.refs_3_ = bf16[8,160,128]{2,1,0:T(8,128)(2,1)S(1)} collective-permute-done((bf16[8,160,128]{2,1,0:T(8,128)(2,1)S(1)}, bf16[8,160,128]{2,1,0:T(8,128)(2,1)S(1)}, u32[]{:S(2)}, u32[]{:S(2)}) %collective-permute-start.8) | collective-permute-done | bytes 327712 | tf_op jit(solution)/shard_map/ppermute | solution.py:182
  110.2 0.1 collective-permute-done.7.refs_2_
  110.3 9.2 %collective-permute-done.6.refs_1_ = bf16[8,160,128]{2,1,0:T(8,128)(2,1)S(1)} collective-permute-done((bf16[8,160,128]{2,1,0:T(8,128)(2,1)S(1)}, bf16[8,160,128]{2,1,0:T(8,128)(2,1)S(1)}, u32[]{:S(2)}, u32[]{:S(2)}) %collective-permute-start.6) | collective-permute-done | bytes 327712 | tf_op jit(solution)/shard_map/ppermute | solution.py:182
  119.5 1.2 copy-done.3
  120.7 12.2 %polynomial.1 = f32[224,1024]{1,0:T(8,128)S(1)} custom-call(s32[1]{0:T(128)} %bitcast.place_ref, f32[224,1024]{1,0:T(8,128)S(1)} %copy-done.3, bf16[8,160,128]{2,1,0:T(8,128)(2,1)S(1)} %all_to_all.22.refs_0_, bf16[8,160,128]{2,1,0:T(8,128)(2,1)S(1)} %collective-permute-done.6.refs_1_, bf16[8,160,128]{2,1,0:T(8,128)(2,1)S(1)} %collective-permute-done.7.refs_2_, ...), custom_call_target="tpu_custom_call" | custom-call | tf_op jit(solution)/shard_map/polynomial/pallas_call | solution.py:169
  132.9 0.1 multiply_convert_fusion
  133.0 21.3 %all-gather.2 = f16[1792,1024]{1,0:T(8,128)(2,1)S(1)} all-gather(f16[224,1024]{1,0:T(8,128)(2,1)S(1)} %multiply_convert_fusion), channel_id=2, replica_groups=mesh['y'=4,'core'=2,'x'=4,'z'=8] {'y','core'}, dimensions={0}, use_global_device_ids=true | all-gather | bytes 4128768 | tf_op jit(solution)/shard_map/all_gather | solution.py:229
  154.2 4.1 %convert_multiply_fusion = f32[1792,1024]{1,0:T(8,128)} fusion(f16[1792,1024]{1,0:T(8,128)(2,1)S(1)} %all-gather.2), kind=kLoop, calls=%fused_computation | loop fusion | flops 3670016 | bytes 11010048 | tf_op jit(solution)/shard_map/mul | solution.py:230
  (11 shorter events, 0.0 us)
Async XLA Ops:
  0.6 34.3 %copy-start = (s32[8,8]{1,0:T(8,128)S(1)}, s32[8,8]{1,0:T(8,128)}, u32[]{:S(2)}) copy-start(s32[8,8]{1,0:T(8,128)} %param.7) | copy-start | bytes 772
  16.0 45.2 %all-to-all-start = ((bf16[8,128,1024]{2,1,0:T(8,128)(2,1)}), bf16[8,128,1024]{2,1,0:T(8,128)(2,1)S(1)}, u32[]{:S(2)}, u32[]{:S(2)}) async-start(bf16[8,128,1024]{2,1,0:T(8,128)(2,1)} %param.4), calls=%async_computation | async-start | bytes 4194304 | tf_op jit(solution)/shard_map/all_to_all | solution.py:202
  20.5 1.2 copy-start.1
  22.8 10.8 %collective-permute-start = (bf16[224,768]{1,0:T(8,128)(2,1)S(1)}, bf16[224,768]{1,0:T(8,128)(2,1)S(1)}, u32[]{:S(2)}, u32[]{:S(2)}) collective-permute-start(bf16[224,768]{1,0:T(8,128)(2,1)S(1)} %get-tuple-element.7), channel_id=1, source_target_pairs={{0,8},{8,16},{16,24},{24,0},{1,9},{9,17},{17,25},{25,1},{2,10},{10... | collective-permute-start | bytes 1032200 | tf_op jit(solution)/shard_map/ppermute | solution.py:182
  23.4 37.8 %collective-permute-start.5 = (bf16[8,224,128]{2,1,0:T(8,128)(2,1)S(1)}, bf16[8,224,128]{2,1,0:T(8,128)(2,1)S(1)}, u32[]{:S(2)}, u32[]{:S(2)}) collective-permute-start(bf16[8,224,128]{2,1,0:T(8,128)(2,1)S(1)} %all_to_all.20.tokens_ref), channel_id=1, source_target_pairs={{0,24},{8,0},{16,8},{24,16},{1,25},{9,1},{17,9},{25,17},{2,26},{10... | collective-permute-start | bytes 1376264 | tf_op jit(solution)/shard_map/ppermute | solution.py:182
  25.5 35.7 %collective-permute-start.4 = (bf16[8,224,128]{2,1,0:T(8,128)(2,1)S(1)}, bf16[8,224,128]{2,1,0:T(8,128)(2,1)S(1)}, u32[]{:S(2)}, u32[]{:S(2)}) collective-permute-start(bf16[8,224,128]{2,1,0:T(8,128)(2,1)S(1)} %all_to_all.20.tokens_ref), channel_id=1, source_target_pairs={{0,16},{8,24},{16,0},{24,8},{1,17},{9,25},{17,1},{25,9},{2,18},{10... | collective-permute-start | bytes 1376264 | tf_op jit(solution)/shard_map/ppermute | solution.py:182
  26.4 34.8 %collective-permute-start.3 = (bf16[8,224,128]{2,1,0:T(8,128)(2,1)S(1)}, bf16[8,224,128]{2,1,0:T(8,128)(2,1)}, u32[]{:S(2)}, u32[]{:S(2)}) collective-permute-start(bf16[8,224,128]{2,1,0:T(8,128)(2,1)S(1)} %all_to_all.20.tokens_ref), channel_id=1, source_target_pairs={{0,8},{8,16},{16,24},{24,0},{1,9},{9,17},{17,25},{25,1},{2,10},{10... | collective-permute-start | bytes 1376264 | tf_op jit(solution)/shard_map/ppermute | solution.py:182
  26.7 34.5 %collective-permute-start.1 = (bf16[224,768]{1,0:T(8,128)(2,1)}, bf16[224,768]{1,0:T(8,128)(2,1)}, u32[]{:S(2)}, u32[]{:S(2)}) collective-permute-start(bf16[224,768]{1,0:T(8,128)(2,1)} %get-tuple-element.8), channel_id=1, source_target_pairs={{0,16},{8,24},{16,0},{24,8},{1,17},{9,25},{17,1},{25,9},{2,18},{10... | collective-permute-start | bytes 1032200 | tf_op jit(solution)/shard_map/ppermute | solution.py:182
  33.6 0.7 copy-start.4
  34.3 26.8 %collective-permute-start.2 = (bf16[224,768]{1,0:T(8,128)(2,1)}, bf16[224,768]{1,0:T(8,128)(2,1)}, u32[]{:S(2)}, u32[]{:S(2)}) collective-permute-start(bf16[224,768]{1,0:T(8,128)(2,1)} %get-tuple-element.9), channel_id=1, source_target_pairs={{0,24},{8,0},{16,8},{24,16},{1,25},{9,1},{17,9},{25,17},{2,26},{10... | collective-permute-start | bytes 1032200 | tf_op jit(solution)/shard_map/ppermute | solution.py:182
  61.2 1.2 copy-start.2
  62.4 1.0 copy-start.5
  100.3 9.8 %collective-permute-start.8 = (bf16[8,160,128]{2,1,0:T(8,128)(2,1)S(1)}, bf16[8,160,128]{2,1,0:T(8,128)(2,1)S(1)}, u32[]{:S(2)}, u32[]{:S(2)}) collective-permute-start(bf16[8,160,128]{2,1,0:T(8,128)(2,1)S(1)} %all_to_all.22.refs_0_), channel_id=1, source_target_pairs={{0,24},{8,0},{16,8},{24,16},{1,25},{9,1},{17,9},{25,17},{2,26},{10... | collective-permute-start | bytes 983048 | tf_op jit(solution)/shard_map/ppermute | solution.py:182
  102.7 7.5 %collective-permute-start.7 = (bf16[8,160,128]{2,1,0:T(8,128)(2,1)S(1)}, bf16[8,160,128]{2,1,0:T(8,128)(2,1)S(1)}, u32[]{:S(2)}, u32[]{:S(2)}) collective-permute-start(bf16[8,160,128]{2,1,0:T(8,128)(2,1)S(1)} %all_to_all.22.refs_0_), channel_id=1, source_target_pairs={{0,16},{8,24},{16,0},{24,8},{1,17},{9,25},{17,1},{25,9},{2,18},{10... | collective-permute-start | bytes 983048 | tf_op jit(solution)/shard_map/ppermute | solution.py:182
  102.7 16.8 %collective-permute-start.6 = (bf16[8,160,128]{2,1,0:T(8,128)(2,1)S(1)}, bf16[8,160,128]{2,1,0:T(8,128)(2,1)S(1)}, u32[]{:S(2)}, u32[]{:S(2)}) collective-permute-start(bf16[8,160,128]{2,1,0:T(8,128)(2,1)S(1)} %all_to_all.22.refs_0_), channel_id=1, source_target_pairs={{0,8},{8,16},{16,24},{24,0},{1,9},{9,17},{17,25},{25,1},{2,10},{10... | collective-permute-start | bytes 983048 | tf_op jit(solution)/shard_map/ppermute | solution.py:182
  119.5 1.2 copy-start.3

commit v4 on v3

--- a/solution.py
+++ b/solution.py
@@ -58,8 +58,22 @@
             column_ref[:, block * BLOCK : (block + 1) * BLOCK] = value.astype(BF16)
 
 
-def gram_kernel(place_ref, counts_ref, hidden_ref, momentum_ref, tokens_ref, *refs):
-    *other_refs, moment_ref, cut_ref, needed_ref = refs
+def fetched(sources, targets, semaphores):
+    copies = [
+        pltpu.make_async_copy(source, target, semaphores.at[at])
+        for at, (source, target) in enumerate(zip(sources, targets))
+    ]
+    for copy in copies:
+        copy.start()
+    return copies
+
+
+def gram_kernel(place_ref, counts_ref, hidden_ref, tokens_ref, *refs):
+    count = (len(refs) - 4) // 2
+    away_refs, moment_ref, cut_ref, needed_ref = refs[:count], *refs[count : count + 3]
+    here_refs, semaphores = refs[count + 3 : -1], refs[-1]
+    copies = fetched(away_refs, here_refs, semaphores)
+    momentum_ref, other_refs = here_refs[0], here_refs[1:]
     groups, height, width = tokens_ref.shape
     place = place_ref[0]
     lanes = lax.broadcasted_iota(jnp.int32, (height, width), 1)
@@ -71,6 +85,7 @@
     gradient = jnp.dot(
         tokens_of(tokens_ref), hidden_ref[...].reshape(groups * width, FF), preferred_element_type=F32
     )
+    copies[0].wait()
     moment = MOMENTUM_DECAY * momentum_ref[...] + gradient
     moment_ref[...] = moment
 
@@ -80,6 +95,8 @@
                 g, :, column(place, block)
             ]
     values = [jnp.concatenate([moment_ref[:, column(place, block)] for block in range(NEEDED)], axis=1)]
+    for copy in copies[1:]:
+        copy.wait()
     others = len(other_refs) // 2
     for momentum_columns, other_tokens in zip(other_refs[:others], other_refs[others:]):
         gradient = jnp.dot(tokens_of(other_tokens), needed_ref[...], preferred_element_type=F32)
@@ -120,8 +137,9 @@
         copies_ref[target, rows:] = tile
 
 
-def polynomial_kernel(place_ref, moment_ref, *refs):
-    *chunk_refs, update_ref, packed_ref, gram_ref = refs
+def polynomial_kernel(place_ref, moment_away_ref, *refs):
+    *chunk_refs, update_ref, packed_ref, gram_ref, moment_ref, semaphores = refs
+    copies = fetched([moment_away_ref], [moment_ref], semaphores)
     chunks = len(chunk_refs)
     pieces, height, _ = chunk_refs[0].shape
     rows = height - UNIT
@@ -153,6 +171,7 @@
     def by_second_gram(value):
         return by_first(by_gram(by_first(value)))
 
+    copies[0].wait()
     once = by_first(moment_ref[...] * factor)
     twice = COEF_A * once + by_second_gram(COEF_B * once + COEF_C * by_second_gram(once))
     update_ref[...] = twice * math.sqrt(max(FF, D))
@@ -162,17 +181,20 @@
     return pl.BlockSpec(memory_space=memory_space)
 
 
-PARAMS = pltpu.CompilerParams(vmem_limit_bytes=48 * 1024 * 1024)
-
-
-def call(kernel, out_shape, inputs, scratch=(), scalars=0):
+MIB = 1024 * 1024
+
+
+def call(kernel, out_shape, inputs, scratch=(), scalars=0, away=(), mib=8):
     return pl.pallas_call(
         kernel,
         out_shape=out_shape,
-        in_specs=[whole(pltpu.SMEM)] * scalars + [whole()] * (len(inputs) - scalars),
+        in_specs=[
+            whole(pltpu.SMEM if at < scalars else pltpu.HBM if at in away else pltpu.VMEM)
+            for at in range(len(inputs))
+        ],
         out_specs=jax.tree.map(lambda _: whole(), out_shape),
         scratch_shapes=scratch,
-        compiler_params=PARAMS,
+        compiler_params=pltpu.CompilerParams(vmem_limit_bytes=mib * MIB),
         name=kernel.__name__.removesuffix("_kernel"),
     )(*inputs)
 
@@ -196,19 +218,31 @@
         [place, momentum[0]],
         scalars=1,
     )
+    columns, gradient_token_tiles = lax.optimization_barrier((columns, gradient_token_tiles))
     other_columns = [shifted(columns[k - 1], "x", k) for k in distances]
     tokens = lax.all_to_all(gradient_token_tiles, DP, 0, 0, tiled=True)
+    other_columns[0], other_columns[-1], tokens, hidden_token_tiles = lax.optimization_barrier(
+        (other_columns[0], other_columns[-1], tokens, hidden_token_tiles)
+    )
     other_tokens = [shifted(tokens, "x", k) for k in distances]
     hidden = lax.all_to_all(hidden_token_tiles, DP, 0, 0, tiled=True)
+    fetch = [
+        pltpu.with_memory_space_constraint(value, pltpu.HBM)
+        for value in [momentum[0]] + other_columns + other_tokens
+    ]
     moment, cut = call(
         gram_kernel,
         (
             jax.ShapeDtypeStruct((rows, FF), F32),
             jax.ShapeDtypeStruct((along_z, piece + UNIT, BLOCK), BF16),
         ),
-        [place, counts, hidden, momentum[0], tokens] + other_columns + other_tokens,
-        scratch=[pltpu.VMEM((hidden.shape[0] * hidden.shape[1], NEEDED * BLOCK), BF16)],
+        [place, counts, hidden, tokens] + fetch,
+        scratch=[pltpu.VMEM((hidden.shape[0] * hidden.shape[1], NEEDED * BLOCK), BF16)]
+        + [pltpu.VMEM(value.shape, value.dtype) for value in fetch]
+        + [pltpu.SemaphoreType.DMA((len(fetch),))],
+        away=range(4, 4 + len(fetch)),
         scalars=2,
+        mib=28,
     )
     copies = call(
         sum_kernel,
@@ -219,12 +253,16 @@
     update = call(
         polynomial_kernel,
         jax.ShapeDtypeStruct((rows, FF), F32),
-        [place, moment, own] + [shifted(own, "x", k) for k in distances],
+        [place, pltpu.with_memory_space_constraint(moment, pltpu.HBM), own] + [shifted(own, "x", k) for k in distances],
         scratch=[
             pltpu.VMEM((along_x, along_z * piece, BLOCK), BF16),
             pltpu.VMEM((FF, FF), BF16),
+            pltpu.VMEM((rows, FF), F32),
+            pltpu.SemaphoreType.DMA((1,)),
         ],
+        away=(1,),
         scalars=1,
+        mib=20,
     )
     gathered = lax.all_gather((update * 256.0).astype(jnp.float16), DP, axis=0, tiled=False)
     return (moment[None], gathered.astype(F32) * (1.0 / 256.0))

time: 159 us -> 152 us (0.956)
  blocking collectives: 69 us -> 53.9 us
  starting transfers between devices: 13.7 us -> 21.3 us
  waiting for transfers between devices: 47.4 us -> 50.3 us
  local copies, waits for them, and re-layouts: 5.44 us -> 2.86 us
    all_to_all x1 -> x0, blocking collectives: 15.4 us -> none  [body(): tokens = lax.all_to_all(gradient_token_tiles, DP, 0, 0, tiled=True)]
    all_to_all x0 -> x1, starting transfers between devices: none -> 6.63 us  [body(): tokens = lax.all_to_all(gradient_token_tiles, DP, 0, 0, tiled=True)]
    ppermute x9, waiting for transfers between devices: 47.4 us -> 50.3 us  [shifted(): lax.ppermute(value, axis, [(i, (i + distance) % size) for i in range(size)])]
    unnamed x12 -> x8, local copies, waits for them, and re-layouts: 5.25 us -> 2.67 us
  transfers between devices with their start and end apart: 10 -> 11, of which waited for: 5 -> 5; matrix products, arithmetic and copies ran while one was open for 0% -> 0% of each run, Pallas kernels for 1% -> 0%
where the time goes in v4:
time: 152 us
  blocking collectives  53.9 us (35%)
  waiting for transfers between devices  50.3 us (33%)
  starting transfers between devices  21.3 us (14%)
  Pallas kernels  18.9 us (12%)
  other arithmetic  4.15 us (3%)
  local copies, waits for them, and re-layouts  2.86 us (2%)
    ppermute x9, waiting for transfers between devices, shifted(): lax.ppermute(value, axis, [(i, (i + distance) % size) for i in range(size)])  50.3 us
    all_gather x1, blocking collectives, body(): lax.all_gather((update * 256.0).astype(jnp.float16), DP, axis=0, tiled=Fa...  22.3 us
    pallas_call x4, Pallas kernels, call(): pl.pallas_call(kernel, out_shape=out_shape, in_specs=[whole(pltpu.SMEM if...  18.9 us
    all_to_all x1, blocking collectives, body(): lax.all_to_all(cut, 'z', 0, 0, tiled=True)  18.4 us
    all_to_all x1, blocking collectives, body(): own = lax.all_to_all(copies, 'z', 0, 0, tiled=True)  13.3 us
    ppermute x9, starting transfers between devices, shifted(): lax.ppermute(value, axis, [(i, (i + distance) % size) for i in range(size)])  9.19 us
    all_to_all x1, starting transfers between devices, body(): tokens = lax.all_to_all(gradient_token_tiles, DP, 0, 0, tiled=True)  6.63 us
    all_to_all x1, starting transfers between devices, body(): hidden = lax.all_to_all(hidden_token_tiles, DP, 0, 0, tiled=True)  5.45 us
  transfers between devices with their start and end apart: 11, of which 5 were waited for; matrix products, arithmetic and copies ran while one was open for 0% of the time, Pallas kernels for 0%

profile of v4, /device:TPU:1, one launch (start us, length us, event | category | flops | bytes accessed | tf_op | source)
XLA Modules:
  0.0 152.1 jit_solution(8650758743860033282)
XLA Ops:
  0.6 0.0 copy-start
  0.7 0.0 copy-start.1
  0.7 1.2 copy-done.1
  1.8 0.3 columns.1
  2.1 6.6 %all-to-all-start = ((bf16[8,224,128]{2,1,0:T(8,128)(2,1)}), bf16[8,224,128]{2,1,0:T(8,128)(2,1)S(1)}, u32[]{:S(2)}, u32[]{:S(2)}) async-start(bf16[8,224,128]{2,1,0:T(8,128)(2,1)} %param.5), calls=%async_computation | async-start | bytes 917504 | tf_op jit(solution)/shard_map/all_to_all | solution.py:223
  8.7 0.6 collective-permute-start
  9.3 2.1 %collective-permute-start.1 = (bf16[224,768]{1,0:T(8,128)(2,1)S(1)}, bf16[224,768]{1,0:T(8,128)(2,1)}, u32[]{:S(2)}, u32[]{:S(2)}) collective-permute-start(bf16[224,768]{1,0:T(8,128)(2,1)S(1)} %get-tuple-element.19), channel_id=1, source_target_pairs={{0,24},{8,0},{16,8},{24,16},{1,25},{9,1},{17,9},{25,17},{2,26},{10... | collective-permute-start | bytes 1032200 | tf_op jit(solution)/shard_map/ppermute | solution.py:204
  11.4 8.0 %collective-permute-done.refs_1_ = bf16[224,768]{1,0:T(8,128)(2,1)S(1)} collective-permute-done((bf16[224,768]{1,0:T(8,128)(2,1)S(1)}, bf16[224,768]{1,0:T(8,128)(2,1)S(1)}, u32[]{:S(2)}, u32[]{:S(2)}) %collective-permute-start) | collective-permute-done | bytes 344096 | tf_op jit(solution)/shard_map/ppermute | solution.py:204
  19.4 0.7 copy-done.3
  20.2 0.0 collective-permute-done.1.refs_3_
  20.2 0.0 all-to-all-done.tokens_ref
  20.2 5.5 %all-to-all-start.1 = ((bf16[8,128,1024]{2,1,0:T(8,128)(2,1)}), bf16[8,128,1024]{2,1,0:T(8,128)(2,1)S(1)}, u32[]{:S(2)}, u32[]{:S(2)}) async-start(bf16[8,128,1024]{2,1,0:T(8,128)(2,1)} %param.4), calls=%async_computation.1 | async-start | bytes 4194304 | tf_op jit(solution)/shard_map/all_to_all | solution.py:228
  25.6 2.0 %collective-permute-start.5 = (bf16[8,224,128]{2,1,0:T(8,128)(2,1)S(1)}, bf16[8,224,128]{2,1,0:T(8,128)(2,1)S(1)}, u32[]{:S(2)}, u32[]{:S(2)}) collective-permute-start(bf16[8,224,128]{2,1,0:T(8,128)(2,1)S(1)} %all-to-all-done.tokens_ref), channel_id=1, source_target_pairs={{0,24},{8,0},{16,8},{24,16},{1,25},{9,1},{17,9},{25,17},{2,26},{10... | collective-permute-start | bytes 1376264 | tf_op jit(solution)/shard_map/ppermute | solution.py:204
  27.7 0.0 collective-permute-start.4
  27.7 0.6 collective-permute-start.3
  28.3 2.4 %collective-permute-start.2 = (bf16[224,768]{1,0:T(8,128)(2,1)S(1)}, bf16[224,768]{1,0:T(8,128)(2,1)}, u32[]{:S(2)}, u32[]{:S(2)}) collective-permute-start(bf16[224,768]{1,0:T(8,128)(2,1)S(1)} %get-tuple-element.24), channel_id=1, source_target_pairs={{0,16},{8,24},{16,0},{24,8},{1,17},{9,25},{17,1},{25,9},{2,18},{10... | collective-permute-start | bytes 1032200 | tf_op jit(solution)/shard_map/ppermute | solution.py:204
  30.7 0.2 dynamic-slice_reduce_fusion.counts_ref
  30.9 27.5 %collective-permute-done.2.refs_2_ = bf16[224,768]{1,0:T(8,128)(2,1)} collective-permute-done((bf16[224,768]{1,0:T(8,128)(2,1)S(1)}, bf16[224,768]{1,0:T(8,128)(2,1)}, u32[]{:S(2)}, u32[]{:S(2)}) %collective-permute-start.2) | collective-permute-done | bytes 344096 | tf_op jit(solution)/shard_map/ppermute | solution.py:204
  58.4 0.7 copy-done.2
  59.1 5.1 %gram.1 = (f32[224,1024]{1,0:T(8,128)}, bf16[8,160,128]{2,1,0:T(8,128)(2,1)S(1)}) custom-call(s32[1]{0:T(128)} %bitcast.place_ref, s32[8]{0:T(128)S(1)} %dynamic-slice_reduce_fusion.counts_ref, bf16[8,128,1024]{2,1,0:T(8,128)(2,1)S(1)} %all-to-all-done.1.hidden_ref, bf16[8,224,128]{2,1,0:T(8,128)(2,1)S(1)} %all-to-all-done.tokens_ref, f32[224,1024]{1,0:T(8,128)} %bitcast.4, ...), custom_call_target="tpu_custom_call" | custom-call | tf_op jit(solution)/shard_map/gram/pallas_call | solution.py:188
  64.3 18.4 %all_to_all.20.parts_ref = bf16[8,160,128]{2,1,0:T(8,128)(2,1)S(1)} all-to-all(bf16[8,160,128]{2,1,0:T(8,128)(2,1)S(1)} %get-tuple-element.27), channel_id=1, replica_groups=mesh['y'=4,'core'=2,'x'=4,'z'=8] {'z'}, dimensions={0} | all-to-all | bytes 655360 | tf_op jit(solution)/shard_map/all_to_all | solution.py:250
  82.7 0.1 sum.1
  82.8 13.3 %all_to_all.21.refs_0_ = bf16[8,160,128]{2,1,0:T(8,128)(2,1)S(1)} all-to-all(bf16[8,160,128]{2,1,0:T(8,128)(2,1)S(1)} %sum.1), channel_id=1, replica_groups=mesh['y'=4,'core'=2,'x'=4,'z'=8] {'z'}, dimensions={0} | all-to-all | bytes 655360 | tf_op jit(solution)/shard_map/all_to_all | solution.py:252
  96.0 0.3 collective-permute-start.7
  96.4 1.1 collective-permute-start.6
  97.5 4.5 %collective-permute-done.8.refs_3_ = bf16[8,160,128]{2,1,0:T(8,128)(2,1)S(1)} collective-permute-done((bf16[8,160,128]{2,1,0:T(8,128)(2,1)S(1)}, bf16[8,160,128]{2,1,0:T(8,128)(2,1)S(1)}, u32[]{:S(2)}, u32[]{:S(2)}) %collective-permute-start.8) | collective-permute-done | bytes 327712 | tf_op jit(solution)/shard_map/ppermute | solution.py:204
  102.0 1.6 %collective-permute-done.7.refs_2_ = bf16[8,160,128]{2,1,0:T(8,128)(2,1)S(1)} collective-permute-done((bf16[8,160,128]{2,1,0:T(8,128)(2,1)S(1)}, bf16[8,160,128]{2,1,0:T(8,128)(2,1)S(1)}, u32[]{:S(2)}, u32[]{:S(2)}) %collective-permute-start.7) | collective-permute-done | bytes 327712 | tf_op jit(solution)/shard_map/ppermute | solution.py:204
  103.6 8.7 %collective-permute-done.6.refs_1_ = bf16[8,160,128]{2,1,0:T(8,128)(2,1)S(1)} collective-permute-done((bf16[8,160,128]{2,1,0:T(8,128)(2,1)S(1)}, bf16[8,160,128]{2,1,0:T(8,128)(2,1)S(1)}, u32[]{:S(2)}, u32[]{:S(2)}) %collective-permute-start.6) | collective-permute-done | bytes 327712 | tf_op jit(solution)/shard_map/ppermute | solution.py:204
  112.2 13.4 %polynomial.1 = f32[224,1024]{1,0:T(8,128)S(1)} custom-call(s32[1]{0:T(128)} %bitcast.place_ref, f32[224,1024]{1,0:T(8,128)} %get-tuple-element.26.moment_away_ref, bf16[8,160,128]{2,1,0:T(8,128)(2,1)S(1)} %all_to_all.21.refs_0_, bf16[8,160,128]{2,1,0:T(8,128)(2,1)S(1)} %collective-permute-done.6.refs_1_, ...), custom_call_target="tpu_custom_call" | custom-call | tf_op jit(solution)/shard_map/polynomial/pallas_call | solution.py:188
  125.6 0.1 multiply_convert_fusion
  125.7 22.3 %all-gather.2 = f16[1792,1024]{1,0:T(8,128)(2,1)S(1)} all-gather(f16[224,1024]{1,0:T(8,128)(2,1)S(1)} %multiply_convert_fusion), channel_id=2, replica_groups=mesh['y'=4,'core'=2,'x'=4,'z'=8] {'y','core'}, dimensions={0}, use_global_device_ids=true | all-gather | bytes 4128768 | tf_op jit(solution)/shard_map/all_gather | solution.py:267
  148.0 4.1 %convert_multiply_fusion = f32[1792,1024]{1,0:T(8,128)} fusion(f16[1792,1024]{1,0:T(8,128)(2,1)S(1)} %all-gather.2), kind=kLoop, calls=%fused_computation | loop fusion | flops 3670016 | bytes 11010048 | tf_op jit(solution)/shard_map/mul | solution.py:268
  (8 shorter events, 0.0 us)
Async XLA Ops:
  0.6 30.1 %copy-start = (s32[8,8]{1,0:T(8,128)S(1)}, s32[8,8]{1,0:T(8,128)}, u32[]{:S(2)}) copy-start(s32[8,8]{1,0:T(8,128)} %param.7) | copy-start | bytes 772
  0.7 1.2 copy-start.1
  2.1 18.1 %all-to-all-start = ((bf16[8,224,128]{2,1,0:T(8,128)(2,1)}), bf16[8,224,128]{2,1,0:T(8,128)(2,1)S(1)}, u32[]{:S(2)}, u32[]{:S(2)}) async-start(bf16[8,224,128]{2,1,0:T(8,128)(2,1)} %param.5), calls=%async_computation | async-start | bytes 917504 | tf_op jit(solution)/shard_map/all_to_all | solution.py:223
  8.7 10.7 %collective-permute-start = (bf16[224,768]{1,0:T(8,128)(2,1)S(1)}, bf16[224,768]{1,0:T(8,128)(2,1)S(1)}, u32[]{:S(2)}, u32[]{:S(2)}) collective-permute-start(bf16[224,768]{1,0:T(8,128)(2,1)S(1)} %get-tuple-element.18), channel_id=1, source_target_pairs={{0,8},{8,16},{16,24},{24,0},{1,9},{9,17},{17,25},{25,1},{2,10},{10... | collective-permute-start | bytes 1032200 | tf_op jit(solution)/shard_map/ppermute | solution.py:204
  9.3 10.9 %collective-permute-start.1 = (bf16[224,768]{1,0:T(8,128)(2,1)S(1)}, bf16[224,768]{1,0:T(8,128)(2,1)}, u32[]{:S(2)}, u32[]{:S(2)}) collective-permute-start(bf16[224,768]{1,0:T(8,128)(2,1)S(1)} %get-tuple-element.19), channel_id=1, source_target_pairs={{0,24},{8,0},{16,8},{24,16},{1,25},{9,1},{17,9},{25,17},{2,26},{10... | collective-permute-start | bytes 1032200 | tf_op jit(solution)/shard_map/ppermute | solution.py:204
  19.4 0.8 copy-start.3
  20.2 38.2 %all-to-all-start.1 = ((bf16[8,128,1024]{2,1,0:T(8,128)(2,1)}), bf16[8,128,1024]{2,1,0:T(8,128)(2,1)S(1)}, u32[]{:S(2)}, u32[]{:S(2)}) async-start(bf16[8,128,1024]{2,1,0:T(8,128)(2,1)} %param.4), calls=%async_computation.1 | async-start | bytes 4194304 | tf_op jit(solution)/shard_map/all_to_all | solution.py:228
  25.6 32.7 %collective-permute-start.5 = (bf16[8,224,128]{2,1,0:T(8,128)(2,1)S(1)}, bf16[8,224,128]{2,1,0:T(8,128)(2,1)S(1)}, u32[]{:S(2)}, u32[]{:S(2)}) collective-permute-start(bf16[8,224,128]{2,1,0:T(8,128)(2,1)S(1)} %all-to-all-done.tokens_ref), channel_id=1, source_target_pairs={{0,24},{8,0},{16,8},{24,16},{1,25},{9,1},{17,9},{25,17},{2,26},{10... | collective-permute-start | bytes 1376264 | tf_op jit(solution)/shard_map/ppermute | solution.py:204
  27.7 30.7 %collective-permute-start.4 = (bf16[8,224,128]{2,1,0:T(8,128)(2,1)S(1)}, bf16[8,224,128]{2,1,0:T(8,128)(2,1)}, u32[]{:S(2)}, u32[]{:S(2)}) collective-permute-start(bf16[8,224,128]{2,1,0:T(8,128)(2,1)S(1)} %all-to-all-done.tokens_ref), channel_id=1, source_target_pairs={{0,16},{8,24},{16,0},{24,8},{1,17},{9,25},{17,1},{25,9},{2,18},{10... | collective-permute-start | bytes 1376264 | tf_op jit(solution)/shard_map/ppermute | solution.py:204
  27.7 30.7 %collective-permute-start.3 = (bf16[8,224,128]{2,1,0:T(8,128)(2,1)S(1)}, bf16[8,224,128]{2,1,0:T(8,128)(2,1)}, u32[]{:S(2)}, u32[]{:S(2)}) collective-permute-start(bf16[8,224,128]{2,1,0:T(8,128)(2,1)S(1)} %all-to-all-done.tokens_ref), channel_id=1, source_target_pairs={{0,8},{8,16},{16,24},{24,0},{1,9},{9,17},{17,25},{25,1},{2,10},{10... | collective-permute-start | bytes 1376264 | tf_op jit(solution)/shard_map/ppermute | solution.py:204
  28.3 30.1 %collective-permute-start.2 = (bf16[224,768]{1,0:T(8,128)(2,1)S(1)}, bf16[224,768]{1,0:T(8,128)(2,1)}, u32[]{:S(2)}, u32[]{:S(2)}) collective-permute-start(bf16[224,768]{1,0:T(8,128)(2,1)S(1)} %get-tuple-element.24), channel_id=1, source_target_pairs={{0,16},{8,24},{16,0},{24,8},{1,17},{9,25},{17,1},{25,9},{2,18},{10... | collective-permute-start | bytes 1032200 | tf_op jit(solution)/shard_map/ppermute | solution.py:204
  58.4 0.8 copy-start.2
  96.0 5.9 %collective-permute-start.8 = (bf16[8,160,128]{2,1,0:T(8,128)(2,1)S(1)}, bf16[8,160,128]{2,1,0:T(8,128)(2,1)S(1)}, u32[]{:S(2)}, u32[]{:S(2)}) collective-permute-start(bf16[8,160,128]{2,1,0:T(8,128)(2,1)S(1)} %all_to_all.21.refs_0_), channel_id=1, source_target_pairs={{0,24},{8,0},{16,8},{24,16},{1,25},{9,1},{17,9},{25,17},{2,26},{10... | collective-permute-start | bytes 983048 | tf_op jit(solution)/shard_map/ppermute | solution.py:204
  96.0 7.5 %collective-permute-start.7 = (bf16[8,160,128]{2,1,0:T(8,128)(2,1)S(1)}, bf16[8,160,128]{2,1,0:T(8,128)(2,1)S(1)}, u32[]{:S(2)}, u32[]{:S(2)}) collective-permute-start(bf16[8,160,128]{2,1,0:T(8,128)(2,1)S(1)} %all_to_all.21.refs_0_), channel_id=1, source_target_pairs={{0,16},{8,24},{16,0},{24,8},{1,17},{9,25},{17,1},{25,9},{2,18},{10... | collective-permute-start | bytes 983048 | tf_op jit(solution)/shard_map/ppermute | solution.py:204
  96.4 15.9 %collective-permute-start.6 = (bf16[8,160,128]{2,1,0:T(8,128)(2,1)S(1)}, bf16[8,160,128]{2,1,0:T(8,128)(2,1)S(1)}, u32[]{:S(2)}, u32[]{:S(2)}) collective-permute-start(bf16[8,160,128]{2,1,0:T(8,128)(2,1)S(1)} %all_to_all.21.refs_0_), channel_id=1, source_target_pairs={{0,8},{8,16},{16,24},{24,0},{1,9},{9,17},{17,25},{25,1},{2,10},{10... | collective-permute-start | bytes 983048 | tf_op jit(solution)/shard_map/ppermute | solution.py:204

commit v5 on v4

--- a/solution.py
+++ b/solution.py
@@ -14,6 +14,7 @@
 BLOCK = 128
 UNIT = 16
 NEEDED = 6
+CORES = 2
 
 MOMENTUM_DECAY = 0.95
 EPSILON = 1e-07
@@ -51,11 +52,18 @@
     return pl.ds(pl.multiple_of(lax.rem(2 * place + block, FF // BLOCK) * BLOCK, BLOCK), BLOCK)
 
 
-def columns_kernel(place_ref, momentum_ref, *column_refs):
+def outgoing_kernel(place_ref, group_ref, momentum_ref, tokens_ref, *refs):
+    *column_refs, kept_ref, sent_ref = refs
+    chip, core = lax.div(group_ref[0], CORES), lax.rem(group_ref[0], CORES)
+    chips = kept_ref.shape[0]
     for distance, column_ref in enumerate(column_refs, 1):
         for block in range(NEEDED):
             value = momentum_ref[:, column(place_ref[0] + distance, block)]
             column_ref[:, block * BLOCK : (block + 1) * BLOCK] = value.astype(BF16)
+    for distance in range(chips):
+        first = lax.rem(chip + distance, chips) * CORES
+        kept_ref[distance] = tokens_ref[first + core]
+        sent_ref[distance] = tokens_ref[first + 1 - core]
 
 
 def fetched(sources, targets, semaphores):
@@ -68,7 +76,7 @@
     return copies
 
 
-def gram_kernel(place_ref, counts_ref, hidden_ref, tokens_ref, *refs):
+def gram_kernel(place_ref, group_ref, counts_ref, hidden_ref, tokens_ref, *refs):
     count = (len(refs) - 4) // 2
     away_refs, moment_ref, cut_ref, needed_ref = refs[:count], *refs[count : count + 3]
     here_refs, semaphores = refs[count + 3 : -1], refs[-1]
@@ -79,8 +87,13 @@
     lanes = lax.broadcasted_iota(jnp.int32, (height, width), 1)
 
     def tokens_of(ref):
-        kept = [jnp.where(lanes < counts_ref[g] * TILE, ref[g].astype(F32), 0.0) for g in range(groups)]
-        return jnp.concatenate(kept, axis=1).astype(BF16)
+        kept = []
+        for g in range(groups):
+            chip, core = divmod(g, CORES)
+            distance = lax.rem(lax.div(group_ref[0], CORES) - chip + groups, groups // CORES)
+            tokens = ref[CORES * distance + lax.rem(group_ref[0] + core, CORES)].astype(F32)
+            kept.append(jnp.where(lanes < counts_ref[g] * TILE, tokens, 0.0).astype(BF16))
+        return jnp.concatenate(kept, axis=1)
 
     gradient = jnp.dot(
         tokens_of(tokens_ref), hidden_ref[...].reshape(groups * width, FF), preferred_element_type=F32
@@ -208,24 +221,26 @@
     along_x, along_z = lax.axis_size("x"), lax.axis_size("z")
     rows = momentum.shape[1]
     piece = len(block_pairs(0)) * BLOCK // along_z
-    counts = lax.dynamic_index_in_dim(filled_tile_count, lax.axis_index(DP), 1, keepdims=False)
+    group = lax.axis_index(DP).astype(jnp.int32)
+    counts = lax.dynamic_index_in_dim(filled_tile_count, group, 1, keepdims=False)
+    group = group.reshape(1)
     place = lax.axis_index("x").astype(jnp.int32).reshape(1)
     distances = range(1, along_x)
-
-    columns = call(
-        columns_kernel,
-        [jax.ShapeDtypeStruct((rows, NEEDED * BLOCK), BF16) for _ in distances],
-        [place, momentum[0]],
-        scalars=1,
-    )
-    columns, gradient_token_tiles = lax.optimization_barrier((columns, gradient_token_tiles))
+    along_y = lax.axis_size("y")
+
+    hidden = lax.all_to_all(hidden_token_tiles, DP, 0, 0, tiled=True)
+    half = jax.ShapeDtypeStruct((along_y, *gradient_token_tiles.shape[1:]), BF16)
+    *columns, kept, sent = call(
+        outgoing_kernel,
+        [jax.ShapeDtypeStruct((rows, NEEDED * BLOCK), BF16) for _ in distances] + [half, half],
+        [place, group, momentum[0], gradient_token_tiles],
+        scalars=2,
+    )
     other_columns = [shifted(columns[k - 1], "x", k) for k in distances]
-    tokens = lax.all_to_all(gradient_token_tiles, DP, 0, 0, tiled=True)
-    other_columns[0], other_columns[-1], tokens, hidden_token_tiles = lax.optimization_barrier(
-        (other_columns[0], other_columns[-1], tokens, hidden_token_tiles)
-    )
+    both = jnp.stack([kept, shifted(sent, "core", 1)], axis=1)
+    tokens = jnp.concatenate([both[0]] + [shifted(both[k], "y", k) for k in range(1, along_y)])
+    *other_columns, tokens = lax.optimization_barrier((*other_columns, tokens))
     other_tokens = [shifted(tokens, "x", k) for k in distances]
-    hidden = lax.all_to_all(hidden_token_tiles, DP, 0, 0, tiled=True)
     fetch = [
         pltpu.with_memory_space_constraint(value, pltpu.HBM)
         for value in [momentum[0]] + other_columns + other_tokens
@@ -236,12 +251,12 @@
             jax.ShapeDtypeStruct((rows, FF), F32),
             jax.ShapeDtypeStruct((along_z, piece + UNIT, BLOCK), BF16),
         ),
-        [place, counts, hidden, tokens] + fetch,
+        [place, group, counts, hidden, tokens] + fetch,
         scratch=[pltpu.VMEM((hidden.shape[0] * hidden.shape[1], NEEDED * BLOCK), BF16)]
         + [pltpu.VMEM(value.shape, value.dtype) for value in fetch]
         + [pltpu.SemaphoreType.DMA((len(fetch),))],
-        away=range(4, 4 + len(fetch)),
-        scalars=2,
+        away=range(5, 5 + len(fetch)),
+        scalars=3,
         mib=28,
     )
     copies = call(

time: 152 us -> 163 us (1.072)
  waiting for transfers between devices: 50.3 us -> 62.1 us
  starting transfers between devices: 21.3 us -> 18.8 us
    ppermute x9 -> x13, waiting for transfers between devices: 50.3 us -> 62.1 us  [shifted(): lax.ppermute(value, axis, [(i, (i + distance) % size) for i in range(size)])]
    all_to_all x1 -> x0, starting transfers between devices: 6.63 us -> none  [body(): tokens = lax.all_to_all(gradient_token_tiles, DP, 0, 0, tiled=True)]
    ppermute x9 -> x13, starting transfers between devices: 9.19 us -> 12.1 us  [shifted(): lax.ppermute(value, axis, [(i, (i + distance) % size) for i in range(size)])]
    all_to_all x1, blocking collectives: 18.4 us -> 20.6 us  [body(): lax.all_to_all(cut, 'z', 0, 0, tiled=True)]
  transfers between devices with their start and end apart: 11 -> 14, of which waited for: 5 -> 9; matrix products, arithmetic and copies ran while one was open for 0% -> 0% of each run, Pallas kernels for 0% -> 0%
where the time goes in v5:
time: 163 us; the launch traced here: 162 us
  waiting for transfers between devices  62.1 us (38%)
  blocking collectives  54.5 us (33%)
  Pallas kernels  19.5 us (12%)
  starting transfers between devices  18.8 us (12%)
  other arithmetic  4.25 us (3%)
  local copies, waits for them, and re-layouts  2.41 us (1%)
    ppermute x13, waiting for transfers between devices, shifted(): lax.ppermute(value, axis, [(i, (i + distance) % size) for i in range(size)])  62.1 us
    all_gather x1, blocking collectives, body(): lax.all_gather((update * 256.0).astype(jnp.float16), DP, axis=0, tiled=Fa...  20.8 us
    all_to_all x1, blocking collectives, body(): lax.all_to_all(cut, 'z', 0, 0, tiled=True)  20.6 us
    pallas_call x4, Pallas kernels, call(): pl.pallas_call(kernel, out_shape=out_shape, in_specs=[whole(pltpu.SMEM if...  19.5 us
    all_to_all x1, blocking collectives, body(): own = lax.all_to_all(copies, 'z', 0, 0, tiled=True)  13.1 us
    ppermute x13, starting transfers between devices, shifted(): lax.ppermute(value, axis, [(i, (i + distance) % size) for i in range(size)])  12.1 us
    all_to_all x1, starting transfers between devices, body(): hidden = lax.all_to_all(hidden_token_tiles, DP, 0, 0, tiled=True)  6.76 us
    mul x1, other arithmetic, body(): return (moment[None], gathered.astype(F32) * (1.0 / 256.0))  4.07 us
  transfers between devices with their start and end apart: 14, of which 9 were waited for; matrix products, arithmetic and copies ran while one was open for 0% of the time, Pallas kernels for 0%

profile of v5, /device:TPU:1, one launch (start us, length us, event | category | flops | bytes accessed | tf_op | source)
XLA Modules:
  0.0 162.3 jit_solution(12259848263810676576)
XLA Ops:
  0.6 6.8 %all-to-all-start = ((bf16[8,128,1024]{2,1,0:T(8,128)(2,1)}), bf16[8,128,1024]{2,1,0:T(8,128)(2,1)S(1)}, u32[]{:S(2)}, u32[]{:S(2)}) async-start(bf16[8,128,1024]{2,1,0:T(8,128)(2,1)} %param.4), calls=%async_computation | async-start | bytes 4194304 | tf_op jit(solution)/shard_map/all_to_all | solution.py:231
  7.4 1.2 copy-done.1
  8.6 1.0 copy-done.2
  9.6 0.3 outgoing.1
  9.9 0.2 collective-permute-start.3
  10.1 1.4 collective-permute-done.3
  11.5 1.5 collective-permute-start.4
  13.0 0.4 collective-permute-start
  13.4 2.5 %collective-permute-start.1 = (bf16[224,768]{1,0:T(8,128)(2,1)S(1)}, bf16[224,768]{1,0:T(8,128)(2,1)S(1)}, u32[]{:S(2)}, u32[]{:S(2)}) collective-permute-start(bf16[224,768]{1,0:T(8,128)(2,1)S(1)} %get-tuple-element.14), channel_id=1, source_target_pairs={{0,16},{8,24},{16,0},{24,8},{1,17},{9,25},{17,1},{25,9},{2,18},{10... | collective-permute-start | bytes 1032200 | tf_op jit(solution)/shard_map/ppermute | solution.py:217
  15.9 1.2 collective-permute-start.2
  17.0 1.3 collective-permute-start.6
  18.3 17.8 %collective-permute-done.4 = bf16[2,224,128]{2,1,0:T(8,128)(2,1)S(1)} collective-permute-done((bf16[2,224,128]{2,1,0:T(8,128)(2,1)S(1)}, bf16[2,224,128]{2,1,0:T(8,128)(2,1)S(1)}, u32[]{:S(2)}, u32[]{:S(2)}) %collective-permute-start.4) | collective-permute-done | bytes 114720 | tf_op jit(solution)/shard_map/ppermute | solution.py:217
  36.1 0.4 collective-permute-start.5
  36.5 5.1 %collective-permute-done.5 = bf16[2,224,128]{2,1,0:T(8,128)(2,1)S(1)} collective-permute-done((bf16[2,224,128]{2,1,0:T(8,128)(2,1)S(1)}, bf16[2,224,128]{2,1,0:T(8,128)(2,1)S(1)}, u32[]{:S(2)}, u32[]{:S(2)}) %collective-permute-start.5) | collective-permute-done | bytes 114720 | tf_op jit(solution)/shard_map/ppermute | solution.py:217
  41.7 1.7 %collective-permute-start.9 = (bf16[8,224,128]{2,1,0:T(8,128)(2,1)S(1)}, bf16[8,224,128]{2,1,0:T(8,128)(2,1)S(1)}, u32[]{:S(2)}, u32[]{:S(2)}) collective-permute-start(bf16[8,224,128]{2,1,0:T(8,128)(2,1)S(1)} %pad_maximum_fusion.tokens_ref), channel_id=1, source_target_pairs={{0,24},{8,0},{16,8},{24,16},{1,25},{9,1},{17,9},{25,17},{2,26},{10... | collective-permute-start | bytes 1376264 | tf_op jit(solution)/shard_map/ppermute | solution.py:217
  43.4 0.9 collective-permute-start.8
  44.3 0.3 collective-permute-start.7
  44.6 0.2 dynamic-slice_reduce_fusion.counts_ref
  44.8 7.4 %collective-permute-done.9.refs_6_ = bf16[8,224,128]{2,1,0:T(8,128)(2,1)S(1)} collective-permute-done((bf16[8,224,128]{2,1,0:T(8,128)(2,1)S(1)}, bf16[8,224,128]{2,1,0:T(8,128)(2,1)S(1)}, u32[]{:S(2)}, u32[]{:S(2)}) %collective-permute-start.9) | collective-permute-done | bytes 458784 | tf_op jit(solution)/shard_map/ppermute | solution.py:217
  52.2 2.9 %collective-permute-done.8.refs_5_ = bf16[8,224,128]{2,1,0:T(8,128)(2,1)S(1)} collective-permute-done((bf16[8,224,128]{2,1,0:T(8,128)(2,1)S(1)}, bf16[8,224,128]{2,1,0:T(8,128)(2,1)S(1)}, u32[]{:S(2)}, u32[]{:S(2)}) %collective-permute-start.8) | collective-permute-done | bytes 458784 | tf_op jit(solution)/shard_map/ppermute | solution.py:217
  55.1 12.2 %collective-permute-done.7.refs_4_ = bf16[8,224,128]{2,1,0:T(8,128)(2,1)} collective-permute-done((bf16[8,224,128]{2,1,0:T(8,128)(2,1)S(1)}, bf16[8,224,128]{2,1,0:T(8,128)(2,1)}, u32[]{:S(2)}, u32[]{:S(2)}) %collective-permute-start.7) | collective-permute-done | bytes 458784 | tf_op jit(solution)/shard_map/ppermute | solution.py:217
  67.3 5.7 %gram.1 = (f32[224,1024]{1,0:T(8,128)}, bf16[8,160,128]{2,1,0:T(8,128)(2,1)S(1)}) custom-call(s32[1]{0:T(128)} %bitcast.place_ref, s32[1]{0:T(128)} %bitcast.1.group_ref, s32[8]{0:T(128)S(1)} %dynamic-slice_reduce_fusion.counts_ref, bf16[8,128,1024]{2,1,0:T(8,128)(2,1)S(1)} %all-to-all-done.hidden_ref, bf16[8,224,128]{2,1,0:T(8,128)(2,1)S(1)} %pad_maximum_fusion.tokens_ref, ...), custom_call_target="tpu_custom_call" | custom-call | tf_op jit(solution)/shard_map/gram/pallas_call | solution.py:201
  73.0 20.6 %all_to_all.15.parts_ref = bf16[8,160,128]{2,1,0:T(8,128)(2,1)S(1)} all-to-all(bf16[8,160,128]{2,1,0:T(8,128)(2,1)S(1)} %get-tuple-element.23), channel_id=1, replica_groups=mesh['y'=4,'core'=2,'x'=4,'z'=8] {'z'}, dimensions={0} | all-to-all | bytes 655360 | tf_op jit(solution)/shard_map/all_to_all | solution.py:265
  93.7 13.1 %all_to_all.16.refs_0_ = bf16[8,160,128]{2,1,0:T(8,128)(2,1)S(1)} all-to-all(bf16[8,160,128]{2,1,0:T(8,128)(2,1)S(1)} %sum.1), channel_id=1, replica_groups=mesh['y'=4,'core'=2,'x'=4,'z'=8] {'z'}, dimensions={0} | all-to-all | bytes 655360 | tf_op jit(solution)/shard_map/all_to_all | solution.py:267
  106.8 0.9 collective-permute-start.11
  107.7 0.9 collective-permute-start.10
  108.6 4.2 %collective-permute-done.12.refs_3_ = bf16[8,160,128]{2,1,0:T(8,128)(2,1)S(1)} collective-permute-done((bf16[8,160,128]{2,1,0:T(8,128)(2,1)S(1)}, bf16[8,160,128]{2,1,0:T(8,128)(2,1)S(1)}, u32[]{:S(2)}, u32[]{:S(2)}) %collective-permute-start.12) | collective-permute-done | bytes 327712 | tf_op jit(solution)/shard_map/ppermute | solution.py:217
  112.7 1.6 collective-permute-done.11.refs_2_
  114.3 9.6 %collective-permute-done.10.refs_1_ = bf16[8,160,128]{2,1,0:T(8,128)(2,1)S(1)} collective-permute-done((bf16[8,160,128]{2,1,0:T(8,128)(2,1)S(1)}, bf16[8,160,128]{2,1,0:T(8,128)(2,1)S(1)}, u32[]{:S(2)}, u32[]{:S(2)}) %collective-permute-start.10) | collective-permute-done | bytes 327712 | tf_op jit(solution)/shard_map/ppermute | solution.py:217
  124.0 13.4 %polynomial.1 = f32[224,1024]{1,0:T(8,128)S(1)} custom-call(s32[1]{0:T(128)} %bitcast.place_ref, f32[224,1024]{1,0:T(8,128)} %get-tuple-element.22.moment_away_ref, bf16[8,160,128]{2,1,0:T(8,128)(2,1)S(1)} %all_to_all.16.refs_0_, bf16[8,160,128]{2,1,0:T(8,128)(2,1)S(1)} %collective-permute-done.10.refs_1_, ...), custom_call_target="tpu_custom_call" | custom-call | tf_op jit(solution)/shard_map/polynomial/pallas_call | solution.py:201
  137.5 20.8 %all-gather.2 = f16[1792,1024]{1,0:T(8,128)(2,1)S(1)} all-gather(f16[224,1024]{1,0:T(8,128)(2,1)S(1)} %multiply_convert_fusion), channel_id=2, replica_groups=mesh['y'=4,'core'=2,'x'=4,'z'=8] {'y','core'}, dimensions={0}, use_global_device_ids=true | all-gather | bytes 4128768 | tf_op jit(solution)/shard_map/all_gather | solution.py:282
  158.2 4.1 %convert_multiply_fusion = f32[1792,1024]{1,0:T(8,128)} fusion(f16[1792,1024]{1,0:T(8,128)(2,1)S(1)} %all-gather.2), kind=kLoop, calls=%fused_computation | loop fusion | flops 3670016 | bytes 11010048 | tf_op jit(solution)/shard_map/mul | solution.py:283
  (24 shorter events, 0.3 us)
Async XLA Ops:
  0.6 44.0 %copy-start = (s32[8,8]{1,0:T(8,128)S(1)}, s32[8,8]{1,0:T(8,128)}, u32[]{:S(2)}) copy-start(s32[8,8]{1,0:T(8,128)} %param.7) | copy-start | bytes 772
  0.6 66.7 %all-to-all-start = ((bf16[8,128,1024]{2,1,0:T(8,128)(2,1)}), bf16[8,128,1024]{2,1,0:T(8,128)(2,1)S(1)}, u32[]{:S(2)}, u32[]{:S(2)}) async-start(bf16[8,128,1024]{2,1,0:T(8,128)(2,1)} %param.4), calls=%async_computation | async-start | bytes 4194304 | tf_op jit(solution)/shard_map/all_to_all | solution.py:231
  7.4 1.2 copy-start.1
  8.6 1.0 copy-start.2
  9.9 1.6 collective-permute-start.3
  11.5 24.6 %collective-permute-start.4 = (bf16[2,224,128]{2,1,0:T(8,128)(2,1)S(1)}, bf16[2,224,128]{2,1,0:T(8,128)(2,1)S(1)}, u32[]{:S(2)}, u32[]{:S(2)}) collective-permute-start(bf16[2,224,128]{2,1,0:T(8,128)(2,1)S(1)} %get-tuple-element.25), channel_id=1, source_target_pairs={{0,64},{64,128},{128,192},{192,0},{1,65},{65,129},{129,193},{193,1... | collective-permute-start | bytes 344072 | tf_op jit(solution)/shard_map/ppermute | solution.py:217
  13.0 28.7 %collective-permute-start = (bf16[224,768]{1,0:T(8,128)(2,1)S(1)}, bf16[224,768]{1,0:T(8,128)(2,1)S(1)}, u32[]{:S(2)}, u32[]{:S(2)}) collective-permute-start(bf16[224,768]{1,0:T(8,128)(2,1)S(1)} %get-tuple-element.13), channel_id=1, source_target_pairs={{0,8},{8,16},{16,24},{24,0},{1,9},{9,17},{17,25},{25,1},{2,10},{10... | collective-permute-start | bytes 1032200 | tf_op jit(solution)/shard_map/ppermute | solution.py:217
  13.4 28.2 %collective-permute-start.1 = (bf16[224,768]{1,0:T(8,128)(2,1)S(1)}, bf16[224,768]{1,0:T(8,128)(2,1)S(1)}, u32[]{:S(2)}, u32[]{:S(2)}) collective-permute-start(bf16[224,768]{1,0:T(8,128)(2,1)S(1)} %get-tuple-element.14), channel_id=1, source_target_pairs={{0,16},{8,24},{16,0},{24,8},{1,17},{9,25},{17,1},{25,9},{2,18},{10... | collective-permute-start | bytes 1032200 | tf_op jit(solution)/shard_map/ppermute | solution.py:217
  15.9 25.8 %collective-permute-start.2 = (bf16[224,768]{1,0:T(8,128)(2,1)S(1)}, bf16[224,768]{1,0:T(8,128)(2,1)S(1)}, u32[]{:S(2)}, u32[]{:S(2)}) collective-permute-start(bf16[224,768]{1,0:T(8,128)(2,1)S(1)} %get-tuple-element.15), channel_id=1, source_target_pairs={{0,24},{8,0},{16,8},{24,16},{1,25},{9,1},{17,9},{25,17},{2,26},{10... | collective-permute-start | bytes 1032200 | tf_op jit(solution)/shard_map/ppermute | solution.py:217
  17.0 19.5 %collective-permute-start.6 = (bf16[2,224,128]{2,1,0:T(8,128)(2,1)S(1)}, bf16[2,224,128]{2,1,0:T(8,128)(2,1)S(1)}, u32[]{:S(2)}, u32[]{:S(2)}) collective-permute-start(bf16[2,224,128]{2,1,0:T(8,128)(2,1)S(1)} %get-tuple-element.26), channel_id=1, source_target_pairs={{0,192},{64,0},{128,64},{192,128},{1,193},{65,1},{129,65},{193,129... | collective-permute-start | bytes 344072 | tf_op jit(solution)/shard_map/ppermute | solution.py:217
  36.1 5.5 %collective-permute-start.5 = (bf16[2,224,128]{2,1,0:T(8,128)(2,1)S(1)}, bf16[2,224,128]{2,1,0:T(8,128)(2,1)S(1)}, u32[]{:S(2)}, u32[]{:S(2)}) collective-permute-start(bf16[2,224,128]{2,1,0:T(8,128)(2,1)S(1)} %get-tuple-element.27), channel_id=1, source_target_pairs={{0,128},{64,192},{128,0},{192,64},{1,129},{65,193},{129,1},{193,65... | collective-permute-start | bytes 344072 | tf_op jit(solution)/shard_map/ppermute | solution.py:217
  41.7 1.8 %copy-start.5 = (bf16[224,768]{1,0:T(8,128)(2,1)}, bf16[224,768]{1,0:T(8,128)(2,1)S(1)}, u32[]{:S(2)}) copy-start(bf16[224,768]{1,0:T(8,128)(2,1)S(1)} %collective-permute-done.refs_1_) | copy-start | bytes 1032196
  41.7 2.6 %copy-start.6 = (bf16[224,768]{1,0:T(8,128)(2,1)}, bf16[224,768]{1,0:T(8,128)(2,1)S(1)}, u32[]{:S(2)}) copy-start(bf16[224,768]{1,0:T(8,128)(2,1)S(1)} %collective-permute-done.1.refs_2_) | copy-start | bytes 1032196
  41.7 2.6 %copy-start.7 = (bf16[224,768]{1,0:T(8,128)(2,1)}, bf16[224,768]{1,0:T(8,128)(2,1)S(1)}, u32[]{:S(2)}) copy-start(bf16[224,768]{1,0:T(8,128)(2,1)S(1)} %collective-permute-done.2.refs_3_) | copy-start | bytes 1032196
  41.7 10.5 %collective-permute-start.9 = (bf16[8,224,128]{2,1,0:T(8,128)(2,1)S(1)}, bf16[8,224,128]{2,1,0:T(8,128)(2,1)S(1)}, u32[]{:S(2)}, u32[]{:S(2)}) collective-permute-start(bf16[8,224,128]{2,1,0:T(8,128)(2,1)S(1)} %pad_maximum_fusion.tokens_ref), channel_id=1, source_target_pairs={{0,24},{8,0},{16,8},{24,16},{1,25},{9,1},{17,9},{25,17},{2,26},{10... | collective-permute-start | bytes 1376264 | tf_op jit(solution)/shard_map/ppermute | solution.py:217
  43.4 11.7 %collective-permute-start.8 = (bf16[8,224,128]{2,1,0:T(8,128)(2,1)S(1)}, bf16[8,224,128]{2,1,0:T(8,128)(2,1)S(1)}, u32[]{:S(2)}, u32[]{:S(2)}) collective-permute-start(bf16[8,224,128]{2,1,0:T(8,128)(2,1)S(1)} %pad_maximum_fusion.tokens_ref), channel_id=1, source_target_pairs={{0,16},{8,24},{16,0},{24,8},{1,17},{9,25},{17,1},{25,9},{2,18},{10... | collective-permute-start | bytes 1376264 | tf_op jit(solution)/shard_map/ppermute | solution.py:217
  44.3 23.0 %collective-permute-start.7 = (bf16[8,224,128]{2,1,0:T(8,128)(2,1)S(1)}, bf16[8,224,128]{2,1,0:T(8,128)(2,1)}, u32[]{:S(2)}, u32[]{:S(2)}) collective-permute-start(bf16[8,224,128]{2,1,0:T(8,128)(2,1)S(1)} %pad_maximum_fusion.tokens_ref), channel_id=1, source_target_pairs={{0,8},{8,16},{16,24},{24,0},{1,9},{9,17},{17,25},{25,1},{2,10},{10... | collective-permute-start | bytes 1376264 | tf_op jit(solution)/shard_map/ppermute | solution.py:217
  52.2 15.1 %copy-start.3 = (bf16[8,224,128]{2,1,0:T(8,128)(2,1)}, bf16[8,224,128]{2,1,0:T(8,128)(2,1)S(1)}, u32[]{:S(2)}) copy-start(bf16[8,224,128]{2,1,0:T(8,128)(2,1)S(1)} %collective-permute-done.9.refs_6_) | copy-start | bytes 1376260
  55.1 12.2 %copy-start.4 = (bf16[8,224,128]{2,1,0:T(8,128)(2,1)}, bf16[8,224,128]{2,1,0:T(8,128)(2,1)S(1)}, u32[]{:S(2)}) copy-start(bf16[8,224,128]{2,1,0:T(8,128)(2,1)S(1)} %collective-permute-done.8.refs_5_) | copy-start | bytes 1376260
  106.8 5.9 %collective-permute-start.12 = (bf16[8,160,128]{2,1,0:T(8,128)(2,1)S(1)}, bf16[8,160,128]{2,1,0:T(8,128)(2,1)S(1)}, u32[]{:S(2)}, u32[]{:S(2)}) collective-permute-start(bf16[8,160,128]{2,1,0:T(8,128)(2,1)S(1)} %all_to_all.16.refs_0_), channel_id=1, source_target_pairs={{0,24},{8,0},{16,8},{24,16},{1,25},{9,1},{17,9},{25,17},{2,26},{10... | collective-permute-start | bytes 983048 | tf_op jit(solution)/shard_map/ppermute | solution.py:217
  106.8 7.5 %collective-permute-start.11 = (bf16[8,160,128]{2,1,0:T(8,128)(2,1)S(1)}, bf16[8,160,128]{2,1,0:T(8,128)(2,1)S(1)}, u32[]{:S(2)}, u32[]{:S(2)}) collective-permute-start(bf16[8,160,128]{2,1,0:T(8,128)(2,1)S(1)} %all_to_all.16.refs_0_), channel_id=1, source_target_pairs={{0,16},{8,24},{16,0},{24,8},{1,17},{9,25},{17,1},{25,9},{2,18},{10... | collective-permute-start | bytes 983048 | tf_op jit(solution)/shard_map/ppermute | solution.py:217
  107.7 16.3 %collective-permute-start.10 = (bf16[8,160,128]{2,1,0:T(8,128)(2,1)S(1)}, bf16[8,160,128]{2,1,0:T(8,128)(2,1)S(1)}, u32[]{:S(2)}, u32[]{:S(2)}) collective-permute-start(bf16[8,160,128]{2,1,0:T(8,128)(2,1)S(1)} %all_to_all.16.refs_0_), channel_id=1, source_target_pairs={{0,8},{8,16},{16,24},{24,0},{1,9},{9,17},{17,25},{25,1},{2,10},{10... | collective-permute-start | bytes 983048 | tf_op jit(solution)/shard_map/ppermute | solution.py:217

commit v6 on v5

--- a/solution.py
+++ b/solution.py
@@ -228,7 +228,6 @@
     distances = range(1, along_x)
     along_y = lax.axis_size("y")
 
-    hidden = lax.all_to_all(hidden_token_tiles, DP, 0, 0, tiled=True)
     half = jax.ShapeDtypeStruct((along_y, *gradient_token_tiles.shape[1:]), BF16)
     *columns, kept, sent = call(
         outgoing_kernel,
@@ -238,8 +237,12 @@
     )
     other_columns = [shifted(columns[k - 1], "x", k) for k in distances]
     both = jnp.stack([kept, shifted(sent, "core", 1)], axis=1)
-    tokens = jnp.concatenate([both[0]] + [shifted(both[k], "y", k) for k in range(1, along_y)])
-    *other_columns, tokens = lax.optimization_barrier((*other_columns, tokens))
+    moved = [shifted(both[k], "y", k) for k in range(1, along_y)]
+    *moved, other_columns[0], other_columns[-1], hidden_token_tiles = lax.optimization_barrier(
+        (*moved, other_columns[0], other_columns[-1], hidden_token_tiles)
+    )
+    hidden = lax.all_to_all(hidden_token_tiles, DP, 0, 0, tiled=True)
+    tokens = jnp.concatenate([both[0]] + moved)
     other_tokens = [shifted(tokens, "x", k) for k in distances]
     fetch = [
         pltpu.with_memory_space_constraint(value, pltpu.HBM)

time: 163 us -> 150 us (0.920)
  waiting for transfers between devices: 62.1 us -> 46.2 us
  starting transfers between devices: 18.8 us -> 21.7 us
    ppermute x13, waiting for transfers between devices: 62.1 us -> 46.2 us  [shifted(): lax.ppermute(value, axis, [(i, (i + distance) % size) for i in range(size)])]
    ppermute x13, starting transfers between devices: 12.1 us -> 15.9 us  [shifted(): lax.ppermute(value, axis, [(i, (i + distance) % size) for i in range(size)])]
    all_to_all x1, blocking collectives: 20.6 us -> 18.3 us  [body(): lax.all_to_all(cut, 'z', 0, 0, tiled=True)]
    unnamed x16 -> x12, local copies, waits for them, and re-layouts: 2.23 us -> 3.81 us
  transfers between devices with their start and end apart: 14 -> 14, of which waited for: 9 -> 7; matrix products, arithmetic and copies ran while one was open for 0% -> 0% of each run, Pallas kernels for 0% -> 0%
where the time goes in v6:
time: 150 us
  blocking collectives  53.8 us (36%)
  waiting for transfers between devices  46.2 us (31%)
  starting transfers between devices  21.7 us (14%)
  Pallas kernels  19.5 us (13%)
  other arithmetic  4.25 us (3%)
  local copies, waits for them, and re-layouts  4 us (3%)
    ppermute x13, waiting for transfers between devices, shifted(): lax.ppermute(value, axis, [(i, (i + distance) % size) for i in range(size)])  46.2 us
    all_gather x1, blocking collectives, body(): lax.all_gather((update * 256.0).astype(jnp.float16), DP, axis=0, tiled=Fa...  22.2 us
    pallas_call x4, Pallas kernels, call(): pl.pallas_call(kernel, out_shape=out_shape, in_specs=[whole(pltpu.SMEM if...  19.5 us
    all_to_all x1, blocking collectives, body(): lax.all_to_all(cut, 'z', 0, 0, tiled=True)  18.3 us
    ppermute x13, starting transfers between devices, shifted(): lax.ppermute(value, axis, [(i, (i + distance) % size) for i in range(size)])  15.9 us
    all_to_all x1, blocking collectives, body(): own = lax.all_to_all(copies, 'z', 0, 0, tiled=True)  13.3 us
    all_to_all x1, starting transfers between devices, body(): hidden = lax.all_to_all(hidden_token_tiles, DP, 0, 0, tiled=True)  5.74 us
    mul x1, other arithmetic, body(): return (moment[None], gathered.astype(F32) * (1.0 / 256.0))  4.07 us
  transfers between devices with their start and end apart: 14, of which 7 were waited for; matrix products, arithmetic and copies ran while one was open for 0% of the time, Pallas kernels for 0%

profile of v6, /device:TPU:1, one launch (start us, length us, event | category | flops | bytes accessed | tf_op | source)
XLA Modules:
  0.0 150.1 jit_solution(7842736196913285124)
XLA Ops:
  0.7 1.2 copy-done.1
  1.8 1.0 copy-done.2
  2.9 0.3 outgoing.1
  3.2 3.3 %collective-permute-start = (bf16[4,224,128]{2,1,0:T(8,128)(2,1)S(1)}, bf16[4,224,128]{2,1,0:T(8,128)(2,1)S(1)}, u32[]{:S(2)}, u32[]{:S(2)}) collective-permute-start(bf16[4,224,128]{2,1,0:T(8,128)(2,1)S(1)} %get-tuple-element.16), channel_id=1, source_target_pairs={{0,32},{32,0},{1,33},{33,1},{2,34},{34,2},{3,35},{35,3},{4,36},{36... | collective-permute-start | bytes 688136 | tf_op jit(solution)/shard_map/ppermute | solution.py:217
  6.5 2.7 %collective-permute-start.5 = (bf16[224,768]{1,0:T(8,128)(2,1)S(1)}, bf16[224,768]{1,0:T(8,128)(2,1)S(1)}, u32[]{:S(2)}, u32[]{:S(2)}) collective-permute-start(bf16[224,768]{1,0:T(8,128)(2,1)S(1)} %get-tuple-element.18), channel_id=1, source_target_pairs={{0,24},{8,0},{16,8},{24,16},{1,25},{9,1},{17,9},{25,17},{2,26},{10... | collective-permute-start | bytes 1032200 | tf_op jit(solution)/shard_map/ppermute | solution.py:217
  9.2 0.1 collective-permute-start.1
  9.3 2.2 %collective-permute-start.2 = (bf16[2,224,128]{2,1,0:T(8,128)(2,1)S(1)}, bf16[2,224,128]{2,1,0:T(8,128)(2,1)S(1)}, u32[]{:S(2)}, u32[]{:S(2)}) collective-permute-start(bf16[2,224,128]{2,1,0:T(8,128)(2,1)S(1)} %get-tuple-element.30), channel_id=1, source_target_pairs={{0,128},{64,192},{128,0},{192,64},{1,129},{65,193},{129,1},{193,65... | collective-permute-start | bytes 344072 | tf_op jit(solution)/shard_map/ppermute | solution.py:217
  11.5 1.1 collective-permute-start.3
  12.5 2.7 %collective-permute-done.1 = bf16[2,224,128]{2,1,0:T(8,128)(2,1)S(1)} collective-permute-done((bf16[2,224,128]{2,1,0:T(8,128)(2,1)S(1)}, bf16[2,224,128]{2,1,0:T(8,128)(2,1)S(1)}, u32[]{:S(2)}, u32[]{:S(2)}) %collective-permute-start.1) | collective-permute-done | bytes 114720 | tf_op jit(solution)/shard_map/ppermute | solution.py:217
  15.3 1.2 collective-permute-done.2
  16.5 0.8 collective-permute-done.3
  17.3 0.7 copy-done.4
  18.1 0.1 copy-done.5
  18.2 5.7 %all-to-all-start = ((bf16[8,128,1024]{2,1,0:T(8,128)(2,1)}), bf16[8,128,1024]{2,1,0:T(8,128)(2,1)S(1)}, u32[]{:S(2)}, u32[]{:S(2)}) async-start(bf16[8,128,1024]{2,1,0:T(8,128)(2,1)} %param.4), calls=%async_computation | async-start | bytes 4194304 | tf_op jit(solution)/shard_map/all_to_all | solution.py:244
  24.0 1.3 collective-permute-start.9
  25.3 0.7 collective-permute-start.7
  26.0 3.1 %collective-permute-start.6 = (bf16[224,768]{1,0:T(8,128)(2,1)S(1)}, bf16[224,768]{1,0:T(8,128)(2,1)}, u32[]{:S(2)}, u32[]{:S(2)}) collective-permute-start(bf16[224,768]{1,0:T(8,128)(2,1)S(1)} %get-tuple-element.24), channel_id=1, source_target_pairs={{0,16},{8,24},{16,0},{24,8},{1,17},{9,25},{17,1},{25,9},{2,18},{10... | collective-permute-start | bytes 1032200 | tf_op jit(solution)/shard_map/ppermute | solution.py:217
  29.1 0.2 dynamic-slice_reduce_fusion.counts_ref
  29.3 26.6 %collective-permute-done.6.refs_2_ = bf16[224,768]{1,0:T(8,128)(2,1)} collective-permute-done((bf16[224,768]{1,0:T(8,128)(2,1)S(1)}, bf16[224,768]{1,0:T(8,128)(2,1)}, u32[]{:S(2)}, u32[]{:S(2)}) %collective-permute-start.6) | collective-permute-done | bytes 344096 | tf_op jit(solution)/shard_map/ppermute | solution.py:217
  55.9 0.7 copy-done.3
  56.7 5.7 %gram.1 = (f32[224,1024]{1,0:T(8,128)}, bf16[8,160,128]{2,1,0:T(8,128)(2,1)S(1)}) custom-call(s32[1]{0:T(128)} %bitcast.place_ref, s32[1]{0:T(128)} %bitcast.1.group_ref, s32[8]{0:T(128)S(1)} %dynamic-slice_reduce_fusion.counts_ref, bf16[8,128,1024]{2,1,0:T(8,128)(2,1)S(1)} %all-to-all-done.hidden_ref, bf16[8,224,128]{2,1,0:T(8,128)(2,1)S(1)} %pad_maximum_fusion.tokens_ref, ...), custom_call_target="tpu_custom_call" | custom-call | tf_op jit(solution)/shard_map/gram/pallas_call | solution.py:201
  62.4 18.3 %all_to_all.15.parts_ref = bf16[8,160,128]{2,1,0:T(8,128)(2,1)S(1)} all-to-all(bf16[8,160,128]{2,1,0:T(8,128)(2,1)S(1)} %get-tuple-element.27), channel_id=1, replica_groups=mesh['y'=4,'core'=2,'x'=4,'z'=8] {'z'}, dimensions={0} | all-to-all | bytes 655360 | tf_op jit(solution)/shard_map/all_to_all | solution.py:268
  80.7 0.1 sum.1
  80.8 13.3 %all_to_all.16.refs_0_ = bf16[8,160,128]{2,1,0:T(8,128)(2,1)S(1)} all-to-all(bf16[8,160,128]{2,1,0:T(8,128)(2,1)S(1)} %sum.1), channel_id=1, replica_groups=mesh['y'=4,'core'=2,'x'=4,'z'=8] {'z'}, dimensions={0} | all-to-all | bytes 655360 | tf_op jit(solution)/shard_map/all_to_all | solution.py:270
  94.1 0.3 collective-permute-start.11
  94.4 1.1 collective-permute-start.10
  95.5 4.5 %collective-permute-done.12.refs_3_ = bf16[8,160,128]{2,1,0:T(8,128)(2,1)S(1)} collective-permute-done((bf16[8,160,128]{2,1,0:T(8,128)(2,1)S(1)}, bf16[8,160,128]{2,1,0:T(8,128)(2,1)S(1)}, u32[]{:S(2)}, u32[]{:S(2)}) %collective-permute-start.12) | collective-permute-done | bytes 327712 | tf_op jit(solution)/shard_map/ppermute | solution.py:217
  100.0 1.6 %collective-permute-done.11.refs_2_ = bf16[8,160,128]{2,1,0:T(8,128)(2,1)S(1)} collective-permute-done((bf16[8,160,128]{2,1,0:T(8,128)(2,1)S(1)}, bf16[8,160,128]{2,1,0:T(8,128)(2,1)S(1)}, u32[]{:S(2)}, u32[]{:S(2)}) %collective-permute-start.11) | collective-permute-done | bytes 327712 | tf_op jit(solution)/shard_map/ppermute | solution.py:217
  101.6 8.7 %collective-permute-done.10.refs_1_ = bf16[8,160,128]{2,1,0:T(8,128)(2,1)S(1)} collective-permute-done((bf16[8,160,128]{2,1,0:T(8,128)(2,1)S(1)}, bf16[8,160,128]{2,1,0:T(8,128)(2,1)S(1)}, u32[]{:S(2)}, u32[]{:S(2)}) %collective-permute-start.10) | collective-permute-done | bytes 327712 | tf_op jit(solution)/shard_map/ppermute | solution.py:217
  110.3 13.4 %polynomial.1 = f32[224,1024]{1,0:T(8,128)S(1)} custom-call(s32[1]{0:T(128)} %bitcast.place_ref, f32[224,1024]{1,0:T(8,128)} %get-tuple-element.26.moment_away_ref, bf16[8,160,128]{2,1,0:T(8,128)(2,1)S(1)} %all_to_all.16.refs_0_, bf16[8,160,128]{2,1,0:T(8,128)(2,1)S(1)} %collective-permute-done.10.refs_1_, ...), custom_call_target="tpu_custom_call" | custom-call | tf_op jit(solution)/shard_map/polynomial/pallas_call | solution.py:201
  123.8 22.2 %all-gather.2 = f16[1792,1024]{1,0:T(8,128)(2,1)S(1)} all-gather(f16[224,1024]{1,0:T(8,128)(2,1)S(1)} %multiply_convert_fusion), channel_id=2, replica_groups=mesh['y'=4,'core'=2,'x'=4,'z'=8] {'y','core'}, dimensions={0}, use_global_device_ids=true | all-gather | bytes 4128768 | tf_op jit(solution)/shard_map/all_gather | solution.py:285
  146.0 4.1 %convert_multiply_fusion = f32[1792,1024]{1,0:T(8,128)} fusion(f16[1792,1024]{1,0:T(8,128)(2,1)S(1)} %all-gather.2), kind=kLoop, calls=%fused_computation | loop fusion | flops 3670016 | bytes 11010048 | tf_op jit(solution)/shard_map/mul | solution.py:286
  (20 shorter events, 0.3 us)
Async XLA Ops:
  0.6 28.5 %copy-start = (s32[8,8]{1,0:T(8,128)S(1)}, s32[8,8]{1,0:T(8,128)}, u32[]{:S(2)}) copy-start(s32[8,8]{1,0:T(8,128)} %param.7) | copy-start | bytes 772
  0.7 1.2 copy-start.1
  1.8 1.0 copy-start.2
  3.2 6.0 %collective-permute-start = (bf16[4,224,128]{2,1,0:T(8,128)(2,1)S(1)}, bf16[4,224,128]{2,1,0:T(8,128)(2,1)S(1)}, u32[]{:S(2)}, u32[]{:S(2)}) collective-permute-start(bf16[4,224,128]{2,1,0:T(8,128)(2,1)S(1)} %get-tuple-element.16), channel_id=1, source_target_pairs={{0,32},{32,0},{1,33},{33,1},{2,34},{34,2},{3,35},{35,3},{4,36},{36... | collective-permute-start | bytes 688136 | tf_op jit(solution)/shard_map/ppermute | solution.py:217
  6.5 10.8 %collective-permute-start.4 = (bf16[224,768]{1,0:T(8,128)(2,1)S(1)}, bf16[224,768]{1,0:T(8,128)(2,1)S(1)}, u32[]{:S(2)}, u32[]{:S(2)}) collective-permute-start(bf16[224,768]{1,0:T(8,128)(2,1)S(1)} %get-tuple-element.17), channel_id=1, source_target_pairs={{0,8},{8,16},{16,24},{24,0},{1,9},{9,17},{17,25},{25,1},{2,10},{10... | collective-permute-start | bytes 1032200 | tf_op jit(solution)/shard_map/ppermute | solution.py:217
  6.5 10.8 %collective-permute-start.5 = (bf16[224,768]{1,0:T(8,128)(2,1)S(1)}, bf16[224,768]{1,0:T(8,128)(2,1)S(1)}, u32[]{:S(2)}, u32[]{:S(2)}) collective-permute-start(bf16[224,768]{1,0:T(8,128)(2,1)S(1)} %get-tuple-element.18), channel_id=1, source_target_pairs={{0,24},{8,0},{16,8},{24,16},{1,25},{9,1},{17,9},{25,17},{2,26},{10... | collective-permute-start | bytes 1032200 | tf_op jit(solution)/shard_map/ppermute | solution.py:217
  9.2 6.1 %collective-permute-start.1 = (bf16[2,224,128]{2,1,0:T(8,128)(2,1)S(1)}, bf16[2,224,128]{2,1,0:T(8,128)(2,1)S(1)}, u32[]{:S(2)}, u32[]{:S(2)}) collective-permute-start(bf16[2,224,128]{2,1,0:T(8,128)(2,1)S(1)} %get-tuple-element.29), channel_id=1, source_target_pairs={{0,64},{64,128},{128,192},{192,0},{1,65},{65,129},{129,193},{193,1... | collective-permute-start | bytes 344072 | tf_op jit(solution)/shard_map/ppermute | solution.py:217
  9.3 7.2 %collective-permute-start.2 = (bf16[2,224,128]{2,1,0:T(8,128)(2,1)S(1)}, bf16[2,224,128]{2,1,0:T(8,128)(2,1)S(1)}, u32[]{:S(2)}, u32[]{:S(2)}) collective-permute-start(bf16[2,224,128]{2,1,0:T(8,128)(2,1)S(1)} %get-tuple-element.30), channel_id=1, source_target_pairs={{0,128},{64,192},{128,0},{192,64},{1,129},{65,193},{129,1},{193,65... | collective-permute-start | bytes 344072 | tf_op jit(solution)/shard_map/ppermute | solution.py:217
  11.5 5.8 %collective-permute-start.3 = (bf16[2,224,128]{2,1,0:T(8,128)(2,1)S(1)}, bf16[2,224,128]{2,1,0:T(8,128)(2,1)S(1)}, u32[]{:S(2)}, u32[]{:S(2)}) collective-permute-start(bf16[2,224,128]{2,1,0:T(8,128)(2,1)S(1)} %get-tuple-element.31), channel_id=1, source_target_pairs={{0,192},{64,0},{128,64},{192,128},{1,193},{65,1},{129,65},{193,129... | collective-permute-start | bytes 344072 | tf_op jit(solution)/shard_map/ppermute | solution.py:217
  17.3 0.7 copy-start.4
  17.3 0.9 copy-start.5
  18.2 37.7 %all-to-all-start = ((bf16[8,128,1024]{2,1,0:T(8,128)(2,1)}), bf16[8,128,1024]{2,1,0:T(8,128)(2,1)S(1)}, u32[]{:S(2)}, u32[]{:S(2)}) async-start(bf16[8,128,1024]{2,1,0:T(8,128)(2,1)} %param.4), calls=%async_computation | async-start | bytes 4194304 | tf_op jit(solution)/shard_map/all_to_all | solution.py:244
  24.0 31.9 %collective-permute-start.9 = (bf16[8,224,128]{2,1,0:T(8,128)(2,1)S(1)}, bf16[8,224,128]{2,1,0:T(8,128)(2,1)S(1)}, u32[]{:S(2)}, u32[]{:S(2)}) collective-permute-start(bf16[8,224,128]{2,1,0:T(8,128)(2,1)S(1)} %pad_maximum_fusion.tokens_ref), channel_id=1, source_target_pairs={{0,24},{8,0},{16,8},{24,16},{1,25},{9,1},{17,9},{25,17},{2,26},{10... | collective-permute-start | bytes 1376264 | tf_op jit(solution)/shard_map/ppermute | solution.py:217
  25.3 30.6 %collective-permute-start.8 = (bf16[8,224,128]{2,1,0:T(8,128)(2,1)S(1)}, bf16[8,224,128]{2,1,0:T(8,128)(2,1)}, u32[]{:S(2)}, u32[]{:S(2)}) collective-permute-start(bf16[8,224,128]{2,1,0:T(8,128)(2,1)S(1)} %pad_maximum_fusion.tokens_ref), channel_id=1, source_target_pairs={{0,16},{8,24},{16,0},{24,8},{1,17},{9,25},{17,1},{25,9},{2,18},{10... | collective-permute-start | bytes 1376264 | tf_op jit(solution)/shard_map/ppermute | solution.py:217
  25.3 30.6 %collective-permute-start.7 = (bf16[8,224,128]{2,1,0:T(8,128)(2,1)S(1)}, bf16[8,224,128]{2,1,0:T(8,128)(2,1)}, u32[]{:S(2)}, u32[]{:S(2)}) collective-permute-start(bf16[8,224,128]{2,1,0:T(8,128)(2,1)S(1)} %pad_maximum_fusion.tokens_ref), channel_id=1, source_target_pairs={{0,8},{8,16},{16,24},{24,0},{1,9},{9,17},{17,25},{25,1},{2,10},{10... | collective-permute-start | bytes 1376264 | tf_op jit(solution)/shard_map/ppermute | solution.py:217
  26.0 29.9 %collective-permute-start.6 = (bf16[224,768]{1,0:T(8,128)(2,1)S(1)}, bf16[224,768]{1,0:T(8,128)(2,1)}, u32[]{:S(2)}, u32[]{:S(2)}) collective-permute-start(bf16[224,768]{1,0:T(8,128)(2,1)S(1)} %get-tuple-element.24), channel_id=1, source_target_pairs={{0,16},{8,24},{16,0},{24,8},{1,17},{9,25},{17,1},{25,9},{2,18},{10... | collective-permute-start | bytes 1032200 | tf_op jit(solution)/shard_map/ppermute | solution.py:217
  55.9 0.8 copy-start.3
  94.1 5.9 %collective-permute-start.12 = (bf16[8,160,128]{2,1,0:T(8,128)(2,1)S(1)}, bf16[8,160,128]{2,1,0:T(8,128)(2,1)S(1)}, u32[]{:S(2)}, u32[]{:S(2)}) collective-permute-start(bf16[8,160,128]{2,1,0:T(8,128)(2,1)S(1)} %all_to_all.16.refs_0_), channel_id=1, source_target_pairs={{0,24},{8,0},{16,8},{24,16},{1,25},{9,1},{17,9},{25,17},{2,26},{10... | collective-permute-start | bytes 983048 | tf_op jit(solution)/shard_map/ppermute | solution.py:217
  94.1 7.5 %collective-permute-start.11 = (bf16[8,160,128]{2,1,0:T(8,128)(2,1)S(1)}, bf16[8,160,128]{2,1,0:T(8,128)(2,1)S(1)}, u32[]{:S(2)}, u32[]{:S(2)}) collective-permute-start(bf16[8,160,128]{2,1,0:T(8,128)(2,1)S(1)} %all_to_all.16.refs_0_), channel_id=1, source_target_pairs={{0,16},{8,24},{16,0},{24,8},{1,17},{9,25},{17,1},{25,9},{2,18},{10... | collective-permute-start | bytes 983048 | tf_op jit(solution)/shard_map/ppermute | solution.py:217
  94.4 16.0 %collective-permute-start.10 = (bf16[8,160,128]{2,1,0:T(8,128)(2,1)S(1)}, bf16[8,160,128]{2,1,0:T(8,128)(2,1)S(1)}, u32[]{:S(2)}, u32[]{:S(2)}) collective-permute-start(bf16[8,160,128]{2,1,0:T(8,128)(2,1)S(1)} %all_to_all.16.refs_0_), channel_id=1, source_target_pairs={{0,8},{8,16},{16,24},{24,0},{1,9},{9,17},{17,25},{25,1},{2,10},{10... | collective-permute-start | bytes 983048 | tf_op jit(solution)/shard_map/ppermute | solution.py:217

commit v7 on v6

--- a/solution.py
+++ b/solution.py
@@ -23,7 +23,7 @@
 COEF_C = 2.0315
 
 DP = ("y", "core")
-EXPERT = ("x", "z")
+EXPERT = ("x", "z_pair", "z_low")
 
 BF16 = jnp.bfloat16
 F32 = jnp.float32
@@ -52,18 +52,23 @@
     return pl.ds(pl.multiple_of(lax.rem(2 * place + block, FF // BLOCK) * BLOCK, BLOCK), BLOCK)
 
 
-def outgoing_kernel(place_ref, group_ref, momentum_ref, tokens_ref, *refs):
-    *column_refs, kept_ref, sent_ref = refs
+def outgoing_kernel(place_ref, group_ref, momentum_away_ref, tokens_ref, *refs):
+    *column_refs, kept_ref, sent_ref, momentum_ref, semaphores = refs
     chip, core = lax.div(group_ref[0], CORES), lax.rem(group_ref[0], CORES)
     chips = kept_ref.shape[0]
+    sources, targets = [momentum_away_ref], [momentum_ref]
+    for distance in range(chips):
+        first = lax.rem(chip + distance, chips) * CORES
+        sources += [tokens_ref.at[first + core], tokens_ref.at[first + 1 - core]]
+        targets += [kept_ref.at[distance], sent_ref.at[distance]]
+    copies = fetched(sources, targets, semaphores)
+    copies[0].wait()
     for distance, column_ref in enumerate(column_refs, 1):
         for block in range(NEEDED):
             value = momentum_ref[:, column(place_ref[0] + distance, block)]
             column_ref[:, block * BLOCK : (block + 1) * BLOCK] = value.astype(BF16)
-    for distance in range(chips):
-        first = lax.rem(chip + distance, chips) * CORES
-        kept_ref[distance] = tokens_ref[first + core]
-        sent_ref[distance] = tokens_ref[first + 1 - core]
+    for copy in copies[1:]:
+        copy.wait()
 
 
 def fetched(sources, targets, semaphores):
@@ -127,27 +132,28 @@
 
     blocks = [block_of(i, j) for i, j in block_pairs(0)[:-1]]
     blocks.append(jnp.where(place < 2, block_of(*block_pairs(0)[-1]), block_of(*block_pairs(2)[-1])))
-    per_device = cut_ref.shape[1] // UNIT - 1
-    for unit in range(cut_ref.shape[0] * per_device):
-        device, at = divmod(unit, per_device)
+    pairs = cut_ref.shape[0]
+    per_pair = cut_ref.shape[1] // UNIT - 1
+    for unit in range(pairs * per_pair):
+        pair, at = divmod(unit, per_pair)
         block, row = divmod(unit * UNIT, BLOCK)
-        cut_ref[device, at * UNIT : (at + 1) * UNIT] = blocks[block][row : row + UNIT]
+        cut_ref[lax.rem(pair - place_ref[1] + pairs, pairs), at * UNIT : (at + 1) * UNIT] = blocks[block][
+            row : row + UNIT
+        ]
     total = jnp.sum(jnp.sum(moment * moment, axis=0, keepdims=True), axis=1, keepdims=True)
-    for device in range(cut_ref.shape[0]):
-        cut_ref[device, per_device * UNIT :] = pieces_of(total, (UNIT, BLOCK))
-
-
-def sum_kernel(parts_ref, copies_ref):
-    total = parts_ref[0].astype(F32)
-    for source in range(1, parts_ref.shape[0]):
-        total = total + parts_ref[source].astype(F32)
+    for pair in range(pairs):
+        cut_ref[pair, per_pair * UNIT :] = pieces_of(total, (UNIT, BLOCK))
+
+
+def sum_kernel(*refs):
+    *part_refs, sum_ref = refs
+    total = part_refs[0][...].astype(F32)
+    for part_ref in part_refs[1:]:
+        total = total + part_ref[...].astype(F32)
     rows = total.shape[0] - UNIT
+    sum_ref[:rows] = total[:rows].astype(BF16)
     squares = jnp.sum(total[rows:, 0:1], axis=0, keepdims=True)
-    piece = total[:rows].astype(BF16)
-    tile = pieces_of(squares, (UNIT, BLOCK))
-    for target in range(copies_ref.shape[0]):
-        copies_ref[target, :rows] = piece
-        copies_ref[target, rows:] = tile
+    sum_ref[rows:] = pieces_of(squares, (UNIT, BLOCK))
 
 
 def polynomial_kernel(place_ref, moment_away_ref, *refs):
@@ -160,7 +166,8 @@
     for distance, chunk_ref in enumerate(chunk_refs):
         source = lax.rem(place_ref[0] - distance + chunks, chunks)
         for piece in range(pieces):
-            packed_ref[source, piece * rows : (piece + 1) * rows] = chunk_ref[piece, :rows]
+            start = lax.rem(place_ref[1] - piece + pieces, pieces) * rows
+            packed_ref[source, pl.ds(pl.multiple_of(start, UNIT), rows)] = chunk_ref[piece, :rows]
         squares = squares + jnp.sum(chunk_ref[0, rows:].astype(F32)[:, 0:1], axis=0, keepdims=True)
     factor = 1.0 / (jnp.sqrt(squares) + EPSILON)
     for source in range(chunks):
@@ -218,13 +225,13 @@
 
 
 def body(hidden_token_tiles, gradient_token_tiles, momentum, filled_tile_count):
-    along_x, along_z = lax.axis_size("x"), lax.axis_size("z")
+    along_x, pairs = lax.axis_size("x"), lax.axis_size("z_pair")
     rows = momentum.shape[1]
-    piece = len(block_pairs(0)) * BLOCK // along_z
+    piece = len(block_pairs(0)) * BLOCK // pairs
     group = lax.axis_index(DP).astype(jnp.int32)
     counts = lax.dynamic_index_in_dim(filled_tile_count, group, 1, keepdims=False)
     group = group.reshape(1)
-    place = lax.axis_index("x").astype(jnp.int32).reshape(1)
+    place = jnp.stack([lax.axis_index("x"), lax.axis_index("z_pair")]).astype(jnp.int32)
     distances = range(1, along_x)
     along_y = lax.axis_size("y")
 
@@ -232,7 +239,10 @@
     *columns, kept, sent = call(
         outgoing_kernel,
         [jax.ShapeDtypeStruct((rows, NEEDED * BLOCK), BF16) for _ in distances] + [half, half],
-        [place, group, momentum[0], gradient_token_tiles],
+        [place, group]
+        + [pltpu.with_memory_space_constraint(value, pltpu.HBM) for value in (momentum[0], gradient_token_tiles)],
+        scratch=[pltpu.VMEM((rows, FF), F32), pltpu.SemaphoreType.DMA((1 + CORES * along_y,))],
+        away=(2, 3),
         scalars=2,
     )
     other_columns = [shifted(columns[k - 1], "x", k) for k in distances]
@@ -248,11 +258,11 @@
         pltpu.with_memory_space_constraint(value, pltpu.HBM)
         for value in [momentum[0]] + other_columns + other_tokens
     ]
-    moment, cut = call(
+    moment, parts = call(
         gram_kernel,
         (
             jax.ShapeDtypeStruct((rows, FF), F32),
-            jax.ShapeDtypeStruct((along_z, piece + UNIT, BLOCK), BF16),
+            jax.ShapeDtypeStruct((pairs, piece + UNIT, BLOCK), BF16),
         ),
         [place, group, counts, hidden, tokens] + fetch,
         scratch=[pltpu.VMEM((hidden.shape[0] * hidden.shape[1], NEEDED * BLOCK), BF16)]
@@ -262,18 +272,16 @@
         scalars=3,
         mib=28,
     )
-    copies = call(
-        sum_kernel,
-        jax.ShapeDtypeStruct((along_z, piece + UNIT, BLOCK), BF16),
-        [lax.all_to_all(cut, "z", 0, 0, tiled=True)],
-    )
-    own = lax.all_to_all(copies, "z", 0, 0, tiled=True)
+    summed = jax.ShapeDtypeStruct((piece + UNIT, BLOCK), BF16)
+    part = call(sum_kernel, summed, [parts[0]] + [shifted(parts[k], "z_pair", k) for k in range(1, pairs)])
+    part = call(sum_kernel, summed, [part, shifted(part, "z_low", 1)])
+    own = jnp.stack([part] + [shifted(part, "z_pair", k) for k in range(1, pairs)])
     update = call(
         polynomial_kernel,
         jax.ShapeDtypeStruct((rows, FF), F32),
         [place, pltpu.with_memory_space_constraint(moment, pltpu.HBM), own] + [shifted(own, "x", k) for k in distances],
         scratch=[
-            pltpu.VMEM((along_x, along_z * piece, BLOCK), BF16),
+            pltpu.VMEM((along_x, pairs * piece, BLOCK), BF16),
             pltpu.VMEM((FF, FF), BF16),
             pltpu.VMEM((rows, FF), F32),
             pltpu.SemaphoreType.DMA((1,)),
@@ -287,7 +295,7 @@
 
 
 def solution(mesh):
-    split = Mesh(mesh.devices.reshape(4, 2, 4, 8), ("y", "core", "x", "z"))
+    split = Mesh(mesh.devices.reshape(4, 2, 4, 4, 2), ("y", "core", "x", "z_pair", "z_low"))
     placed = (P(None, DP, None), P(None, EXPERT, DP), P(DP, EXPERT, None), P())
     return jax.shard_map(
         body,

time: 150 us -> 147 us (0.980)
  blocking collectives: 53.8 us -> 22.7 us
  starting transfers between devices: 21.7 us -> 37.6 us
  waiting for transfers between devices: 46.2 us -> 57.2 us
  Pallas kernels: 19.5 us -> 22.5 us
  local copies, waits for them, and re-layouts: 4 us -> 1.82 us
    all_to_all x2 -> x0, blocking collectives: 31.6 us -> none  [the longest x1 18.3 us: body(): lax.all_to_all(cut, 'z', 0, 0, tiled=True)]
    ppermute x13 -> x20, starting transfers between devices: 15.9 us -> 31.9 us  [shifted(): lax.ppermute(value, axis, [(i, (i + distance) % size) for i in range(size)])]
    ppermute x13 -> x20, waiting for transfers between devices: 46.2 us -> 57.2 us  [shifted(): lax.ppermute(value, axis, [(i, (i + distance) % size) for i in range(size)])]
    pallas_call x4 -> x5, Pallas kernels: 19.5 us -> 22.5 us  [call(): pl.pallas_call(kernel, out_shape=out_shape, in_specs=[whole(pltpu.SMEM if...]
    unnamed x12 -> x8, local copies, waits for them, and re-layouts: 3.81 us -> 1.61 us
  transfers between devices with their start and end apart: 14 -> 21, of which waited for: 7 -> 12; matrix products, arithmetic and copies ran while one was open for 0% -> 0% of each run, Pallas kernels for 0% -> 0%
where the time goes in v7:
time: 147 us
  waiting for transfers between devices  57.2 us (39%)
  starting transfers between devices  37.6 us (26%)
  blocking collectives  22.7 us (15%)
  Pallas kernels  22.5 us (15%)
  other arithmetic  4.37 us (3%)
  local copies, waits for them, and re-layouts  1.82 us (1%)
    ppermute x20, waiting for transfers between devices, shifted(): lax.ppermute(value, axis, [(i, (i + distance) % size) for i in range(size)])  57.2 us
    ppermute x20, starting transfers between devices, shifted(): lax.ppermute(value, axis, [(i, (i + distance) % size) for i in range(size)])  31.9 us
    all_gather x1, blocking collectives, body(): lax.all_gather((update * 256.0).astype(jnp.float16), DP, axis=0, tiled=Fa...  22.7 us
    pallas_call x5, Pallas kernels, call(): pl.pallas_call(kernel, out_shape=out_shape, in_specs=[whole(pltpu.SMEM if...  22.5 us
    all_to_all x1, starting transfers between devices, body(): hidden = lax.all_to_all(hidden_token_tiles, DP, 0, 0, tiled=True)  5.74 us
    mul x1, other arithmetic, body(): return (moment[None], gathered.astype(F32) * (1.0 / 256.0))  4.07 us
  transfers between devices with their start and end apart: 21, of which 12 were waited for; matrix products, arithmetic and copies ran while one was open for 0% of the time, Pallas kernels for 0%

profile of v7, /device:TPU:1, one launch (start us, length us, event | category | flops | bytes accessed | tf_op | source)
XLA Modules:
  0.0 147.0 jit_solution(9429818470938841727)
XLA Ops:
  0.7 2.1 %outgoing.1 = (bf16[224,768]{1,0:T(8,128)(2,1)S(1)}, bf16[224,768]{1,0:T(8,128)(2,1)S(1)}, bf16[224,768]{1,0:T(8,128)(2,1)S(1)}, bf16[4,224,128]{2,1,0:T(8,128)(2,1)S(1)}, bf16[4,224,128]{2,1,0:T(8,128)(2,1)S(1)}) custom-call(s32[2]{0:T(128)S(1)} %pad_add_fusion.place_ref, s32[1]{0:T(128)} %bitcast.2.group_ref, f32[224,1024]{1,0:T(8,128)} %bitcast.31, ...), custom_call_target="tpu_custom_call" | custom-call | tf_op jit(solution)/shard_map/outgoing/pallas_call | solution.py:208
  2.8 3.3 %collective-permute-start = (bf16[4,224,128]{2,1,0:T(8,128)(2,1)S(1)}, bf16[4,224,128]{2,1,0:T(8,128)(2,1)S(1)}, u32[]{:S(2)}, u32[]{:S(2)}) collective-permute-start(bf16[4,224,128]{2,1,0:T(8,128)(2,1)S(1)} %get-tuple-element.16), channel_id=1, source_target_pairs={{0,32},{32,0},{1,33},{33,1},{2,34},{34,2},{3,35},{35,3},{4,36},{36... | collective-permute-start | bytes 688136 | tf_op jit(solution)/shard_map/ppermute | solution.py:224
  6.1 2.7 %collective-permute-start.5 = (bf16[224,768]{1,0:T(8,128)(2,1)S(1)}, bf16[224,768]{1,0:T(8,128)(2,1)S(1)}, u32[]{:S(2)}, u32[]{:S(2)}) collective-permute-start(bf16[224,768]{1,0:T(8,128)(2,1)S(1)} %get-tuple-element.18), channel_id=1, source_target_pairs={{0,24},{8,0},{16,8},{24,16},{1,25},{9,1},{17,9},{25,17},{2,26},{10... | collective-permute-start | bytes 1032200 | tf_op jit(solution)/shard_map/ppermute | solution.py:224
  9.0 2.2 %collective-permute-start.2 = (bf16[2,224,128]{2,1,0:T(8,128)(2,1)S(1)}, bf16[2,224,128]{2,1,0:T(8,128)(2,1)S(1)}, u32[]{:S(2)}, u32[]{:S(2)}) collective-permute-start(bf16[2,224,128]{2,1,0:T(8,128)(2,1)S(1)} %get-tuple-element.30), channel_id=1, source_target_pairs={{0,128},{64,192},{128,0},{192,64},{1,129},{65,193},{129,1},{193,65... | collective-permute-start | bytes 344072 | tf_op jit(solution)/shard_map/ppermute | solution.py:224
  11.1 1.1 collective-permute-start.3
  12.2 2.7 %collective-permute-done.1 = bf16[2,224,128]{2,1,0:T(8,128)(2,1)S(1)} collective-permute-done((bf16[2,224,128]{2,1,0:T(8,128)(2,1)S(1)}, bf16[2,224,128]{2,1,0:T(8,128)(2,1)S(1)}, u32[]{:S(2)}, u32[]{:S(2)}) %collective-permute-start.1) | collective-permute-done | bytes 114720 | tf_op jit(solution)/shard_map/ppermute | solution.py:224
  15.0 1.2 collective-permute-done.2
  16.2 0.8 collective-permute-done.3
  17.8 5.7 %all-to-all-start = ((bf16[8,128,1024]{2,1,0:T(8,128)(2,1)}), bf16[8,128,1024]{2,1,0:T(8,128)(2,1)S(1)}, u32[]{:S(2)}, u32[]{:S(2)}) async-start(bf16[8,128,1024]{2,1,0:T(8,128)(2,1)} %param.4), calls=%async_computation | async-start | bytes 4194304 | tf_op jit(solution)/shard_map/all_to_all | solution.py:254
  23.6 1.3 collective-permute-start.9
  25.6 3.1 %collective-permute-start.6 = (bf16[224,768]{1,0:T(8,128)(2,1)S(1)}, bf16[224,768]{1,0:T(8,128)(2,1)}, u32[]{:S(2)}, u32[]{:S(2)}) collective-permute-start(bf16[224,768]{1,0:T(8,128)(2,1)S(1)} %get-tuple-element.24), channel_id=1, source_target_pairs={{0,16},{8,24},{16,0},{24,8},{1,17},{9,25},{17,1},{25,9},{2,18},{10... | collective-permute-start | bytes 1032200 | tf_op jit(solution)/shard_map/ppermute | solution.py:224
  29.0 26.6 %collective-permute-done.6.refs_2_ = bf16[224,768]{1,0:T(8,128)(2,1)} collective-permute-done((bf16[224,768]{1,0:T(8,128)(2,1)S(1)}, bf16[224,768]{1,0:T(8,128)(2,1)}, u32[]{:S(2)}, u32[]{:S(2)}) %collective-permute-start.6) | collective-permute-done | bytes 344096 | tf_op jit(solution)/shard_map/ppermute | solution.py:224
  55.6 0.7 copy-done.1
  56.3 6.4 %gram.1 = (f32[224,1024]{1,0:T(8,128)}, bf16[4,304,128]{2,1,0:T(8,128)(2,1)S(1)}) custom-call(s32[2]{0:T(128)S(1)} %pad_add_fusion.place_ref, s32[1]{0:T(128)} %bitcast.2.group_ref, s32[8]{0:T(128)S(1)} %dynamic-slice_reduce_fusion.counts_ref, bf16[8,128,1024]{2,1,0:T(8,128)(2,1)S(1)} %all-to-all-done.hidden_ref, ...), custom_call_target="tpu_custom_call" | custom-call | tf_op jit(solution)/shard_map/gram/pallas_call | solution.py:208
  62.7 5.4 %collective-permute-start.12 = (bf16[304,128]{1,0:T(8,128)(2,1)S(1)}, bf16[304,128]{1,0:T(8,128)(2,1)S(1)}, u32[]{:S(2)}, u32[]{:S(2)}) collective-permute-start(bf16[304,128]{1,0:T(8,128)(2,1)S(1)} %get-tuple-element.32), channel_id=1, source_target_pairs={{0,6},{2,0},{4,2},{6,4},{1,7},{3,1},{5,3},{7,5},{8,14},{10,8},{12,... | collective-permute-start | bytes 233480 | tf_op jit(solution)/shard_map/ppermute | solution.py:224
  68.1 1.2 collective-permute-start.11
  69.3 2.1 %collective-permute-start.10 = (bf16[304,128]{1,0:T(8,128)(2,1)S(1)}, bf16[304,128]{1,0:T(8,128)(2,1)S(1)}, u32[]{:S(2)}, u32[]{:S(2)}) collective-permute-start(bf16[304,128]{1,0:T(8,128)(2,1)S(1)} %get-tuple-element.34), channel_id=1, source_target_pairs={{0,2},{2,4},{4,6},{6,0},{1,3},{3,5},{5,7},{7,1},{8,10},{10,12},{12... | collective-permute-start | bytes 233480 | tf_op jit(solution)/shard_map/ppermute | solution.py:224
  71.4 4.1 %collective-permute-done.11.refs_2_ = bf16[304,128]{1,0:T(8,128)(2,1)S(1)} collective-permute-done((bf16[304,128]{1,0:T(8,128)(2,1)S(1)}, bf16[304,128]{1,0:T(8,128)(2,1)S(1)}, u32[]{:S(2)}, u32[]{:S(2)}) %collective-permute-start.11) | collective-permute-done | bytes 77856 | tf_op jit(solution)/shard_map/ppermute | solution.py:224
  75.5 1.1 collective-permute-done.10.refs_1_
  76.8 3.2 %collective-permute-done.13.refs_1_ = bf16[304,128]{1,0:T(8,128)(2,1)S(1)} collective-permute-done((bf16[304,128]{1,0:T(8,128)(2,1)S(1)}, bf16[304,128]{1,0:T(8,128)(2,1)S(1)}, u32[]{:S(2)}, u32[]{:S(2)}) %collective-permute-start.13) | collective-permute-done | bytes 77856 | tf_op jit(solution)/shard_map/ppermute | solution.py:224
  80.1 2.8 %collective-permute-start.16 = (bf16[304,128]{1,0:T(8,128)(2,1)S(1)}, bf16[304,128]{1,0:T(8,128)(2,1)S(1)}, u32[]{:S(2)}, u32[]{:S(2)}) collective-permute-start(bf16[304,128]{1,0:T(8,128)(2,1)S(1)} %sum.3), channel_id=1, source_target_pairs={{0,6},{2,0},{4,2},{6,4},{1,7},{3,1},{5,3},{7,5},{8,14},{10,8},{12,... | collective-permute-start | bytes 233480 | tf_op jit(solution)/shard_map/ppermute | solution.py:224
  82.9 2.2 %collective-permute-start.15 = (bf16[304,128]{1,0:T(8,128)(2,1)S(1)}, bf16[304,128]{1,0:T(8,128)(2,1)S(1)}, u32[]{:S(2)}, u32[]{:S(2)}) collective-permute-start(bf16[304,128]{1,0:T(8,128)(2,1)S(1)} %sum.3), channel_id=1, source_target_pairs={{0,4},{2,6},{4,0},{6,2},{1,5},{3,7},{5,1},{7,3},{8,12},{10,14},{12... | collective-permute-start | bytes 233480 | tf_op jit(solution)/shard_map/ppermute | solution.py:224
  85.1 2.2 %collective-permute-start.14 = (bf16[304,128]{1,0:T(8,128)(2,1)S(1)}, bf16[304,128]{1,0:T(8,128)(2,1)S(1)}, u32[]{:S(2)}, u32[]{:S(2)}) collective-permute-start(bf16[304,128]{1,0:T(8,128)(2,1)S(1)} %sum.3), channel_id=1, source_target_pairs={{0,2},{2,4},{4,6},{6,0},{1,3},{3,5},{5,7},{7,1},{8,10},{10,12},{12... | collective-permute-start | bytes 233480 | tf_op jit(solution)/shard_map/ppermute | solution.py:224
  87.3 3.0 %collective-permute-done.15 = bf16[304,128]{1,0:T(8,128)(2,1)S(1)} collective-permute-done((bf16[304,128]{1,0:T(8,128)(2,1)S(1)}, bf16[304,128]{1,0:T(8,128)(2,1)S(1)}, u32[]{:S(2)}, u32[]{:S(2)}) %collective-permute-start.15) | collective-permute-done | bytes 77856 | tf_op jit(solution)/shard_map/ppermute | solution.py:224
  90.3 0.8 collective-permute-done.14
  91.6 1.0 collective-permute-start.17
  92.7 4.3 %collective-permute-done.19.refs_3_ = bf16[4,304,128]{2,1,0:T(8,128)(2,1)S(1)} collective-permute-done((bf16[4,304,128]{2,1,0:T(8,128)(2,1)S(1)}, bf16[4,304,128]{2,1,0:T(8,128)(2,1)S(1)}, u32[]{:S(2)}, u32[]{:S(2)}) %collective-permute-start.19) | collective-permute-done | bytes 311328 | tf_op jit(solution)/shard_map/ppermute | solution.py:224
  96.9 1.7 %collective-permute-done.18.refs_2_ = bf16[4,304,128]{2,1,0:T(8,128)(2,1)S(1)} collective-permute-done((bf16[4,304,128]{2,1,0:T(8,128)(2,1)S(1)}, bf16[4,304,128]{2,1,0:T(8,128)(2,1)S(1)}, u32[]{:S(2)}, u32[]{:S(2)}) %collective-permute-start.18) | collective-permute-done | bytes 311328 | tf_op jit(solution)/shard_map/ppermute | solution.py:224
  98.6 7.6 %collective-permute-done.17.refs_1_ = bf16[4,304,128]{2,1,0:T(8,128)(2,1)S(1)} collective-permute-done((bf16[4,304,128]{2,1,0:T(8,128)(2,1)S(1)}, bf16[4,304,128]{2,1,0:T(8,128)(2,1)S(1)}, u32[]{:S(2)}, u32[]{:S(2)}) %collective-permute-start.17) | collective-permute-done | bytes 311328 | tf_op jit(solution)/shard_map/ppermute | solution.py:224
  106.2 13.9 %polynomial.1 = f32[224,1024]{1,0:T(8,128)S(1)} custom-call(s32[2]{0:T(128)S(1)} %pad_add_fusion.place_ref, f32[224,1024]{1,0:T(8,128)} %get-tuple-element.26.moment_away_ref, bf16[4,304,128]{2,1,0:T(8,128)(2,1)S(1)} %pad_maximum_fusion.1.refs_0_, bf16[4,304,128]{2,1,0:T(8,128)(2,1)S(1)} %collective-permute-done.17.refs_1_, ...), custom_call_target="tpu_custom_call" | custom-call | tf_op jit(solution)/shard_map/polynomial/pallas_call | solution.py:208
  120.2 22.7 %all-gather.2 = f16[1792,1024]{1,0:T(8,128)(2,1)S(1)} all-gather(f16[224,1024]{1,0:T(8,128)(2,1)S(1)} %multiply_convert_fusion), channel_id=2, replica_groups=mesh['y'=4,'core'=2,'x'=4,'z_pair'=4,'z_low'=2] {'y','core'}, dimensions={0}, use_global_device_ids=true | all-gather | bytes 4128768 | tf_op jit(solution)/shard_map/all_gather | solution.py:293
  142.9 4.1 %convert_multiply_fusion = f32[1792,1024]{1,0:T(8,128)} fusion(f16[1792,1024]{1,0:T(8,128)(2,1)S(1)} %all-gather.2), kind=kLoop, calls=%fused_computation | loop fusion | flops 3670016 | bytes 11010048 | tf_op jit(solution)/shard_map/mul | solution.py:294
  (32 shorter events, 2.9 us)
Async XLA Ops:
  0.6 28.1 %copy-start = (s32[8,8]{1,0:T(8,128)S(1)}, s32[8,8]{1,0:T(8,128)}, u32[]{:S(2)}) copy-start(s32[8,8]{1,0:T(8,128)} %param.7) | copy-start | bytes 772
  2.8 6.0 %collective-permute-start = (bf16[4,224,128]{2,1,0:T(8,128)(2,1)S(1)}, bf16[4,224,128]{2,1,0:T(8,128)(2,1)S(1)}, u32[]{:S(2)}, u32[]{:S(2)}) collective-permute-start(bf16[4,224,128]{2,1,0:T(8,128)(2,1)S(1)} %get-tuple-element.16), channel_id=1, source_target_pairs={{0,32},{32,0},{1,33},{33,1},{2,34},{34,2},{3,35},{35,3},{4,36},{36... | collective-permute-start | bytes 688136 | tf_op jit(solution)/shard_map/ppermute | solution.py:224
  6.1 10.8 %collective-permute-start.4 = (bf16[224,768]{1,0:T(8,128)(2,1)S(1)}, bf16[224,768]{1,0:T(8,128)(2,1)S(1)}, u32[]{:S(2)}, u32[]{:S(2)}) collective-permute-start(bf16[224,768]{1,0:T(8,128)(2,1)S(1)} %get-tuple-element.17), channel_id=1, source_target_pairs={{0,8},{8,16},{16,24},{24,0},{1,9},{9,17},{17,25},{25,1},{2,10},{10... | collective-permute-start | bytes 1032200 | tf_op jit(solution)/shard_map/ppermute | solution.py:224
  6.1 10.8 %collective-permute-start.5 = (bf16[224,768]{1,0:T(8,128)(2,1)S(1)}, bf16[224,768]{1,0:T(8,128)(2,1)S(1)}, u32[]{:S(2)}, u32[]{:S(2)}) collective-permute-start(bf16[224,768]{1,0:T(8,128)(2,1)S(1)} %get-tuple-element.18), channel_id=1, source_target_pairs={{0,24},{8,0},{16,8},{24,16},{1,25},{9,1},{17,9},{25,17},{2,26},{10... | collective-permute-start | bytes 1032200 | tf_op jit(solution)/shard_map/ppermute | solution.py:224
  8.9 6.1 %collective-permute-start.1 = (bf16[2,224,128]{2,1,0:T(8,128)(2,1)S(1)}, bf16[2,224,128]{2,1,0:T(8,128)(2,1)S(1)}, u32[]{:S(2)}, u32[]{:S(2)}) collective-permute-start(bf16[2,224,128]{2,1,0:T(8,128)(2,1)S(1)} %get-tuple-element.29), channel_id=1, source_target_pairs={{0,64},{64,128},{128,192},{192,0},{1,65},{65,129},{129,193},{193,1... | collective-permute-start | bytes 344072 | tf_op jit(solution)/shard_map/ppermute | solution.py:224
  9.0 7.2 %collective-permute-start.2 = (bf16[2,224,128]{2,1,0:T(8,128)(2,1)S(1)}, bf16[2,224,128]{2,1,0:T(8,128)(2,1)S(1)}, u32[]{:S(2)}, u32[]{:S(2)}) collective-permute-start(bf16[2,224,128]{2,1,0:T(8,128)(2,1)S(1)} %get-tuple-element.30), channel_id=1, source_target_pairs={{0,128},{64,192},{128,0},{192,64},{1,129},{65,193},{129,1},{193,65... | collective-permute-start | bytes 344072 | tf_op jit(solution)/shard_map/ppermute | solution.py:224
  11.1 5.8 %collective-permute-start.3 = (bf16[2,224,128]{2,1,0:T(8,128)(2,1)S(1)}, bf16[2,224,128]{2,1,0:T(8,128)(2,1)S(1)}, u32[]{:S(2)}, u32[]{:S(2)}) collective-permute-start(bf16[2,224,128]{2,1,0:T(8,128)(2,1)S(1)} %get-tuple-element.31), channel_id=1, source_target_pairs={{0,192},{64,0},{128,64},{192,128},{1,193},{65,1},{129,65},{193,129... | collective-permute-start | bytes 344072 | tf_op jit(solution)/shard_map/ppermute | solution.py:224
  17.0 0.7 copy-start.2
  17.0 0.9 copy-start.3
  17.8 37.7 %all-to-all-start = ((bf16[8,128,1024]{2,1,0:T(8,128)(2,1)}), bf16[8,128,1024]{2,1,0:T(8,128)(2,1)S(1)}, u32[]{:S(2)}, u32[]{:S(2)}) async-start(bf16[8,128,1024]{2,1,0:T(8,128)(2,1)} %param.4), calls=%async_computation | async-start | bytes 4194304 | tf_op jit(solution)/shard_map/all_to_all | solution.py:254
  23.6 31.9 %collective-permute-start.9 = (bf16[8,224,128]{2,1,0:T(8,128)(2,1)S(1)}, bf16[8,224,128]{2,1,0:T(8,128)(2,1)S(1)}, u32[]{:S(2)}, u32[]{:S(2)}) collective-permute-start(bf16[8,224,128]{2,1,0:T(8,128)(2,1)S(1)} %pad_maximum_fusion.tokens_ref), channel_id=1, source_target_pairs={{0,24},{8,0},{16,8},{24,16},{1,25},{9,1},{17,9},{25,17},{2,26},{10... | collective-permute-start | bytes 1376264 | tf_op jit(solution)/shard_map/ppermute | solution.py:224
  25.0 30.6 %collective-permute-start.8 = (bf16[8,224,128]{2,1,0:T(8,128)(2,1)S(1)}, bf16[8,224,128]{2,1,0:T(8,128)(2,1)}, u32[]{:S(2)}, u32[]{:S(2)}) collective-permute-start(bf16[8,224,128]{2,1,0:T(8,128)(2,1)S(1)} %pad_maximum_fusion.tokens_ref), channel_id=1, source_target_pairs={{0,16},{8,24},{16,0},{24,8},{1,17},{9,25},{17,1},{25,9},{2,18},{10... | collective-permute-start | bytes 1376264 | tf_op jit(solution)/shard_map/ppermute | solution.py:224
  25.0 30.6 %collective-permute-start.7 = (bf16[8,224,128]{2,1,0:T(8,128)(2,1)S(1)}, bf16[8,224,128]{2,1,0:T(8,128)(2,1)}, u32[]{:S(2)}, u32[]{:S(2)}) collective-permute-start(bf16[8,224,128]{2,1,0:T(8,128)(2,1)S(1)} %pad_maximum_fusion.tokens_ref), channel_id=1, source_target_pairs={{0,8},{8,16},{16,24},{24,0},{1,9},{9,17},{17,25},{25,1},{2,10},{10... | collective-permute-start | bytes 1376264 | tf_op jit(solution)/shard_map/ppermute | solution.py:224
  25.6 29.9 %collective-permute-start.6 = (bf16[224,768]{1,0:T(8,128)(2,1)S(1)}, bf16[224,768]{1,0:T(8,128)(2,1)}, u32[]{:S(2)}, u32[]{:S(2)}) collective-permute-start(bf16[224,768]{1,0:T(8,128)(2,1)S(1)} %get-tuple-element.24), channel_id=1, source_target_pairs={{0,16},{8,24},{16,0},{24,8},{1,17},{9,25},{17,1},{25,9},{2,18},{10... | collective-permute-start | bytes 1032200 | tf_op jit(solution)/shard_map/ppermute | solution.py:224
  55.6 0.8 copy-start.1
  62.7 8.6 %collective-permute-start.12 = (bf16[304,128]{1,0:T(8,128)(2,1)S(1)}, bf16[304,128]{1,0:T(8,128)(2,1)S(1)}, u32[]{:S(2)}, u32[]{:S(2)}) collective-permute-start(bf16[304,128]{1,0:T(8,128)(2,1)S(1)} %get-tuple-element.32), channel_id=1, source_target_pairs={{0,6},{2,0},{4,2},{6,4},{1,7},{3,1},{5,3},{7,5},{8,14},{10,8},{12,... | collective-permute-start | bytes 233480 | tf_op jit(solution)/shard_map/ppermute | solution.py:224
  68.1 7.4 %collective-permute-start.11 = (bf16[304,128]{1,0:T(8,128)(2,1)S(1)}, bf16[304,128]{1,0:T(8,128)(2,1)S(1)}, u32[]{:S(2)}, u32[]{:S(2)}) collective-permute-start(bf16[304,128]{1,0:T(8,128)(2,1)S(1)} %get-tuple-element.33), channel_id=1, source_target_pairs={{0,4},{2,6},{4,0},{6,2},{1,5},{3,7},{5,1},{7,3},{8,12},{10,14},{12... | collective-permute-start | bytes 233480 | tf_op jit(solution)/shard_map/ppermute | solution.py:224
  69.3 7.3 %collective-permute-start.10 = (bf16[304,128]{1,0:T(8,128)(2,1)S(1)}, bf16[304,128]{1,0:T(8,128)(2,1)S(1)}, u32[]{:S(2)}, u32[]{:S(2)}) collective-permute-start(bf16[304,128]{1,0:T(8,128)(2,1)S(1)} %get-tuple-element.34), channel_id=1, source_target_pairs={{0,2},{2,4},{4,6},{6,0},{1,3},{3,5},{5,7},{7,1},{8,10},{10,12},{12... | collective-permute-start | bytes 233480 | tf_op jit(solution)/shard_map/ppermute | solution.py:224
  76.7 3.3 %collective-permute-start.13 = (bf16[304,128]{1,0:T(8,128)(2,1)S(1)}, bf16[304,128]{1,0:T(8,128)(2,1)S(1)}, u32[]{:S(2)}, u32[]{:S(2)}) collective-permute-start(bf16[304,128]{1,0:T(8,128)(2,1)S(1)} %sum.2.refs_0_), channel_id=1, source_target_pairs={{0,1},{1,0},{2,3},{3,2},{4,5},{5,4},{6,7},{7,6},{8,9},{9,8},{10,11... | collective-permute-start | bytes 233480 | tf_op jit(solution)/shard_map/ppermute | solution.py:224
  80.1 7.2 %collective-permute-start.16 = (bf16[304,128]{1,0:T(8,128)(2,1)S(1)}, bf16[304,128]{1,0:T(8,128)(2,1)S(1)}, u32[]{:S(2)}, u32[]{:S(2)}) collective-permute-start(bf16[304,128]{1,0:T(8,128)(2,1)S(1)} %sum.3), channel_id=1, source_target_pairs={{0,6},{2,0},{4,2},{6,4},{1,7},{3,1},{5,3},{7,5},{8,14},{10,8},{12,... | collective-permute-start | bytes 233480 | tf_op jit(solution)/shard_map/ppermute | solution.py:224
  82.9 7.3 %collective-permute-start.15 = (bf16[304,128]{1,0:T(8,128)(2,1)S(1)}, bf16[304,128]{1,0:T(8,128)(2,1)S(1)}, u32[]{:S(2)}, u32[]{:S(2)}) collective-permute-start(bf16[304,128]{1,0:T(8,128)(2,1)S(1)} %sum.3), channel_id=1, source_target_pairs={{0,4},{2,6},{4,0},{6,2},{1,5},{3,7},{5,1},{7,3},{8,12},{10,14},{12... | collective-permute-start | bytes 233480 | tf_op jit(solution)/shard_map/ppermute | solution.py:224
  85.1 6.0 %collective-permute-start.14 = (bf16[304,128]{1,0:T(8,128)(2,1)S(1)}, bf16[304,128]{1,0:T(8,128)(2,1)S(1)}, u32[]{:S(2)}, u32[]{:S(2)}) collective-permute-start(bf16[304,128]{1,0:T(8,128)(2,1)S(1)} %sum.3), channel_id=1, source_target_pairs={{0,2},{2,4},{4,6},{6,0},{1,3},{3,5},{5,7},{7,1},{8,10},{10,12},{12... | collective-permute-start | bytes 233480 | tf_op jit(solution)/shard_map/ppermute | solution.py:224
  91.1 5.8 %collective-permute-start.19 = (bf16[4,304,128]{2,1,0:T(8,128)(2,1)S(1)}, bf16[4,304,128]{2,1,0:T(8,128)(2,1)S(1)}, u32[]{:S(2)}, u32[]{:S(2)}) collective-permute-start(bf16[4,304,128]{2,1,0:T(8,128)(2,1)S(1)} %pad_maximum_fusion.1.refs_0_), channel_id=1, source_target_pairs={{0,24},{8,0},{16,8},{24,16},{1,25},{9,1},{17,9},{25,17},{2,26},{10... | collective-permute-start | bytes 933896 | tf_op jit(solution)/shard_map/ppermute | solution.py:224
  91.2 7.4 %collective-permute-start.18 = (bf16[4,304,128]{2,1,0:T(8,128)(2,1)S(1)}, bf16[4,304,128]{2,1,0:T(8,128)(2,1)S(1)}, u32[]{:S(2)}, u32[]{:S(2)}) collective-permute-start(bf16[4,304,128]{2,1,0:T(8,128)(2,1)S(1)} %pad_maximum_fusion.1.refs_0_), channel_id=1, source_target_pairs={{0,16},{8,24},{16,0},{24,8},{1,17},{9,25},{17,1},{25,9},{2,18},{10... | collective-permute-start | bytes 933896 | tf_op jit(solution)/shard_map/ppermute | solution.py:224
  91.6 14.6 %collective-permute-start.17 = (bf16[4,304,128]{2,1,0:T(8,128)(2,1)S(1)}, bf16[4,304,128]{2,1,0:T(8,128)(2,1)S(1)}, u32[]{:S(2)}, u32[]{:S(2)}) collective-permute-start(bf16[4,304,128]{2,1,0:T(8,128)(2,1)S(1)} %pad_maximum_fusion.1.refs_0_), channel_id=1, source_target_pairs={{0,8},{8,16},{16,24},{24,0},{1,9},{9,17},{17,25},{25,1},{2,10},{10... | collective-permute-start | bytes 933896 | tf_op jit(solution)/shard_map/ppermute | solution.py:224

commit v8 on v7

--- a/solution.py
+++ b/solution.py
@@ -52,7 +52,7 @@
     return pl.ds(pl.multiple_of(lax.rem(2 * place + block, FF // BLOCK) * BLOCK, BLOCK), BLOCK)
 
 
-def outgoing_kernel(place_ref, group_ref, momentum_away_ref, tokens_ref, *refs):
+def outgoing_kernel(place_ref, group_ref, counts_ref, momentum_away_ref, tokens_ref, *refs):
     *column_refs, kept_ref, sent_ref, momentum_ref, semaphores = refs
     chip, core = lax.div(group_ref[0], CORES), lax.rem(group_ref[0], CORES)
     chips = kept_ref.shape[0]
@@ -69,6 +69,12 @@
             column_ref[:, block * BLOCK : (block + 1) * BLOCK] = value.astype(BF16)
     for copy in copies[1:]:
         copy.wait()
+    lanes = lax.broadcasted_iota(jnp.int32, tokens_ref.shape[1:], 1)
+    for distance in range(chips):
+        first = lax.rem(chip + distance, chips) * CORES
+        for ref, expert in ((kept_ref, first + core), (sent_ref, first + 1 - core)):
+            tokens = ref[distance].astype(F32)
+            ref[distance] = jnp.where(lanes < counts_ref[expert] * TILE, tokens, 0.0).astype(BF16)
 
 
 def fetched(sources, targets, semaphores):
@@ -81,23 +87,21 @@
     return copies
 
 
-def gram_kernel(place_ref, group_ref, counts_ref, hidden_ref, tokens_ref, *refs):
+def gram_kernel(place_ref, group_ref, hidden_ref, tokens_ref, *refs):
     count = (len(refs) - 4) // 2
     away_refs, moment_ref, cut_ref, needed_ref = refs[:count], *refs[count : count + 3]
     here_refs, semaphores = refs[count + 3 : -1], refs[-1]
     copies = fetched(away_refs, here_refs, semaphores)
     momentum_ref, other_refs = here_refs[0], here_refs[1:]
-    groups, height, width = tokens_ref.shape
+    groups, _, width = tokens_ref.shape
     place = place_ref[0]
-    lanes = lax.broadcasted_iota(jnp.int32, (height, width), 1)
 
     def tokens_of(ref):
         kept = []
         for g in range(groups):
             chip, core = divmod(g, CORES)
             distance = lax.rem(lax.div(group_ref[0], CORES) - chip + groups, groups // CORES)
-            tokens = ref[CORES * distance + lax.rem(group_ref[0] + core, CORES)].astype(F32)
-            kept.append(jnp.where(lanes < counts_ref[g] * TILE, tokens, 0.0).astype(BF16))
+            kept.append(ref[CORES * distance + lax.rem(group_ref[0] + core, CORES)])
         return jnp.concatenate(kept, axis=1)
 
     gradient = jnp.dot(
@@ -183,17 +187,20 @@
         both = jnp.dot(
             jnp.concatenate(split_two(value), axis=0), gram_ref[...], preferred_element_type=F32
         )
-        return (both[:rows] + both[rows:]) * factor * factor
+        return both[:rows] + both[rows:]
+
+    square = factor * factor
+    linear, cubic = COEF_B * square, COEF_C * square * square
 
     def by_first(value):
-        return COEF_A * value + by_gram(COEF_B * value + COEF_C * by_gram(value))
+        return COEF_A * value + by_gram(linear * value + cubic * by_gram(value))
 
     def by_second_gram(value):
         return by_first(by_gram(by_first(value)))
 
     copies[0].wait()
     once = by_first(moment_ref[...] * factor)
-    twice = COEF_A * once + by_second_gram(COEF_B * once + COEF_C * by_second_gram(once))
+    twice = COEF_A * once + by_second_gram(linear * once + cubic * by_second_gram(once))
     update_ref[...] = twice * math.sqrt(max(FF, D))
 
 
@@ -229,7 +236,7 @@
     rows = momentum.shape[1]
     piece = len(block_pairs(0)) * BLOCK // pairs
     group = lax.axis_index(DP).astype(jnp.int32)
-    counts = lax.dynamic_index_in_dim(filled_tile_count, group, 1, keepdims=False)
+    counts = lax.dynamic_index_in_dim(filled_tile_count, group, 0, keepdims=False)
     group = group.reshape(1)
     place = jnp.stack([lax.axis_index("x"), lax.axis_index("z_pair")]).astype(jnp.int32)
     distances = range(1, along_x)
@@ -239,11 +246,11 @@
     *columns, kept, sent = call(
         outgoing_kernel,
         [jax.ShapeDtypeStruct((rows, NEEDED * BLOCK), BF16) for _ in distances] + [half, half],
-        [place, group]
+        [place, group, counts]
         + [pltpu.with_memory_space_constraint(value, pltpu.HBM) for value in (momentum[0], gradient_token_tiles)],
         scratch=[pltpu.VMEM((rows, FF), F32), pltpu.SemaphoreType.DMA((1 + CORES * along_y,))],
-        away=(2, 3),
-        scalars=2,
+        away=(3, 4),
+        scalars=3,
     )
     other_columns = [shifted(columns[k - 1], "x", k) for k in distances]
     both = jnp.stack([kept, shifted(sent, "core", 1)], axis=1)
@@ -264,12 +271,12 @@
             jax.ShapeDtypeStruct((rows, FF), F32),
             jax.ShapeDtypeStruct((pairs, piece + UNIT, BLOCK), BF16),
         ),
-        [place, group, counts, hidden, tokens] + fetch,
+        [place, group, hidden, tokens] + fetch,
         scratch=[pltpu.VMEM((hidden.shape[0] * hidden.shape[1], NEEDED * BLOCK), BF16)]
         + [pltpu.VMEM(value.shape, value.dtype) for value in fetch]
         + [pltpu.SemaphoreType.DMA((len(fetch),))],
-        away=range(5, 5 + len(fetch)),
-        scalars=3,
+        away=range(4, 4 + len(fetch)),
+        scalars=2,
         mib=28,
     )
     summed = jax.ShapeDtypeStruct((piece + UNIT, BLOCK), BF16)

time: 147 us -> 148 us (level)
    unnamed x8 -> x12, local copies, waits for them, and re-layouts: 1.61 us -> 2.96 us
where the time goes in v8:
time: 148 us
  waiting for transfers between devices  57.2 us (39%)
  starting transfers between devices  37.6 us (25%)
  blocking collectives  22.7 us (15%)
  Pallas kernels  22.5 us (15%)
  other arithmetic  4.37 us (3%)
  local copies, waits for them, and re-layouts  2.99 us (2%)
    ppermute x20, waiting for transfers between devices, shifted(): lax.ppermute(value, axis, [(i, (i + distance) % size) for i in range(size)])  57.2 us
    ppermute x20, starting transfers between devices, shifted(): lax.ppermute(value, axis, [(i, (i + distance) % size) for i in range(size)])  31.9 us
    all_gather x1, blocking collectives, body(): lax.all_gather((update * 256.0).astype(jnp.float16), DP, axis=0, tiled=Fa...  22.7 us
    pallas_call x5, Pallas kernels, call(): pl.pallas_call(kernel, out_shape=out_shape, in_specs=[whole(pltpu.SMEM if...  22.5 us
    all_to_all x1, starting transfers between devices, body(): hidden = lax.all_to_all(hidden_token_tiles, DP, 0, 0, tiled=True)  5.74 us
    mul x1, other arithmetic, body(): return (moment[None], gathered.astype(F32) * (1.0 / 256.0))  4.07 us
    unnamed x12, local copies, waits for them, and re-layouts  2.96 us
  transfers between devices with their start and end apart: 21, of which 12 were waited for; matrix products, arithmetic and copies ran while one was open for 0% of the time, Pallas kernels for 0%

profile of v8, /device:TPU:1, one launch (start us, length us, event | category | flops | bytes accessed | tf_op | source)
XLA Modules:
  0.0 148.2 jit_solution(15490950002286051944)
XLA Ops:
  1.3 2.2 %outgoing.1 = (bf16[224,768]{1,0:T(8,128)(2,1)S(1)}, bf16[224,768]{1,0:T(8,128)(2,1)S(1)}, bf16[224,768]{1,0:T(8,128)(2,1)S(1)}, bf16[4,224,128]{2,1,0:T(8,128)(2,1)S(1)}, bf16[4,224,128]{2,1,0:T(8,128)(2,1)S(1)}) custom-call(s32[2]{0:T(128)S(1)} %pad_add_fusion.place_ref, s32[1]{0:T(128)} %bitcast.2.group_ref, s32[8]{0:T(128)S(1)} %dynamic-slice_bitcast_fusion.counts_ref, ...), custom_call_target="tpu_custom_call" | custom-call | tf_op jit(solution)/shard_map/outgoing/pallas_call | solution.py:215
  3.5 3.3 %collective-permute-start = (bf16[4,224,128]{2,1,0:T(8,128)(2,1)S(1)}, bf16[4,224,128]{2,1,0:T(8,128)(2,1)S(1)}, u32[]{:S(2)}, u32[]{:S(2)}) collective-permute-start(bf16[4,224,128]{2,1,0:T(8,128)(2,1)S(1)} %get-tuple-element.16), channel_id=1, source_target_pairs={{0,32},{32,0},{1,33},{33,1},{2,34},{34,2},{3,35},{35,3},{4,36},{36... | collective-permute-start | bytes 688136 | tf_op jit(solution)/shard_map/ppermute | solution.py:231
  6.8 2.7 %collective-permute-start.5 = (bf16[224,768]{1,0:T(8,128)(2,1)S(1)}, bf16[224,768]{1,0:T(8,128)(2,1)S(1)}, u32[]{:S(2)}, u32[]{:S(2)}) collective-permute-start(bf16[224,768]{1,0:T(8,128)(2,1)S(1)} %get-tuple-element.18), channel_id=1, source_target_pairs={{0,24},{8,0},{16,8},{24,16},{1,25},{9,1},{17,9},{25,17},{2,26},{10... | collective-permute-start | bytes 1032200 | tf_op jit(solution)/shard_map/ppermute | solution.py:231
  9.7 2.2 %collective-permute-start.2 = (bf16[2,224,128]{2,1,0:T(8,128)(2,1)S(1)}, bf16[2,224,128]{2,1,0:T(8,128)(2,1)S(1)}, u32[]{:S(2)}, u32[]{:S(2)}) collective-permute-start(bf16[2,224,128]{2,1,0:T(8,128)(2,1)S(1)} %get-tuple-element.30), channel_id=1, source_target_pairs={{0,128},{64,192},{128,0},{192,64},{1,129},{65,193},{129,1},{193,65... | collective-permute-start | bytes 344072 | tf_op jit(solution)/shard_map/ppermute | solution.py:231
  11.8 1.1 collective-permute-start.3
  12.9 2.7 %collective-permute-done.1 = bf16[2,224,128]{2,1,0:T(8,128)(2,1)S(1)} collective-permute-done((bf16[2,224,128]{2,1,0:T(8,128)(2,1)S(1)}, bf16[2,224,128]{2,1,0:T(8,128)(2,1)S(1)}, u32[]{:S(2)}, u32[]{:S(2)}) %collective-permute-start.1) | collective-permute-done | bytes 114720 | tf_op jit(solution)/shard_map/ppermute | solution.py:231
  15.6 1.2 collective-permute-done.2
  16.9 0.8 collective-permute-done.3
  18.5 5.7 %all-to-all-start = ((bf16[8,128,1024]{2,1,0:T(8,128)(2,1)}), bf16[8,128,1024]{2,1,0:T(8,128)(2,1)S(1)}, u32[]{:S(2)}, u32[]{:S(2)}) async-start(bf16[8,128,1024]{2,1,0:T(8,128)(2,1)} %param.4), calls=%async_computation | async-start | bytes 4194304 | tf_op jit(solution)/shard_map/all_to_all | solution.py:261
  24.3 1.3 collective-permute-start.9
  26.3 3.1 %collective-permute-start.6 = (bf16[224,768]{1,0:T(8,128)(2,1)S(1)}, bf16[224,768]{1,0:T(8,128)(2,1)S(1)}, u32[]{:S(2)}, u32[]{:S(2)}) collective-permute-start(bf16[224,768]{1,0:T(8,128)(2,1)S(1)} %get-tuple-element.24), channel_id=1, source_target_pairs={{0,16},{8,24},{16,0},{24,8},{1,17},{9,25},{17,1},{25,9},{2,18},{10... | collective-permute-start | bytes 1032200 | tf_op jit(solution)/shard_map/ppermute | solution.py:231
  29.5 26.7 %collective-permute-done.6.refs_2_ = bf16[224,768]{1,0:T(8,128)(2,1)S(1)} collective-permute-done((bf16[224,768]{1,0:T(8,128)(2,1)S(1)}, bf16[224,768]{1,0:T(8,128)(2,1)S(1)}, u32[]{:S(2)}, u32[]{:S(2)}) %collective-permute-start.6) | collective-permute-done | bytes 344096 | tf_op jit(solution)/shard_map/ppermute | solution.py:231
  56.9 0.8 copy-done.2
  57.6 6.3 %gram.1 = (f32[224,1024]{1,0:T(8,128)}, bf16[4,304,128]{2,1,0:T(8,128)(2,1)S(1)}) custom-call(s32[2]{0:T(128)S(1)} %pad_add_fusion.place_ref, s32[1]{0:T(128)} %bitcast.2.group_ref, bf16[8,128,1024]{2,1,0:T(8,128)(2,1)S(1)} %all-to-all-done.hidden_ref, bf16[8,224,128]{2,1,0:T(8,128)(2,1)S(1)} %pad_maximum_fusion.tokens_ref, f32[224,1024]{1,0:T(8,128)} %bitcast.34, ...), custom_call_target="tpu_custom_call" | custom-call | tf_op jit(solution)/shard_map/gram/pallas_call | solution.py:215
  64.0 5.4 %collective-permute-start.12 = (bf16[304,128]{1,0:T(8,128)(2,1)S(1)}, bf16[304,128]{1,0:T(8,128)(2,1)S(1)}, u32[]{:S(2)}, u32[]{:S(2)}) collective-permute-start(bf16[304,128]{1,0:T(8,128)(2,1)S(1)} %get-tuple-element.32), channel_id=1, source_target_pairs={{0,6},{2,0},{4,2},{6,4},{1,7},{3,1},{5,3},{7,5},{8,14},{10,8},{12,... | collective-permute-start | bytes 233480 | tf_op jit(solution)/shard_map/ppermute | solution.py:231
  69.4 1.2 collective-permute-start.11
  70.6 2.1 %collective-permute-start.10 = (bf16[304,128]{1,0:T(8,128)(2,1)S(1)}, bf16[304,128]{1,0:T(8,128)(2,1)S(1)}, u32[]{:S(2)}, u32[]{:S(2)}) collective-permute-start(bf16[304,128]{1,0:T(8,128)(2,1)S(1)} %get-tuple-element.34), channel_id=1, source_target_pairs={{0,2},{2,4},{4,6},{6,0},{1,3},{3,5},{5,7},{7,1},{8,10},{10,12},{12... | collective-permute-start | bytes 233480 | tf_op jit(solution)/shard_map/ppermute | solution.py:231
  72.7 4.1 %collective-permute-done.11.refs_2_ = bf16[304,128]{1,0:T(8,128)(2,1)S(1)} collective-permute-done((bf16[304,128]{1,0:T(8,128)(2,1)S(1)}, bf16[304,128]{1,0:T(8,128)(2,1)S(1)}, u32[]{:S(2)}, u32[]{:S(2)}) %collective-permute-start.11) | collective-permute-done | bytes 77856 | tf_op jit(solution)/shard_map/ppermute | solution.py:231
  76.8 1.1 collective-permute-done.10.refs_1_
  78.1 3.2 %collective-permute-done.13.refs_1_ = bf16[304,128]{1,0:T(8,128)(2,1)S(1)} collective-permute-done((bf16[304,128]{1,0:T(8,128)(2,1)S(1)}, bf16[304,128]{1,0:T(8,128)(2,1)S(1)}, u32[]{:S(2)}, u32[]{:S(2)}) %collective-permute-start.13) | collective-permute-done | bytes 77856 | tf_op jit(solution)/shard_map/ppermute | solution.py:231
  81.4 2.9 %collective-permute-start.16 = (bf16[304,128]{1,0:T(8,128)(2,1)S(1)}, bf16[304,128]{1,0:T(8,128)(2,1)S(1)}, u32[]{:S(2)}, u32[]{:S(2)}) collective-permute-start(bf16[304,128]{1,0:T(8,128)(2,1)S(1)} %sum.3), channel_id=1, source_target_pairs={{0,6},{2,0},{4,2},{6,4},{1,7},{3,1},{5,3},{7,5},{8,14},{10,8},{12,... | collective-permute-start | bytes 233480 | tf_op jit(solution)/shard_map/ppermute | solution.py:231
  84.3 2.1 %collective-permute-start.15 = (bf16[304,128]{1,0:T(8,128)(2,1)S(1)}, bf16[304,128]{1,0:T(8,128)(2,1)S(1)}, u32[]{:S(2)}, u32[]{:S(2)}) collective-permute-start(bf16[304,128]{1,0:T(8,128)(2,1)S(1)} %sum.3), channel_id=1, source_target_pairs={{0,4},{2,6},{4,0},{6,2},{1,5},{3,7},{5,1},{7,3},{8,12},{10,14},{12... | collective-permute-start | bytes 233480 | tf_op jit(solution)/shard_map/ppermute | solution.py:231
  86.4 2.2 %collective-permute-start.14 = (bf16[304,128]{1,0:T(8,128)(2,1)S(1)}, bf16[304,128]{1,0:T(8,128)(2,1)S(1)}, u32[]{:S(2)}, u32[]{:S(2)}) collective-permute-start(bf16[304,128]{1,0:T(8,128)(2,1)S(1)} %sum.3), channel_id=1, source_target_pairs={{0,2},{2,4},{4,6},{6,0},{1,3},{3,5},{5,7},{7,1},{8,10},{10,12},{12... | collective-permute-start | bytes 233480 | tf_op jit(solution)/shard_map/ppermute | solution.py:231
  88.6 2.9 %collective-permute-done.15 = bf16[304,128]{1,0:T(8,128)(2,1)S(1)} collective-permute-done((bf16[304,128]{1,0:T(8,128)(2,1)S(1)}, bf16[304,128]{1,0:T(8,128)(2,1)S(1)}, u32[]{:S(2)}, u32[]{:S(2)}) %collective-permute-start.15) | collective-permute-done | bytes 77856 | tf_op jit(solution)/shard_map/ppermute | solution.py:231
  91.5 0.8 collective-permute-done.14
  92.9 1.0 collective-permute-start.17
  94.0 4.3 %collective-permute-done.19.refs_3_ = bf16[4,304,128]{2,1,0:T(8,128)(2,1)S(1)} collective-permute-done((bf16[4,304,128]{2,1,0:T(8,128)(2,1)S(1)}, bf16[4,304,128]{2,1,0:T(8,128)(2,1)S(1)}, u32[]{:S(2)}, u32[]{:S(2)}) %collective-permute-start.19) | collective-permute-done | bytes 311328 | tf_op jit(solution)/shard_map/ppermute | solution.py:231
  98.2 1.7 %collective-permute-done.18.refs_2_ = bf16[4,304,128]{2,1,0:T(8,128)(2,1)S(1)} collective-permute-done((bf16[4,304,128]{2,1,0:T(8,128)(2,1)S(1)}, bf16[4,304,128]{2,1,0:T(8,128)(2,1)S(1)}, u32[]{:S(2)}, u32[]{:S(2)}) %collective-permute-start.18) | collective-permute-done | bytes 311328 | tf_op jit(solution)/shard_map/ppermute | solution.py:231
  100.0 7.6 %collective-permute-done.17.refs_1_ = bf16[4,304,128]{2,1,0:T(8,128)(2,1)S(1)} collective-permute-done((bf16[4,304,128]{2,1,0:T(8,128)(2,1)S(1)}, bf16[4,304,128]{2,1,0:T(8,128)(2,1)S(1)}, u32[]{:S(2)}, u32[]{:S(2)}) %collective-permute-start.17) | collective-permute-done | bytes 311328 | tf_op jit(solution)/shard_map/ppermute | solution.py:231
  107.5 13.8 %polynomial.1 = f32[224,1024]{1,0:T(8,128)S(1)} custom-call(s32[2]{0:T(128)S(1)} %pad_add_fusion.place_ref, f32[224,1024]{1,0:T(8,128)} %get-tuple-element.26.moment_away_ref, bf16[4,304,128]{2,1,0:T(8,128)(2,1)S(1)} %pad_maximum_fusion.1.refs_0_, bf16[4,304,128]{2,1,0:T(8,128)(2,1)S(1)} %collective-permute-done.17.refs_1_, ...), custom_call_target="tpu_custom_call" | custom-call | tf_op jit(solution)/shard_map/polynomial/pallas_call | solution.py:215
  121.5 22.7 %all-gather.2 = f16[1792,1024]{1,0:T(8,128)(2,1)S(1)} all-gather(f16[224,1024]{1,0:T(8,128)(2,1)S(1)} %multiply_convert_fusion), channel_id=2, replica_groups=mesh['y'=4,'core'=2,'x'=4,'z_pair'=4,'z_low'=2] {'y','core'}, dimensions={0}, use_global_device_ids=true | all-gather | bytes 4128768 | tf_op jit(solution)/shard_map/all_gather | solution.py:300
  144.2 4.1 %convert_multiply_fusion = f32[1792,1024]{1,0:T(8,128)} fusion(f16[1792,1024]{1,0:T(8,128)(2,1)S(1)} %all-gather.2), kind=kLoop, calls=%fused_computation | loop fusion | flops 3670016 | bytes 11010048 | tf_op jit(solution)/shard_map/mul | solution.py:301
  (36 shorter events, 4.1 us)
Async XLA Ops:
  0.6 0.7 copy-start
  3.5 6.0 %collective-permute-start = (bf16[4,224,128]{2,1,0:T(8,128)(2,1)S(1)}, bf16[4,224,128]{2,1,0:T(8,128)(2,1)S(1)}, u32[]{:S(2)}, u32[]{:S(2)}) collective-permute-start(bf16[4,224,128]{2,1,0:T(8,128)(2,1)S(1)} %get-tuple-element.16), channel_id=1, source_target_pairs={{0,32},{32,0},{1,33},{33,1},{2,34},{34,2},{3,35},{35,3},{4,36},{36... | collective-permute-start | bytes 688136 | tf_op jit(solution)/shard_map/ppermute | solution.py:231
  6.8 10.8 %collective-permute-start.4 = (bf16[224,768]{1,0:T(8,128)(2,1)S(1)}, bf16[224,768]{1,0:T(8,128)(2,1)S(1)}, u32[]{:S(2)}, u32[]{:S(2)}) collective-permute-start(bf16[224,768]{1,0:T(8,128)(2,1)S(1)} %get-tuple-element.17), channel_id=1, source_target_pairs={{0,8},{8,16},{16,24},{24,0},{1,9},{9,17},{17,25},{25,1},{2,10},{10... | collective-permute-start | bytes 1032200 | tf_op jit(solution)/shard_map/ppermute | solution.py:231
  6.8 10.8 %collective-permute-start.5 = (bf16[224,768]{1,0:T(8,128)(2,1)S(1)}, bf16[224,768]{1,0:T(8,128)(2,1)S(1)}, u32[]{:S(2)}, u32[]{:S(2)}) collective-permute-start(bf16[224,768]{1,0:T(8,128)(2,1)S(1)} %get-tuple-element.18), channel_id=1, source_target_pairs={{0,24},{8,0},{16,8},{24,16},{1,25},{9,1},{17,9},{25,17},{2,26},{10... | collective-permute-start | bytes 1032200 | tf_op jit(solution)/shard_map/ppermute | solution.py:231
  9.6 6.1 %collective-permute-start.1 = (bf16[2,224,128]{2,1,0:T(8,128)(2,1)S(1)}, bf16[2,224,128]{2,1,0:T(8,128)(2,1)S(1)}, u32[]{:S(2)}, u32[]{:S(2)}) collective-permute-start(bf16[2,224,128]{2,1,0:T(8,128)(2,1)S(1)} %get-tuple-element.29), channel_id=1, source_target_pairs={{0,64},{64,128},{128,192},{192,0},{1,65},{65,129},{129,193},{193,1... | collective-permute-start | bytes 344072 | tf_op jit(solution)/shard_map/ppermute | solution.py:231
  9.7 7.2 %collective-permute-start.2 = (bf16[2,224,128]{2,1,0:T(8,128)(2,1)S(1)}, bf16[2,224,128]{2,1,0:T(8,128)(2,1)S(1)}, u32[]{:S(2)}, u32[]{:S(2)}) collective-permute-start(bf16[2,224,128]{2,1,0:T(8,128)(2,1)S(1)} %get-tuple-element.30), channel_id=1, source_target_pairs={{0,128},{64,192},{128,0},{192,64},{1,129},{65,193},{129,1},{193,65... | collective-permute-start | bytes 344072 | tf_op jit(solution)/shard_map/ppermute | solution.py:231
  11.8 5.8 %collective-permute-start.3 = (bf16[2,224,128]{2,1,0:T(8,128)(2,1)S(1)}, bf16[2,224,128]{2,1,0:T(8,128)(2,1)S(1)}, u32[]{:S(2)}, u32[]{:S(2)}) collective-permute-start(bf16[2,224,128]{2,1,0:T(8,128)(2,1)S(1)} %get-tuple-element.31), channel_id=1, source_target_pairs={{0,192},{64,0},{128,64},{192,128},{1,193},{65,1},{129,65},{193,129... | collective-permute-start | bytes 344072 | tf_op jit(solution)/shard_map/ppermute | solution.py:231
  17.7 0.7 copy-start.3
  17.7 0.9 copy-start.4
  18.5 39.1 %all-to-all-start = ((bf16[8,128,1024]{2,1,0:T(8,128)(2,1)}), bf16[8,128,1024]{2,1,0:T(8,128)(2,1)S(1)}, u32[]{:S(2)}, u32[]{:S(2)}) async-start(bf16[8,128,1024]{2,1,0:T(8,128)(2,1)} %param.4), calls=%async_computation | async-start | bytes 4194304 | tf_op jit(solution)/shard_map/all_to_all | solution.py:261
  24.3 31.8 %collective-permute-start.9 = (bf16[8,224,128]{2,1,0:T(8,128)(2,1)S(1)}, bf16[8,224,128]{2,1,0:T(8,128)(2,1)S(1)}, u32[]{:S(2)}, u32[]{:S(2)}) collective-permute-start(bf16[8,224,128]{2,1,0:T(8,128)(2,1)S(1)} %pad_maximum_fusion.tokens_ref), channel_id=1, source_target_pairs={{0,24},{8,0},{16,8},{24,16},{1,25},{9,1},{17,9},{25,17},{2,26},{10... | collective-permute-start | bytes 1376264 | tf_op jit(solution)/shard_map/ppermute | solution.py:231
  25.6 30.5 %collective-permute-start.8 = (bf16[8,224,128]{2,1,0:T(8,128)(2,1)S(1)}, bf16[8,224,128]{2,1,0:T(8,128)(2,1)S(1)}, u32[]{:S(2)}, u32[]{:S(2)}) collective-permute-start(bf16[8,224,128]{2,1,0:T(8,128)(2,1)S(1)} %pad_maximum_fusion.tokens_ref), channel_id=1, source_target_pairs={{0,16},{8,24},{16,0},{24,8},{1,17},{9,25},{17,1},{25,9},{2,18},{10... | collective-permute-start | bytes 1376264 | tf_op jit(solution)/shard_map/ppermute | solution.py:231
  25.6 32.0 %collective-permute-start.7 = (bf16[8,224,128]{2,1,0:T(8,128)(2,1)S(1)}, bf16[8,224,128]{2,1,0:T(8,128)(2,1)}, u32[]{:S(2)}, u32[]{:S(2)}) collective-permute-start(bf16[8,224,128]{2,1,0:T(8,128)(2,1)S(1)} %pad_maximum_fusion.tokens_ref), channel_id=1, source_target_pairs={{0,8},{8,16},{16,24},{24,0},{1,9},{9,17},{17,25},{25,1},{2,10},{10... | collective-permute-start | bytes 1376264 | tf_op jit(solution)/shard_map/ppermute | solution.py:231
  26.3 29.8 %collective-permute-start.6 = (bf16[224,768]{1,0:T(8,128)(2,1)S(1)}, bf16[224,768]{1,0:T(8,128)(2,1)S(1)}, u32[]{:S(2)}, u32[]{:S(2)}) collective-permute-start(bf16[224,768]{1,0:T(8,128)(2,1)S(1)} %get-tuple-element.24), channel_id=1, source_target_pairs={{0,16},{8,24},{16,0},{24,8},{1,17},{9,25},{17,1},{25,9},{2,18},{10... | collective-permute-start | bytes 1032200 | tf_op jit(solution)/shard_map/ppermute | solution.py:231
  56.1 0.7 copy-start.5
  56.1 1.5 %copy-start.1 = (bf16[8,224,128]{2,1,0:T(8,128)(2,1)}, bf16[8,224,128]{2,1,0:T(8,128)(2,1)S(1)}, u32[]{:S(2)}) copy-start(bf16[8,224,128]{2,1,0:T(8,128)(2,1)S(1)} %collective-permute-done.9.refs_6_) | copy-start | bytes 1376260
  56.9 0.8 copy-start.2
  64.0 8.6 %collective-permute-start.12 = (bf16[304,128]{1,0:T(8,128)(2,1)S(1)}, bf16[304,128]{1,0:T(8,128)(2,1)S(1)}, u32[]{:S(2)}, u32[]{:S(2)}) collective-permute-start(bf16[304,128]{1,0:T(8,128)(2,1)S(1)} %get-tuple-element.32), channel_id=1, source_target_pairs={{0,6},{2,0},{4,2},{6,4},{1,7},{3,1},{5,3},{7,5},{8,14},{10,8},{12,... | collective-permute-start | bytes 233480 | tf_op jit(solution)/shard_map/ppermute | solution.py:231
  69.4 7.4 %collective-permute-start.11 = (bf16[304,128]{1,0:T(8,128)(2,1)S(1)}, bf16[304,128]{1,0:T(8,128)(2,1)S(1)}, u32[]{:S(2)}, u32[]{:S(2)}) collective-permute-start(bf16[304,128]{1,0:T(8,128)(2,1)S(1)} %get-tuple-element.33), channel_id=1, source_target_pairs={{0,4},{2,6},{4,0},{6,2},{1,5},{3,7},{5,1},{7,3},{8,12},{10,14},{12... | collective-permute-start | bytes 233480 | tf_op jit(solution)/shard_map/ppermute | solution.py:231
  70.6 7.3 %collective-permute-start.10 = (bf16[304,128]{1,0:T(8,128)(2,1)S(1)}, bf16[304,128]{1,0:T(8,128)(2,1)S(1)}, u32[]{:S(2)}, u32[]{:S(2)}) collective-permute-start(bf16[304,128]{1,0:T(8,128)(2,1)S(1)} %get-tuple-element.34), channel_id=1, source_target_pairs={{0,2},{2,4},{4,6},{6,0},{1,3},{3,5},{5,7},{7,1},{8,10},{10,12},{12... | collective-permute-start | bytes 233480 | tf_op jit(solution)/shard_map/ppermute | solution.py:231
  78.0 3.3 %collective-permute-start.13 = (bf16[304,128]{1,0:T(8,128)(2,1)S(1)}, bf16[304,128]{1,0:T(8,128)(2,1)S(1)}, u32[]{:S(2)}, u32[]{:S(2)}) collective-permute-start(bf16[304,128]{1,0:T(8,128)(2,1)S(1)} %sum.2.refs_0_), channel_id=1, source_target_pairs={{0,1},{1,0},{2,3},{3,2},{4,5},{5,4},{6,7},{7,6},{8,9},{9,8},{10,11... | collective-permute-start | bytes 233480 | tf_op jit(solution)/shard_map/ppermute | solution.py:231
  81.4 7.2 %collective-permute-start.16 = (bf16[304,128]{1,0:T(8,128)(2,1)S(1)}, bf16[304,128]{1,0:T(8,128)(2,1)S(1)}, u32[]{:S(2)}, u32[]{:S(2)}) collective-permute-start(bf16[304,128]{1,0:T(8,128)(2,1)S(1)} %sum.3), channel_id=1, source_target_pairs={{0,6},{2,0},{4,2},{6,4},{1,7},{3,1},{5,3},{7,5},{8,14},{10,8},{12,... | collective-permute-start | bytes 233480 | tf_op jit(solution)/shard_map/ppermute | solution.py:231
  84.3 7.3 %collective-permute-start.15 = (bf16[304,128]{1,0:T(8,128)(2,1)S(1)}, bf16[304,128]{1,0:T(8,128)(2,1)S(1)}, u32[]{:S(2)}, u32[]{:S(2)}) collective-permute-start(bf16[304,128]{1,0:T(8,128)(2,1)S(1)} %sum.3), channel_id=1, source_target_pairs={{0,4},{2,6},{4,0},{6,2},{1,5},{3,7},{5,1},{7,3},{8,12},{10,14},{12... | collective-permute-start | bytes 233480 | tf_op jit(solution)/shard_map/ppermute | solution.py:231
  86.4 6.0 %collective-permute-start.14 = (bf16[304,128]{1,0:T(8,128)(2,1)S(1)}, bf16[304,128]{1,0:T(8,128)(2,1)S(1)}, u32[]{:S(2)}, u32[]{:S(2)}) collective-permute-start(bf16[304,128]{1,0:T(8,128)(2,1)S(1)} %sum.3), channel_id=1, source_target_pairs={{0,2},{2,4},{4,6},{6,0},{1,3},{3,5},{5,7},{7,1},{8,10},{10,12},{12... | collective-permute-start | bytes 233480 | tf_op jit(solution)/shard_map/ppermute | solution.py:231
  92.4 5.8 %collective-permute-start.19 = (bf16[4,304,128]{2,1,0:T(8,128)(2,1)S(1)}, bf16[4,304,128]{2,1,0:T(8,128)(2,1)S(1)}, u32[]{:S(2)}, u32[]{:S(2)}) collective-permute-start(bf16[4,304,128]{2,1,0:T(8,128)(2,1)S(1)} %pad_maximum_fusion.1.refs_0_), channel_id=1, source_target_pairs={{0,24},{8,0},{16,8},{24,16},{1,25},{9,1},{17,9},{25,17},{2,26},{10... | collective-permute-start | bytes 933896 | tf_op jit(solution)/shard_map/ppermute | solution.py:231
  92.5 7.4 %collective-permute-start.18 = (bf16[4,304,128]{2,1,0:T(8,128)(2,1)S(1)}, bf16[4,304,128]{2,1,0:T(8,128)(2,1)S(1)}, u32[]{:S(2)}, u32[]{:S(2)}) collective-permute-start(bf16[4,304,128]{2,1,0:T(8,128)(2,1)S(1)} %pad_maximum_fusion.1.refs_0_), channel_id=1, source_target_pairs={{0,16},{8,24},{16,0},{24,8},{1,17},{9,25},{17,1},{25,9},{2,18},{10... | collective-permute-start | bytes 933896 | tf_op jit(solution)/shard_map/ppermute | solution.py:231
  92.9 14.6 %collective-permute-start.17 = (bf16[4,304,128]{2,1,0:T(8,128)(2,1)S(1)}, bf16[4,304,128]{2,1,0:T(8,128)(2,1)S(1)}, u32[]{:S(2)}, u32[]{:S(2)}) collective-permute-start(bf16[4,304,128]{2,1,0:T(8,128)(2,1)S(1)} %pad_maximum_fusion.1.refs_0_), channel_id=1, source_target_pairs={{0,8},{8,16},{16,24},{24,0},{1,9},{9,17},{17,25},{25,1},{2,10},{10... | collective-permute-start | bytes 933896 | tf_op jit(solution)/shard_map/ppermute | solution.py:231

commit v9 on v8

v9 whole, which is shorter than its diff:
```python
import math

import jax
import jax.numpy as jnp
from jax import lax
from jax.experimental import pallas as pl
from jax.experimental.pallas import tpu as pltpu
from jax.sharding import Mesh
from jax.sharding import PartitionSpec as P

D = 7168
FF = 1024
TILE = 16
BLOCK = 128
UNIT = 16
BAND = 32

MOMENTUM_DECAY = 0.95
EPSILON = 1e-07
COEF_A = 3.4445
COEF_B = -4.775
COEF_C = 2.0315

DP = ("y", "core")
EXPERT = ("x", "z_pair", "z_low")

BF16 = jnp.bfloat16
F32 = jnp.float32


def split_two(value):
    high = value.astype(BF16)
    return high, (value - high.astype(F32)).astype(BF16)


def block_pairs():
    count = FF // BLOCK
    return [(i, j) for i in range(count) for j in range(i, count)]


def pieces_of(total, shape):
    first = total.astype(BF16).astype(F32)
    second = (total - first).astype(BF16).astype(F32)
    third = total - first - second
    rows = lax.broadcasted_iota(jnp.int32, shape, 0)
    tile = jnp.where(rows == 0, first, jnp.where(rows == 1, second, jnp.where(rows == 2, third, 0.0)))
    return tile.astype(BF16)


def fetched(sources, targets, semaphores):
    copies = [
        pltpu.make_async_copy(source, target, semaphores.at[at])
        for at, (source, target) in enumerate(zip(sources, targets))
    ]
    for copy in copies:
        copy.start()
    return copies


def pack_kernel(hidden_ref, tokens_ref, packed_ref, semaphores):
    width = hidden_ref.shape[1]
    bands = tokens_ref.shape[1] // BAND
    sources, targets = [hidden_ref], [packed_ref.at[:, :width]]
    for at in range(FF // BLOCK):
        sources.append(tokens_ref.at[:, pl.ds(at % bands * BAND, BAND)])
        targets.append(packed_ref.at[:, pl.ds(width, BAND), pl.ds(at * BLOCK, BLOCK)])
    for copy in fetched(sources, targets, semaphores):
        copy.wait()


def gram_kernel(place_ref, counts_ref, tiles_ref, momentum_ref, moment_ref, packed_ref):
    groups, height, _ = tiles_ref.shape
    width = height - BAND
    lanes = lax.broadcasted_iota(jnp.int32, (BAND, BLOCK), 1)
    bands = momentum_ref.shape[0] // BAND

    def band(g, at):
        kept = tiles_ref[g, width:, at * BLOCK : (at + 1) * BLOCK].astype(F32)
        return jnp.where(lanes < counts_ref[g] * TILE, kept, 0.0).astype(BF16)

    tokens = jnp.concatenate(
        [jnp.concatenate([band(g, at) for at in range(bands)], axis=0) for g in range(groups)], axis=1
    )
    hidden = tiles_ref[:, :width].reshape(groups * width, FF)
    gradient = jnp.dot(tokens, hidden, preferred_element_type=F32)
    moment = MOMENTUM_DECAY * momentum_ref[...] + gradient
    moment_ref[...] = moment

    high, low = split_two(moment)
    left = jnp.concatenate([high, low, high], axis=0).T
    right = jnp.concatenate([high, high, low], axis=0)
    chunks = packed_ref.shape[0]
    per_chunk = len(block_pairs()) // chunks
    at = 0
    for i in range(FF // BLOCK):
        strip = jnp.dot(
            left[i * BLOCK : (i + 1) * BLOCK], right[:, i * BLOCK :], preferred_element_type=F32
        ).astype(BF16)
        for j in range(i, FF // BLOCK):
            chunk, place = divmod(at, per_chunk)
            packed_ref[
                lax.rem(chunk - place_ref[0] + chunks, chunks), place * BLOCK : (place + 1) * BLOCK, :
            ] = strip[:, (j - i) * BLOCK : (j - i + 1) * BLOCK]
            at += 1

    total = jnp.sum(jnp.sum(moment * moment, axis=0, keepdims=True), axis=1, keepdims=True)
    for chunk in range(chunks):
        packed_ref[chunk, per_chunk * BLOCK :, :] = pieces_of(total, (UNIT, BLOCK))


def middle_kernel(place_ref, *refs):
    *part_refs, cut_ref = refs
    pairs, height, _ = cut_ref.shape
    rows = height - UNIT
    total = part_refs[0][...].astype(F32)
    for part_ref in part_refs[1:]:
        total = total + part_ref[...].astype(F32)
    tile = pieces_of(jnp.sum(total[pairs * rows :, 0:1], axis=0, keepdims=True), (UNIT, BLOCK))
    for pair in range(pairs):
        at = lax.rem(pair - place_ref[1] + pairs, pairs)
        cut_ref[at, :rows] = total[pair * rows : (pair + 1) * rows].astype(BF16)
        cut_ref[at, rows:] = tile


def sum_kernel(*refs):
    *part_refs, sum_ref = refs
    total = part_refs[0][...].astype(F32)
    for part_ref in part_refs[1:]:
        total = total + part_ref[...].astype(F32)
    rows = total.shape[0] - UNIT
    sum_ref[:rows] = total[:rows].astype(BF16)
    squares = jnp.sum(total[rows:, 0:1], axis=0, keepdims=True)
    sum_ref[rows:] = pieces_of(squares, (UNIT, BLOCK))


def polynomial_kernel(place_ref, moment_away_ref, *refs):
    *chunk_refs, update_ref, packed_ref, gram_ref, moment_ref, semaphores = refs
    copies = fetched([moment_away_ref], [moment_ref], semaphores)
    chunks = len(chunk_refs)
    pieces, height, _ = chunk_refs[0].shape
    rows = height - UNIT
    squares = jnp.sum(chunk_refs[0][0, rows:].astype(F32)[:, 0:1], axis=0, keepdims=True)
    for distance, chunk_ref in enumerate(chunk_refs):
        source = lax.rem(place_ref[0] - distance + chunks, chunks)
        for piece in range(pieces):
            start = lax.rem(place_ref[1] - piece + pieces, pieces) * rows
            packed_ref[source, pl.ds(pl.multiple_of(start, UNIT), rows)] = chunk_ref[piece, :rows]
    factor = 1.0 / (jnp.sqrt(squares) + EPSILON)
    per_chunk = len(block_pairs()) // chunks
    for source in range(chunks):
        for at, (i, j) in enumerate(block_pairs()[source * per_chunk : (source + 1) * per_chunk]):
            block = packed_ref[source, at * BLOCK : (at + 1) * BLOCK]
            gram_ref[i * BLOCK : (i + 1) * BLOCK, j * BLOCK : (j + 1) * BLOCK] = block
            if i != j:
                gram_ref[j * BLOCK : (j + 1) * BLOCK, i * BLOCK : (i + 1) * BLOCK] = block.T

    def by_gram(value):
        rows = value.shape[0]
        both = jnp.dot(
            jnp.concatenate(split_two(value), axis=0), gram_ref[...], preferred_element_type=F32
        )
        return both[:rows] + both[rows:]

    square = factor * factor
    linear, cubic = COEF_B * square, COEF_C * square * square

    def by_first(value):
        return COEF_A * value + by_gram(linear * value + cubic * by_gram(value))

    def by_second_gram(value):
        return by_first(by_gram(by_first(value)))

    copies[0].wait()
    once = by_first(moment_ref[...] * factor)
    twice = COEF_A * once + by_second_gram(linear * once + cubic * by_second_gram(once))
    update_ref[...] = twice * math.sqrt(max(FF, D))


def whole(memory_space=pltpu.VMEM):
    return pl.BlockSpec(memory_space=memory_space)


MIB = 1024 * 1024


def call(kernel, out_shape, inputs, scratch=(), scalars=0, away=(), mib=8):
    return pl.pallas_call(
        kernel,
        out_shape=out_shape,
        in_specs=[
            whole(pltpu.SMEM if at < scalars else pltpu.HBM if at in away else pltpu.VMEM)
            for at in range(len(inputs))
        ],
        out_specs=jax.tree.map(lambda _: whole(), out_shape),
        scratch_shapes=scratch,
        compiler_params=pltpu.CompilerParams(vmem_limit_bytes=mib * MIB),
        name=kernel.__name__.removesuffix("_kernel"),
    )(*inputs)


def shifted(value, axis, distance):
    size = lax.axis_size(axis)
    return lax.ppermute(value, axis, [(i, (i + distance) % size) for i in range(size)])


def body(hidden_token_tiles, gradient_token_tiles, momentum, filled_tile_count):
    along_x, pairs = lax.axis_size("x"), lax.axis_size("z_pair")
    rows = momentum.shape[1]
    chunk = len(block_pairs()) * BLOCK // along_x
    piece = chunk // pairs
    experts, width, _ = hidden_token_tiles.shape
    counts = lax.dynamic_index_in_dim(filled_tile_count, lax.axis_index(DP), 1, keepdims=False)
    place = jnp.stack([lax.axis_index("x"), lax.axis_index("z_pair")]).astype(jnp.int32)

    packed = pl.pallas_call(
        pack_kernel,
        out_shape=jax.ShapeDtypeStruct((experts, width + BAND, FF), BF16),
        in_specs=[whole(pltpu.HBM), whole(pltpu.HBM)],
        out_specs=whole(pltpu.HBM),
        scratch_shapes=[pltpu.SemaphoreType.DMA((1 + FF // BLOCK,))],
        name="pack",
    )(*(pltpu.with_memory_space_constraint(value, pltpu.HBM) for value in (hidden_token_tiles, gradient_token_tiles)))
    tiles = lax.all_to_all(packed, DP, 0, 0, tiled=True)
    moment, parts = call(
        gram_kernel,
        (
            jax.ShapeDtypeStruct((rows, FF), F32),
            jax.ShapeDtypeStruct((along_x, chunk + UNIT, BLOCK), BF16),
        ),
        [place, counts, tiles, momentum[0]],
        scalars=2,
        mib=28,
    )
    parts = call(
        middle_kernel,
        jax.ShapeDtypeStruct((pairs, piece + UNIT, BLOCK), BF16),
        [place, parts[0]] + [shifted(parts[k], "x", k) for k in range(1, along_x)],
        scalars=1,
    )
    summed = jax.ShapeDtypeStruct((piece + UNIT, BLOCK), BF16)
    part = call(sum_kernel, summed, [parts[0]] + [shifted(parts[k], "z_pair", k) for k in range(1, pairs)])
    part = call(sum_kernel, summed, [part, shifted(part, "z_low", 1)])
    own = jnp.stack([part] + [shifted(part, "z_pair", k) for k in range(1, pairs)])
    update = call(
        polynomial_kernel,
        jax.ShapeDtypeStruct((rows, FF), F32),
        [place, pltpu.with_memory_space_constraint(moment, pltpu.HBM), own] + [shifted(own, "x", k) for k in range(1, along_x)],
        scratch=[
            pltpu.VMEM((along_x, pairs * piece, BLOCK), BF16),
            pltpu.VMEM((FF, FF), BF16),
            pltpu.VMEM((rows, FF), F32),
            pltpu.SemaphoreType.DMA((1,)),
        ],
        away=(1,),
        scalars=1,
        mib=20,
    )
    gathered = lax.all_gather((update * 256.0).astype(jnp.float16), DP, axis=0, tiled=False)
    return (moment[None], gathered.astype(F32) * (1.0 / 256.0))


def solution(mesh):
    split = Mesh(mesh.devices.reshape(4, 2, 4, 4, 2), ("y", "core", "x", "z_pair", "z_low"))
    placed = (P(None, DP, None), P(None, EXPERT, DP), P(DP, EXPERT, None), P())
    return jax.shard_map(
        body,
        mesh=split,
        in_specs=placed,
        out_specs=(P(DP, EXPERT, None), P(None, EXPERT, None)),
        check_vma=False,
    )
```

time: 148 us -> 230 us (1.55)
  Pallas kernels: 22.5 us -> 98.5 us
  waiting for transfers between devices: 57.2 us -> 73.7 us
  starting transfers between devices: 37.6 us -> 29.9 us
  local copies, waits for them, and re-layouts: 2.99 us -> 0.3 us
    pallas_call x0 -> x1, Pallas kernels: none -> 80.6 us  [body(): pl.pallas_call(pack_kernel, out_shape=jax.ShapeDtypeStruct((experts, widt...]
    all_to_all x1, waiting for transfers between devices: 0.01 us -> 31.7 us  [body(): tiles = lax.all_to_all(packed, DP, 0, 0, tiled=True)]
    ppermute x20 -> x13, waiting for transfers between devices: 57.2 us -> 42 us  [shifted(): lax.ppermute(value, axis, [(i, (i + distance) % size) for i in range(size)])]
    ppermute x20 -> x13, starting transfers between devices: 31.9 us -> 23 us  [shifted(): lax.ppermute(value, axis, [(i, (i + distance) % size) for i in range(size)])]
    pallas_call x5, Pallas kernels: 22.5 us -> 17.9 us  [call(): pl.pallas_call(kernel, out_shape=out_shape, in_specs=[whole(pltpu.SMEM if...]
    unnamed x12 -> x4, local copies, waits for them, and re-layouts: 2.96 us -> 0.02 us
  transfers between devices with their start and end apart: 21 -> 14, of which waited for: 12 -> 13; matrix products, arithmetic and copies ran while one was open for 0% -> 0% of each run, Pallas kernels for 0% -> 0%
where the time goes in v9:
time: 230 us; the launch traced here: 229 us
  Pallas kernels  98.5 us (43%)
  waiting for transfers between devices  73.7 us (32%)
  starting transfers between devices  29.9 us (13%)
  blocking collectives  21.2 us (9%)
  other arithmetic  4.26 us (2%)
    pallas_call x1, Pallas kernels, body(): pl.pallas_call(pack_kernel, out_shape=jax.ShapeDtypeStruct((experts, widt...  80.6 us
    ppermute x13, waiting for transfers between devices, shifted(): lax.ppermute(value, axis, [(i, (i + distance) % size) for i in range(size)])  42 us
    all_to_all x1, waiting for transfers between devices, body(): tiles = lax.all_to_all(packed, DP, 0, 0, tiled=True)  31.7 us
    ppermute x13, starting transfers between devices, shifted(): lax.ppermute(value, axis, [(i, (i + distance) % size) for i in range(size)])  23 us
    all_gather x1, blocking collectives, body(): lax.all_gather((update * 256.0).astype(jnp.float16), DP, axis=0, tiled=Fa...  21.2 us
    pallas_call x5, Pallas kernels, call(): pl.pallas_call(kernel, out_shape=out_shape, in_specs=[whole(pltpu.SMEM if...  17.9 us
    all_to_all x1, starting transfers between devices, body(): tiles = lax.all_to_all(packed, DP, 0, 0, tiled=True)  6.91 us
  transfers between devices with their start and end apart: 14, of which 13 were waited for; matrix products, arithmetic and copies ran while one was open for 0% of the time, Pallas kernels for 0%

profile of v9, /device:TPU:1, one launch (start us, length us, event | category | flops | bytes accessed | tf_op | source)
XLA Modules:
  0.0 228.6 jit_solution(5141743915309575520)
XLA Ops:
  0.6 80.6 %pack.1 = bf16[8,160,1024]{2,1,0:T(8,128)(2,1)} custom-call(bf16[8,128,1024]{2,1,0:T(8,128)(2,1)} %hidden_ref.1, bf16[8,224,128]{2,1,0:T(8,128)(2,1)} %tokens_ref.1), custom_call_target="tpu_custom_call" | custom-call | tf_op jit(solution)/shard_map/pack/pallas_call | solution.py:215
  81.3 6.9 %all-to-all-start = ((bf16[8,160,1024]{2,1,0:T(8,128)(2,1)}), bf16[8,160,1024]{2,1,0:T(8,128)(2,1)S(1)}, u32[]{:S(2)}, u32[]{:S(2)}) async-start(bf16[8,160,1024]{2,1,0:T(8,128)(2,1)} %pack.1), calls=%async_computation | async-start | bytes 5242880 | tf_op jit(solution)/shard_map/all_to_all | solution.py:223
  88.4 31.7 %all-to-all-done.tiles_ref = bf16[8,160,1024]{2,1,0:T(8,128)(2,1)S(1)} async-done(((bf16[8,160,1024]{2,1,0:T(8,128)(2,1)}), bf16[8,160,1024]{2,1,0:T(8,128)(2,1)S(1)}, u32[]{:S(2)}, u32[]{:S(2)}) %all-to-all-start) | async-done | bytes 2621472 | tf_op jit(solution)/shard_map/all_to_all | solution.py:223
  120.1 3.1 %gram.1 = (f32[224,1024]{1,0:T(8,128)}, bf16[4,1168,128]{2,1,0:T(8,128)(2,1)S(1)}) custom-call(s32[2]{0:T(128)S(1)} %pad_add_fusion.place_ref, s32[8]{0:T(128)S(1)} %dynamic-slice_reduce_fusion.counts_ref, bf16[8,160,1024]{2,1,0:T(8,128)(2,1)S(1)} %all-to-all-done.tiles_ref, f32[224,1024]{1,0:T(8,128)S(1)} %bitcast.25), custom_call_target="tpu_custom_call" | custom-call | tf_op jit(solution)/shard_map/gram/pallas_call | solution.py:187
  123.3 1.7 collective-permute-start.2
  125.0 0.5 collective-permute-start.1
  125.6 0.6 collective-permute-start
  126.2 5.0 %collective-permute-done.2.refs_3_ = bf16[1168,128]{1,0:T(8,128)(2,1)S(1)} collective-permute-done((bf16[1168,128]{1,0:T(8,128)(2,1)S(1)}, bf16[1168,128]{1,0:T(8,128)(2,1)S(1)}, u32[]{:S(2)}, u32[]{:S(2)}) %collective-permute-start.2) | collective-permute-done | bytes 299040 | tf_op jit(solution)/shard_map/ppermute | solution.py:203
  131.1 2.9 %collective-permute-done.1.refs_2_ = bf16[1168,128]{1,0:T(8,128)(2,1)S(1)} collective-permute-done((bf16[1168,128]{1,0:T(8,128)(2,1)S(1)}, bf16[1168,128]{1,0:T(8,128)(2,1)S(1)}, u32[]{:S(2)}, u32[]{:S(2)}) %collective-permute-start.1) | collective-permute-done | bytes 299040 | tf_op jit(solution)/shard_map/ppermute | solution.py:203
  134.0 7.9 %collective-permute-done.refs_1_ = bf16[1168,128]{1,0:T(8,128)(2,1)S(1)} collective-permute-done((bf16[1168,128]{1,0:T(8,128)(2,1)S(1)}, bf16[1168,128]{1,0:T(8,128)(2,1)S(1)}, u32[]{:S(2)}, u32[]{:S(2)}) %collective-permute-start) | collective-permute-done | bytes 299040 | tf_op jit(solution)/shard_map/ppermute | solution.py:203
  142.0 0.8 middle.1
  142.9 6.1 %collective-permute-start.5 = (bf16[304,128]{1,0:T(8,128)(2,1)S(1)}, bf16[304,128]{1,0:T(8,128)(2,1)S(1)}, u32[]{:S(2)}, u32[]{:S(2)}) collective-permute-start(bf16[304,128]{1,0:T(8,128)(2,1)S(1)} %get-tuple-element.10), channel_id=1, source_target_pairs={{0,6},{2,0},{4,2},{6,4},{1,7},{3,1},{5,3},{7,5},{8,14},{10,8},{12,... | collective-permute-start | bytes 233480 | tf_op jit(solution)/shard_map/ppermute | solution.py:203
  149.0 1.0 collective-permute-start.4
  149.9 2.3 collective-permute-start.3
  152.2 3.2 %collective-permute-done.5.refs_3_ = bf16[304,128]{1,0:T(8,128)(2,1)S(1)} collective-permute-done((bf16[304,128]{1,0:T(8,128)(2,1)S(1)}, bf16[304,128]{1,0:T(8,128)(2,1)S(1)}, u32[]{:S(2)}, u32[]{:S(2)}) %collective-permute-start.5) | collective-permute-done | bytes 77856 | tf_op jit(solution)/shard_map/ppermute | solution.py:203
  155.4 0.9 collective-permute-done.4.refs_2_
  156.3 1.0 collective-permute-done.3.refs_1_
  157.4 1.9 collective-permute-start.6
  159.3 1.8 collective-permute-done.6.refs_1_
  161.1 2.9 %collective-permute-start.9 = (bf16[304,128]{1,0:T(8,128)(2,1)S(1)}, bf16[304,128]{1,0:T(8,128)(2,1)S(1)}, u32[]{:S(2)}, u32[]{:S(2)}) collective-permute-start(bf16[304,128]{1,0:T(8,128)(2,1)S(1)} %sum.3), channel_id=1, source_target_pairs={{0,6},{2,0},{4,2},{6,4},{1,7},{3,1},{5,3},{7,5},{8,14},{10,8},{12,... | collective-permute-start | bytes 233480 | tf_op jit(solution)/shard_map/ppermute | solution.py:203
  164.0 2.5 %collective-permute-start.8 = (bf16[304,128]{1,0:T(8,128)(2,1)S(1)}, bf16[304,128]{1,0:T(8,128)(2,1)S(1)}, u32[]{:S(2)}, u32[]{:S(2)}) collective-permute-start(bf16[304,128]{1,0:T(8,128)(2,1)S(1)} %sum.3), channel_id=1, source_target_pairs={{0,4},{2,6},{4,0},{6,2},{1,5},{3,7},{5,1},{7,3},{8,12},{10,14},{12... | collective-permute-start | bytes 233480 | tf_op jit(solution)/shard_map/ppermute | solution.py:203
  166.5 2.1 collective-permute-start.7
  168.6 2.7 %collective-permute-done.8 = bf16[304,128]{1,0:T(8,128)(2,1)S(1)} collective-permute-done((bf16[304,128]{1,0:T(8,128)(2,1)S(1)}, bf16[304,128]{1,0:T(8,128)(2,1)S(1)}, u32[]{:S(2)}, u32[]{:S(2)}) %collective-permute-start.8) | collective-permute-done | bytes 77856 | tf_op jit(solution)/shard_map/ppermute | solution.py:203
  171.3 1.7 collective-permute-done.7
  173.1 0.6 collective-permute-start.11
  173.7 0.9 collective-permute-start.10
  174.6 4.3 %collective-permute-done.12.refs_3_ = bf16[4,304,128]{2,1,0:T(8,128)(2,1)S(1)} collective-permute-done((bf16[4,304,128]{2,1,0:T(8,128)(2,1)S(1)}, bf16[4,304,128]{2,1,0:T(8,128)(2,1)S(1)}, u32[]{:S(2)}, u32[]{:S(2)}) %collective-permute-start.12) | collective-permute-done | bytes 311328 | tf_op jit(solution)/shard_map/ppermute | solution.py:203
  178.9 1.7 collective-permute-done.11.refs_2_
  180.6 8.9 %collective-permute-done.10.refs_1_ = bf16[4,304,128]{2,1,0:T(8,128)(2,1)S(1)} collective-permute-done((bf16[4,304,128]{2,1,0:T(8,128)(2,1)S(1)}, bf16[4,304,128]{2,1,0:T(8,128)(2,1)S(1)}, u32[]{:S(2)}, u32[]{:S(2)}) %collective-permute-start.10) | collective-permute-done | bytes 311328 | tf_op jit(solution)/shard_map/ppermute | solution.py:203
  189.4 13.8 %polynomial.1 = f32[224,1024]{1,0:T(8,128)S(1)} custom-call(s32[2]{0:T(128)S(1)} %pad_add_fusion.place_ref, f32[224,1024]{1,0:T(8,128)} %get-tuple-element.4.moment_away_ref, bf16[4,304,128]{2,1,0:T(8,128)(2,1)S(1)} %pad_maximum_fusion.refs_0_, bf16[4,304,128]{2,1,0:T(8,128)(2,1)S(1)} %collective-permute-done.10.refs_1_, ...), custom_call_target="tpu_custom_call" | custom-call | tf_op jit(solution)/shard_map/polynomial/pallas_call | solution.py:187
  203.4 21.2 %all-gather.2 = f16[1792,1024]{1,0:T(8,128)(2,1)S(1)} all-gather(f16[224,1024]{1,0:T(8,128)(2,1)S(1)} %multiply_convert_fusion), channel_id=2, replica_groups=mesh['y'=4,'core'=2,'x'=4,'z_pair'=4,'z_low'=2] {'y','core'}, dimensions={0}, use_global_device_ids=true | all-gather | bytes 4128768 | tf_op jit(solution)/shard_map/all_gather | solution.py:258
  224.5 4.1 %convert_multiply_fusion = f32[1792,1024]{1,0:T(8,128)} fusion(f16[1792,1024]{1,0:T(8,128)(2,1)S(1)} %all-gather.2), kind=kLoop, calls=%fused_computation | loop fusion | flops 3670016 | bytes 11010048 | tf_op jit(solution)/shard_map/mul | solution.py:259
  (14 shorter events, 0.8 us)
Async XLA Ops:
  0.6 87.5 %copy-start = (s32[8,8]{1,0:T(8,128)S(1)}, s32[8,8]{1,0:T(8,128)}, u32[]{:S(2)}) copy-start(s32[8,8]{1,0:T(8,128)} %param.7) | copy-start | bytes 772
  81.2 38.9 %copy-start.1 = (f32[1,224,1024]{2,1,0:T(8,128)S(1)}, f32[1,224,1024]{2,1,0:T(8,128)}, u32[]{:S(2)}) copy-start(f32[1,224,1024]{2,1,0:T(8,128)} %param.6) | copy-start | bytes 2752516
  81.3 38.9 %all-to-all-start = ((bf16[8,160,1024]{2,1,0:T(8,128)(2,1)}), bf16[8,160,1024]{2,1,0:T(8,128)(2,1)S(1)}, u32[]{:S(2)}, u32[]{:S(2)}) async-start(bf16[8,160,1024]{2,1,0:T(8,128)(2,1)} %pack.1), calls=%async_computation | async-start | bytes 5242880 | tf_op jit(solution)/shard_map/all_to_all | solution.py:223
  123.3 7.8 %collective-permute-start.2 = (bf16[1168,128]{1,0:T(8,128)(2,1)S(1)}, bf16[1168,128]{1,0:T(8,128)(2,1)S(1)}, u32[]{:S(2)}, u32[]{:S(2)}) collective-permute-start(bf16[1168,128]{1,0:T(8,128)(2,1)S(1)} %get-tuple-element.6), channel_id=1, source_target_pairs={{0,24},{8,0},{16,8},{24,16},{1,25},{9,1},{17,9},{25,17},{2,26},{10... | collective-permute-start | bytes 897032 | tf_op jit(solution)/shard_map/ppermute | solution.py:203
  125.0 9.0 %collective-permute-start.1 = (bf16[1168,128]{1,0:T(8,128)(2,1)S(1)}, bf16[1168,128]{1,0:T(8,128)(2,1)S(1)}, u32[]{:S(2)}, u32[]{:S(2)}) collective-permute-start(bf16[1168,128]{1,0:T(8,128)(2,1)S(1)} %get-tuple-element.7), channel_id=1, source_target_pairs={{0,16},{8,24},{16,0},{24,8},{1,17},{9,25},{17,1},{25,9},{2,18},{10... | collective-permute-start | bytes 897032 | tf_op jit(solution)/shard_map/ppermute | solution.py:203
  125.6 16.4 %collective-permute-start = (bf16[1168,128]{1,0:T(8,128)(2,1)S(1)}, bf16[1168,128]{1,0:T(8,128)(2,1)S(1)}, u32[]{:S(2)}, u32[]{:S(2)}) collective-permute-start(bf16[1168,128]{1,0:T(8,128)(2,1)S(1)} %get-tuple-element.8), channel_id=1, source_target_pairs={{0,8},{8,16},{16,24},{24,0},{1,9},{9,17},{17,25},{25,1},{2,10},{10... | collective-permute-start | bytes 897032 | tf_op jit(solution)/shard_map/ppermute | solution.py:203
  142.9 12.6 %collective-permute-start.5 = (bf16[304,128]{1,0:T(8,128)(2,1)S(1)}, bf16[304,128]{1,0:T(8,128)(2,1)S(1)}, u32[]{:S(2)}, u32[]{:S(2)}) collective-permute-start(bf16[304,128]{1,0:T(8,128)(2,1)S(1)} %get-tuple-element.10), channel_id=1, source_target_pairs={{0,6},{2,0},{4,2},{6,4},{1,7},{3,1},{5,3},{7,5},{8,14},{10,8},{12,... | collective-permute-start | bytes 233480 | tf_op jit(solution)/shard_map/ppermute | solution.py:203
  149.0 7.4 %collective-permute-start.4 = (bf16[304,128]{1,0:T(8,128)(2,1)S(1)}, bf16[304,128]{1,0:T(8,128)(2,1)S(1)}, u32[]{:S(2)}, u32[]{:S(2)}) collective-permute-start(bf16[304,128]{1,0:T(8,128)(2,1)S(1)} %get-tuple-element.11), channel_id=1, source_target_pairs={{0,4},{2,6},{4,0},{6,2},{1,5},{3,7},{5,1},{7,3},{8,12},{10,14},{12... | collective-permute-start | bytes 233480 | tf_op jit(solution)/shard_map/ppermute | solution.py:203
  149.9 7.4 %collective-permute-start.3 = (bf16[304,128]{1,0:T(8,128)(2,1)S(1)}, bf16[304,128]{1,0:T(8,128)(2,1)S(1)}, u32[]{:S(2)}, u32[]{:S(2)}) collective-permute-start(bf16[304,128]{1,0:T(8,128)(2,1)S(1)} %get-tuple-element.12), channel_id=1, source_target_pairs={{0,2},{2,4},{4,6},{6,0},{1,3},{3,5},{5,7},{7,1},{8,10},{10,12},{12... | collective-permute-start | bytes 233480 | tf_op jit(solution)/shard_map/ppermute | solution.py:203
  157.4 3.6 %collective-permute-start.6 = (bf16[304,128]{1,0:T(8,128)(2,1)S(1)}, bf16[304,128]{1,0:T(8,128)(2,1)S(1)}, u32[]{:S(2)}, u32[]{:S(2)}) collective-permute-start(bf16[304,128]{1,0:T(8,128)(2,1)S(1)} %sum.2.refs_0_), channel_id=1, source_target_pairs={{0,1},{1,0},{2,3},{3,2},{4,5},{5,4},{6,7},{7,6},{8,9},{9,8},{10,11... | collective-permute-start | bytes 233480 | tf_op jit(solution)/shard_map/ppermute | solution.py:203
  161.1 7.4 %collective-permute-start.9 = (bf16[304,128]{1,0:T(8,128)(2,1)S(1)}, bf16[304,128]{1,0:T(8,128)(2,1)S(1)}, u32[]{:S(2)}, u32[]{:S(2)}) collective-permute-start(bf16[304,128]{1,0:T(8,128)(2,1)S(1)} %sum.3), channel_id=1, source_target_pairs={{0,6},{2,0},{4,2},{6,4},{1,7},{3,1},{5,3},{7,5},{8,14},{10,8},{12,... | collective-permute-start | bytes 233480 | tf_op jit(solution)/shard_map/ppermute | solution.py:203
  164.0 7.2 %collective-permute-start.8 = (bf16[304,128]{1,0:T(8,128)(2,1)S(1)}, bf16[304,128]{1,0:T(8,128)(2,1)S(1)}, u32[]{:S(2)}, u32[]{:S(2)}) collective-permute-start(bf16[304,128]{1,0:T(8,128)(2,1)S(1)} %sum.3), channel_id=1, source_target_pairs={{0,4},{2,6},{4,0},{6,2},{1,5},{3,7},{5,1},{7,3},{8,12},{10,14},{12... | collective-permute-start | bytes 233480 | tf_op jit(solution)/shard_map/ppermute | solution.py:203
  166.5 6.5 %collective-permute-start.7 = (bf16[304,128]{1,0:T(8,128)(2,1)S(1)}, bf16[304,128]{1,0:T(8,128)(2,1)S(1)}, u32[]{:S(2)}, u32[]{:S(2)}) collective-permute-start(bf16[304,128]{1,0:T(8,128)(2,1)S(1)} %sum.3), channel_id=1, source_target_pairs={{0,2},{2,4},{4,6},{6,0},{1,3},{3,5},{5,7},{7,1},{8,10},{10,12},{12... | collective-permute-start | bytes 233480 | tf_op jit(solution)/shard_map/ppermute | solution.py:203
  173.0 5.8 %collective-permute-start.12 = (bf16[4,304,128]{2,1,0:T(8,128)(2,1)S(1)}, bf16[4,304,128]{2,1,0:T(8,128)(2,1)S(1)}, u32[]{:S(2)}, u32[]{:S(2)}) collective-permute-start(bf16[4,304,128]{2,1,0:T(8,128)(2,1)S(1)} %pad_maximum_fusion.refs_0_), channel_id=1, source_target_pairs={{0,24},{8,0},{16,8},{24,16},{1,25},{9,1},{17,9},{25,17},{2,26},{10... | collective-permute-start | bytes 933896 | tf_op jit(solution)/shard_map/ppermute | solution.py:203
  173.1 7.4 %collective-permute-start.11 = (bf16[4,304,128]{2,1,0:T(8,128)(2,1)S(1)}, bf16[4,304,128]{2,1,0:T(8,128)(2,1)S(1)}, u32[]{:S(2)}, u32[]{:S(2)}) collective-permute-start(bf16[4,304,128]{2,1,0:T(8,128)(2,1)S(1)} %pad_maximum_fusion.refs_0_), channel_id=1, source_target_pairs={{0,16},{8,24},{16,0},{24,8},{1,17},{9,25},{17,1},{25,9},{2,18},{10... | collective-permute-start | bytes 933896 | tf_op jit(solution)/shard_map/ppermute | solution.py:203
  173.7 15.7 %collective-permute-start.10 = (bf16[4,304,128]{2,1,0:T(8,128)(2,1)S(1)}, bf16[4,304,128]{2,1,0:T(8,128)(2,1)S(1)}, u32[]{:S(2)}, u32[]{:S(2)}) collective-permute-start(bf16[4,304,128]{2,1,0:T(8,128)(2,1)S(1)} %pad_maximum_fusion.refs_0_), channel_id=1, source_target_pairs={{0,8},{8,16},{16,24},{24,0},{1,9},{9,17},{17,25},{25,1},{2,10},{10... | collective-permute-start | bytes 933896 | tf_op jit(solution)/shard_map/ppermute | solution.py:203

commit v10 on v7

--- a/solution.py
+++ b/solution.py
@@ -52,23 +52,26 @@
     return pl.ds(pl.multiple_of(lax.rem(2 * place + block, FF // BLOCK) * BLOCK, BLOCK), BLOCK)
 
 
-def outgoing_kernel(place_ref, group_ref, momentum_away_ref, tokens_ref, *refs):
-    *column_refs, kept_ref, sent_ref, momentum_ref, semaphores = refs
+def tiles_kernel(group_ref, tokens_ref, kept_ref, sent_ref, semaphores):
     chip, core = lax.div(group_ref[0], CORES), lax.rem(group_ref[0], CORES)
     chips = kept_ref.shape[0]
-    sources, targets = [momentum_away_ref], [momentum_ref]
+    sources, targets = [], []
     for distance in range(chips):
         first = lax.rem(chip + distance, chips) * CORES
-        sources += [tokens_ref.at[first + core], tokens_ref.at[first + 1 - core]]
-        targets += [kept_ref.at[distance], sent_ref.at[distance]]
-    copies = fetched(sources, targets, semaphores)
-    copies[0].wait()
+        sources += [tokens_ref.at[first + 1 - core], tokens_ref.at[first + core]]
+        targets += [sent_ref.at[distance], kept_ref.at[distance]]
+    for copy in fetched(sources, targets, semaphores):
+        copy.wait()
+
+
+def columns_kernel(place_ref, momentum_away_ref, *refs):
+    *column_refs, momentum_ref, semaphores = refs
+    for copy in fetched([momentum_away_ref], [momentum_ref], semaphores):
+        copy.wait()
     for distance, column_ref in enumerate(column_refs, 1):
         for block in range(NEEDED):
             value = momentum_ref[:, column(place_ref[0] + distance, block)]
             column_ref[:, block * BLOCK : (block + 1) * BLOCK] = value.astype(BF16)
-    for copy in copies[1:]:
-        copy.wait()
 
 
 def fetched(sources, targets, semaphores):
@@ -236,14 +239,21 @@
     along_y = lax.axis_size("y")
 
     half = jax.ShapeDtypeStruct((along_y, *gradient_token_tiles.shape[1:]), BF16)
-    *columns, kept, sent = call(
-        outgoing_kernel,
-        [jax.ShapeDtypeStruct((rows, NEEDED * BLOCK), BF16) for _ in distances] + [half, half],
-        [place, group]
-        + [pltpu.with_memory_space_constraint(value, pltpu.HBM) for value in (momentum[0], gradient_token_tiles)],
-        scratch=[pltpu.VMEM((rows, FF), F32), pltpu.SemaphoreType.DMA((1 + CORES * along_y,))],
-        away=(2, 3),
-        scalars=2,
+    kept, sent = call(
+        tiles_kernel,
+        [half, half],
+        [group, pltpu.with_memory_space_constraint(gradient_token_tiles, pltpu.HBM)],
+        scratch=[pltpu.SemaphoreType.DMA((CORES * along_y,))],
+        away=(1,),
+        scalars=1,
+    )
+    columns = call(
+        columns_kernel,
+        [jax.ShapeDtypeStruct((rows, NEEDED * BLOCK), BF16) for _ in distances],
+        [place, pltpu.with_memory_space_constraint(momentum[0], pltpu.HBM)],
+        scratch=[pltpu.VMEM((rows, FF), F32), pltpu.SemaphoreType.DMA((1,))],
+        away=(1,),
+        scalars=1,
     )
     other_columns = [shifted(columns[k - 1], "x", k) for k in distances]
     both = jnp.stack([kept, shifted(sent, "core", 1)], axis=1)

time: 147 us -> 148 us (level)
    pallas_call x5 -> x6, Pallas kernels: 22.5 us -> 23.5 us  [call(): pl.pallas_call(kernel, out_shape=out_shape, in_specs=[whole(pltpu.SMEM if...]
  transfers between devices with their start and end apart: 21 -> 21, of which waited for: 12 -> 12; matrix products, arithmetic and copies ran while one was open for 0% -> 0% of each run, Pallas kernels for 0% -> 1%
where the time goes in v10:
time: 148 us
  waiting for transfers between devices  57.2 us (39%)
  starting transfers between devices  37.6 us (25%)
  Pallas kernels  23.5 us (16%)
  blocking collectives  22.8 us (15%)
  other arithmetic  4.36 us (3%)
  local copies, waits for them, and re-layouts  1.84 us (1%)
    ppermute x20, waiting for transfers between devices, shifted(): lax.ppermute(value, axis, [(i, (i + distance) % size) for i in range(size)])  57.2 us
    ppermute x20, starting transfers between devices, shifted(): lax.ppermute(value, axis, [(i, (i + distance) % size) for i in range(size)])  32 us
    pallas_call x6, Pallas kernels, call(): pl.pallas_call(kernel, out_shape=out_shape, in_specs=[whole(pltpu.SMEM if...  23.5 us
    all_gather x1, blocking collectives, body(): lax.all_gather((update * 256.0).astype(jnp.float16), DP, axis=0, tiled=Fa...  22.8 us
    all_to_all x1, starting transfers between devices, body(): hidden = lax.all_to_all(hidden_token_tiles, DP, 0, 0, tiled=True)  5.67 us
    mul x1, other arithmetic, body(): return (moment[None], gathered.astype(F32) * (1.0 / 256.0))  4.07 us
  transfers between devices with their start and end apart: 21, of which 12 were waited for; matrix products, arithmetic and copies ran while one was open for 0% of the time, Pallas kernels for 1%

profile of v10, /device:TPU:1, one launch (start us, length us, event | category | flops | bytes accessed | tf_op | source)
XLA Modules:
  0.0 148.1 jit_solution(9206169585172512817)
XLA Ops:
  0.7 1.1 tiles.1
  1.8 3.3 %collective-permute-start = (bf16[4,224,128]{2,1,0:T(8,128)(2,1)S(1)}, bf16[4,224,128]{2,1,0:T(8,128)(2,1)S(1)}, u32[]{:S(2)}, u32[]{:S(2)}) collective-permute-start(bf16[4,224,128]{2,1,0:T(8,128)(2,1)S(1)} %get-tuple-element.16), channel_id=1, source_target_pairs={{0,32},{32,0},{1,33},{33,1},{2,34},{34,2},{3,35},{35,3},{4,36},{36... | collective-permute-start | bytes 688136 | tf_op jit(solution)/shard_map/ppermute | solution.py:227
  5.2 2.0 %columns.1 = (bf16[224,768]{1,0:T(8,128)(2,1)S(1)}, bf16[224,768]{1,0:T(8,128)(2,1)S(1)}, bf16[224,768]{1,0:T(8,128)(2,1)S(1)}) custom-call(s32[2]{0:T(128)S(1)} %pad_add_fusion.place_ref, f32[224,1024]{1,0:T(8,128)} %bitcast.31), custom_call_target="tpu_custom_call" | custom-call | tf_op jit(solution)/shard_map/columns/pallas_call | solution.py:211
  7.3 2.7 %collective-permute-start.5 = (bf16[224,768]{1,0:T(8,128)(2,1)S(1)}, bf16[224,768]{1,0:T(8,128)(2,1)S(1)}, u32[]{:S(2)}, u32[]{:S(2)}) collective-permute-start(bf16[224,768]{1,0:T(8,128)(2,1)S(1)} %get-tuple-element.18), channel_id=1, source_target_pairs={{0,24},{8,0},{16,8},{24,16},{1,25},{9,1},{17,9},{25,17},{2,26},{10... | collective-permute-start | bytes 1032200 | tf_op jit(solution)/shard_map/ppermute | solution.py:227
  10.1 2.2 %collective-permute-start.2 = (bf16[2,224,128]{2,1,0:T(8,128)(2,1)S(1)}, bf16[2,224,128]{2,1,0:T(8,128)(2,1)S(1)}, u32[]{:S(2)}, u32[]{:S(2)}) collective-permute-start(bf16[2,224,128]{2,1,0:T(8,128)(2,1)S(1)} %get-tuple-element.30), channel_id=1, source_target_pairs={{0,128},{64,192},{128,0},{192,64},{1,129},{65,193},{129,1},{193,65... | collective-permute-start | bytes 344072 | tf_op jit(solution)/shard_map/ppermute | solution.py:227
  12.2 1.1 collective-permute-start.3
  13.3 2.7 %collective-permute-done.1 = bf16[2,224,128]{2,1,0:T(8,128)(2,1)S(1)} collective-permute-done((bf16[2,224,128]{2,1,0:T(8,128)(2,1)S(1)}, bf16[2,224,128]{2,1,0:T(8,128)(2,1)S(1)}, u32[]{:S(2)}, u32[]{:S(2)}) %collective-permute-start.1) | collective-permute-done | bytes 114720 | tf_op jit(solution)/shard_map/ppermute | solution.py:227
  16.0 1.4 collective-permute-done.2
  17.3 0.8 collective-permute-done.3
  19.0 5.7 %all-to-all-start = ((bf16[8,128,1024]{2,1,0:T(8,128)(2,1)}), bf16[8,128,1024]{2,1,0:T(8,128)(2,1)S(1)}, u32[]{:S(2)}, u32[]{:S(2)}) async-start(bf16[8,128,1024]{2,1,0:T(8,128)(2,1)} %param.4), calls=%async_computation | async-start | bytes 4194304 | tf_op jit(solution)/shard_map/all_to_all | solution.py:264
  24.7 1.3 collective-permute-start.9
  26.7 3.1 %collective-permute-start.6 = (bf16[224,768]{1,0:T(8,128)(2,1)S(1)}, bf16[224,768]{1,0:T(8,128)(2,1)}, u32[]{:S(2)}, u32[]{:S(2)}) collective-permute-start(bf16[224,768]{1,0:T(8,128)(2,1)S(1)} %get-tuple-element.24), channel_id=1, source_target_pairs={{0,16},{8,24},{16,0},{24,8},{1,17},{9,25},{17,1},{25,9},{2,18},{10... | collective-permute-start | bytes 1032200 | tf_op jit(solution)/shard_map/ppermute | solution.py:227
  30.1 26.6 %collective-permute-done.6.refs_2_ = bf16[224,768]{1,0:T(8,128)(2,1)} collective-permute-done((bf16[224,768]{1,0:T(8,128)(2,1)S(1)}, bf16[224,768]{1,0:T(8,128)(2,1)}, u32[]{:S(2)}, u32[]{:S(2)}) %collective-permute-start.6) | collective-permute-done | bytes 344096 | tf_op jit(solution)/shard_map/ppermute | solution.py:227
  57.4 6.4 %gram.1 = (f32[224,1024]{1,0:T(8,128)}, bf16[4,304,128]{2,1,0:T(8,128)(2,1)S(1)}) custom-call(s32[2]{0:T(128)S(1)} %pad_add_fusion.place_ref, s32[1]{0:T(128)} %bitcast.2.group_ref, s32[8]{0:T(128)S(1)} %dynamic-slice_reduce_fusion.counts_ref, bf16[8,128,1024]{2,1,0:T(8,128)(2,1)S(1)} %all-to-all-done.hidden_ref, ...), custom_call_target="tpu_custom_call" | custom-call | tf_op jit(solution)/shard_map/gram/pallas_call | solution.py:211
  63.8 5.4 %collective-permute-start.12 = (bf16[304,128]{1,0:T(8,128)(2,1)S(1)}, bf16[304,128]{1,0:T(8,128)(2,1)S(1)}, u32[]{:S(2)}, u32[]{:S(2)}) collective-permute-start(bf16[304,128]{1,0:T(8,128)(2,1)S(1)} %get-tuple-element.32), channel_id=1, source_target_pairs={{0,6},{2,0},{4,2},{6,4},{1,7},{3,1},{5,3},{7,5},{8,14},{10,8},{12,... | collective-permute-start | bytes 233480 | tf_op jit(solution)/shard_map/ppermute | solution.py:227
  69.2 1.2 collective-permute-start.11
  70.4 2.1 %collective-permute-start.10 = (bf16[304,128]{1,0:T(8,128)(2,1)S(1)}, bf16[304,128]{1,0:T(8,128)(2,1)S(1)}, u32[]{:S(2)}, u32[]{:S(2)}) collective-permute-start(bf16[304,128]{1,0:T(8,128)(2,1)S(1)} %get-tuple-element.34), channel_id=1, source_target_pairs={{0,2},{2,4},{4,6},{6,0},{1,3},{3,5},{5,7},{7,1},{8,10},{10,12},{12... | collective-permute-start | bytes 233480 | tf_op jit(solution)/shard_map/ppermute | solution.py:227
  72.5 4.1 %collective-permute-done.11.refs_2_ = bf16[304,128]{1,0:T(8,128)(2,1)S(1)} collective-permute-done((bf16[304,128]{1,0:T(8,128)(2,1)S(1)}, bf16[304,128]{1,0:T(8,128)(2,1)S(1)}, u32[]{:S(2)}, u32[]{:S(2)}) %collective-permute-start.11) | collective-permute-done | bytes 77856 | tf_op jit(solution)/shard_map/ppermute | solution.py:227
  76.6 1.1 collective-permute-done.10.refs_1_
  77.9 3.2 %collective-permute-done.13.refs_1_ = bf16[304,128]{1,0:T(8,128)(2,1)S(1)} collective-permute-done((bf16[304,128]{1,0:T(8,128)(2,1)S(1)}, bf16[304,128]{1,0:T(8,128)(2,1)S(1)}, u32[]{:S(2)}, u32[]{:S(2)}) %collective-permute-start.13) | collective-permute-done | bytes 77856 | tf_op jit(solution)/shard_map/ppermute | solution.py:227
  81.2 2.8 %collective-permute-start.16 = (bf16[304,128]{1,0:T(8,128)(2,1)S(1)}, bf16[304,128]{1,0:T(8,128)(2,1)S(1)}, u32[]{:S(2)}, u32[]{:S(2)}) collective-permute-start(bf16[304,128]{1,0:T(8,128)(2,1)S(1)} %sum.3), channel_id=1, source_target_pairs={{0,6},{2,0},{4,2},{6,4},{1,7},{3,1},{5,3},{7,5},{8,14},{10,8},{12,... | collective-permute-start | bytes 233480 | tf_op jit(solution)/shard_map/ppermute | solution.py:227
  84.0 2.2 %collective-permute-start.15 = (bf16[304,128]{1,0:T(8,128)(2,1)S(1)}, bf16[304,128]{1,0:T(8,128)(2,1)S(1)}, u32[]{:S(2)}, u32[]{:S(2)}) collective-permute-start(bf16[304,128]{1,0:T(8,128)(2,1)S(1)} %sum.3), channel_id=1, source_target_pairs={{0,4},{2,6},{4,0},{6,2},{1,5},{3,7},{5,1},{7,3},{8,12},{10,14},{12... | collective-permute-start | bytes 233480 | tf_op jit(solution)/shard_map/ppermute | solution.py:227
  86.2 2.2 %collective-permute-start.14 = (bf16[304,128]{1,0:T(8,128)(2,1)S(1)}, bf16[304,128]{1,0:T(8,128)(2,1)S(1)}, u32[]{:S(2)}, u32[]{:S(2)}) collective-permute-start(bf16[304,128]{1,0:T(8,128)(2,1)S(1)} %sum.3), channel_id=1, source_target_pairs={{0,2},{2,4},{4,6},{6,0},{1,3},{3,5},{5,7},{7,1},{8,10},{10,12},{12... | collective-permute-start | bytes 233480 | tf_op jit(solution)/shard_map/ppermute | solution.py:227
  88.4 3.0 %collective-permute-done.15 = bf16[304,128]{1,0:T(8,128)(2,1)S(1)} collective-permute-done((bf16[304,128]{1,0:T(8,128)(2,1)S(1)}, bf16[304,128]{1,0:T(8,128)(2,1)S(1)}, u32[]{:S(2)}, u32[]{:S(2)}) %collective-permute-start.15) | collective-permute-done | bytes 77856 | tf_op jit(solution)/shard_map/ppermute | solution.py:227
  91.4 0.8 collective-permute-done.14
  92.7 1.0 collective-permute-start.17
  93.7 4.3 %collective-permute-done.19.refs_3_ = bf16[4,304,128]{2,1,0:T(8,128)(2,1)S(1)} collective-permute-done((bf16[4,304,128]{2,1,0:T(8,128)(2,1)S(1)}, bf16[4,304,128]{2,1,0:T(8,128)(2,1)S(1)}, u32[]{:S(2)}, u32[]{:S(2)}) %collective-permute-start.19) | collective-permute-done | bytes 311328 | tf_op jit(solution)/shard_map/ppermute | solution.py:227
  98.0 1.7 %collective-permute-done.18.refs_2_ = bf16[4,304,128]{2,1,0:T(8,128)(2,1)S(1)} collective-permute-done((bf16[4,304,128]{2,1,0:T(8,128)(2,1)S(1)}, bf16[4,304,128]{2,1,0:T(8,128)(2,1)S(1)}, u32[]{:S(2)}, u32[]{:S(2)}) %collective-permute-start.18) | collective-permute-done | bytes 311328 | tf_op jit(solution)/shard_map/ppermute | solution.py:227
  99.7 7.6 %collective-permute-done.17.refs_1_ = bf16[4,304,128]{2,1,0:T(8,128)(2,1)S(1)} collective-permute-done((bf16[4,304,128]{2,1,0:T(8,128)(2,1)S(1)}, bf16[4,304,128]{2,1,0:T(8,128)(2,1)S(1)}, u32[]{:S(2)}, u32[]{:S(2)}) %collective-permute-start.17) | collective-permute-done | bytes 311328 | tf_op jit(solution)/shard_map/ppermute | solution.py:227
  107.3 13.9 %polynomial.1 = f32[224,1024]{1,0:T(8,128)S(1)} custom-call(s32[2]{0:T(128)S(1)} %pad_add_fusion.place_ref, f32[224,1024]{1,0:T(8,128)} %get-tuple-element.26.moment_away_ref, bf16[4,304,128]{2,1,0:T(8,128)(2,1)S(1)} %pad_maximum_fusion.1.refs_0_, bf16[4,304,128]{2,1,0:T(8,128)(2,1)S(1)} %collective-permute-done.17.refs_1_, ...), custom_call_target="tpu_custom_call" | custom-call | tf_op jit(solution)/shard_map/polynomial/pallas_call | solution.py:211
  121.3 22.8 %all-gather.2 = f16[1792,1024]{1,0:T(8,128)(2,1)S(1)} all-gather(f16[224,1024]{1,0:T(8,128)(2,1)S(1)} %multiply_convert_fusion), channel_id=2, replica_groups=mesh['y'=4,'core'=2,'x'=4,'z_pair'=4,'z_low'=2] {'y','core'}, dimensions={0}, use_global_device_ids=true | all-gather | bytes 4128768 | tf_op jit(solution)/shard_map/all_gather | solution.py:303
  144.0 4.1 %convert_multiply_fusion = f32[1792,1024]{1,0:T(8,128)} fusion(f16[1792,1024]{1,0:T(8,128)(2,1)S(1)} %all-gather.2), kind=kLoop, calls=%fused_computation | loop fusion | flops 3670016 | bytes 11010048 | tf_op jit(solution)/shard_map/mul | solution.py:304
  (33 shorter events, 3.8 us)
Async XLA Ops:
  0.6 29.2 %copy-start = (s32[8,8]{1,0:T(8,128)S(1)}, s32[8,8]{1,0:T(8,128)}, u32[]{:S(2)}) copy-start(s32[8,8]{1,0:T(8,128)} %param.7) | copy-start | bytes 772
  1.8 8.2 %collective-permute-start = (bf16[4,224,128]{2,1,0:T(8,128)(2,1)S(1)}, bf16[4,224,128]{2,1,0:T(8,128)(2,1)S(1)}, u32[]{:S(2)}, u32[]{:S(2)}) collective-permute-start(bf16[4,224,128]{2,1,0:T(8,128)(2,1)S(1)} %get-tuple-element.16), channel_id=1, source_target_pairs={{0,32},{32,0},{1,33},{33,1},{2,34},{34,2},{3,35},{35,3},{4,36},{36... | collective-permute-start | bytes 688136 | tf_op jit(solution)/shard_map/ppermute | solution.py:227
  7.2 11.0 %collective-permute-start.4 = (bf16[224,768]{1,0:T(8,128)(2,1)S(1)}, bf16[224,768]{1,0:T(8,128)(2,1)S(1)}, u32[]{:S(2)}, u32[]{:S(2)}) collective-permute-start(bf16[224,768]{1,0:T(8,128)(2,1)S(1)} %get-tuple-element.17), channel_id=1, source_target_pairs={{0,8},{8,16},{16,24},{24,0},{1,9},{9,17},{17,25},{25,1},{2,10},{10... | collective-permute-start | bytes 1032200 | tf_op jit(solution)/shard_map/ppermute | solution.py:227
  7.3 10.9 %collective-permute-start.5 = (bf16[224,768]{1,0:T(8,128)(2,1)S(1)}, bf16[224,768]{1,0:T(8,128)(2,1)S(1)}, u32[]{:S(2)}, u32[]{:S(2)}) collective-permute-start(bf16[224,768]{1,0:T(8,128)(2,1)S(1)} %get-tuple-element.18), channel_id=1, source_target_pairs={{0,24},{8,0},{16,8},{24,16},{1,25},{9,1},{17,9},{25,17},{2,26},{10... | collective-permute-start | bytes 1032200 | tf_op jit(solution)/shard_map/ppermute | solution.py:227
  10.0 6.0 %collective-permute-start.1 = (bf16[2,224,128]{2,1,0:T(8,128)(2,1)S(1)}, bf16[2,224,128]{2,1,0:T(8,128)(2,1)S(1)}, u32[]{:S(2)}, u32[]{:S(2)}) collective-permute-start(bf16[2,224,128]{2,1,0:T(8,128)(2,1)S(1)} %get-tuple-element.29), channel_id=1, source_target_pairs={{0,64},{64,128},{128,192},{192,0},{1,65},{65,129},{129,193},{193,1... | collective-permute-start | bytes 344072 | tf_op jit(solution)/shard_map/ppermute | solution.py:227
  10.1 7.3 %collective-permute-start.2 = (bf16[2,224,128]{2,1,0:T(8,128)(2,1)S(1)}, bf16[2,224,128]{2,1,0:T(8,128)(2,1)S(1)}, u32[]{:S(2)}, u32[]{:S(2)}) collective-permute-start(bf16[2,224,128]{2,1,0:T(8,128)(2,1)S(1)} %get-tuple-element.30), channel_id=1, source_target_pairs={{0,128},{64,192},{128,0},{192,64},{1,129},{65,193},{129,1},{193,65... | collective-permute-start | bytes 344072 | tf_op jit(solution)/shard_map/ppermute | solution.py:227
  12.2 5.9 %collective-permute-start.3 = (bf16[2,224,128]{2,1,0:T(8,128)(2,1)S(1)}, bf16[2,224,128]{2,1,0:T(8,128)(2,1)S(1)}, u32[]{:S(2)}, u32[]{:S(2)}) collective-permute-start(bf16[2,224,128]{2,1,0:T(8,128)(2,1)S(1)} %get-tuple-element.31), channel_id=1, source_target_pairs={{0,192},{64,0},{128,64},{192,128},{1,193},{65,1},{129,65},{193,129... | collective-permute-start | bytes 344072 | tf_op jit(solution)/shard_map/ppermute | solution.py:227
  18.1 0.7 copy-start.2
  18.1 0.9 copy-start.3
  19.0 37.7 %all-to-all-start = ((bf16[8,128,1024]{2,1,0:T(8,128)(2,1)}), bf16[8,128,1024]{2,1,0:T(8,128)(2,1)S(1)}, u32[]{:S(2)}, u32[]{:S(2)}) async-start(bf16[8,128,1024]{2,1,0:T(8,128)(2,1)} %param.4), calls=%async_computation | async-start | bytes 4194304 | tf_op jit(solution)/shard_map/all_to_all | solution.py:264
  24.7 31.9 %collective-permute-start.9 = (bf16[8,224,128]{2,1,0:T(8,128)(2,1)S(1)}, bf16[8,224,128]{2,1,0:T(8,128)(2,1)S(1)}, u32[]{:S(2)}, u32[]{:S(2)}) collective-permute-start(bf16[8,224,128]{2,1,0:T(8,128)(2,1)S(1)} %pad_maximum_fusion.tokens_ref), channel_id=1, source_target_pairs={{0,24},{8,0},{16,8},{24,16},{1,25},{9,1},{17,9},{25,17},{2,26},{10... | collective-permute-start | bytes 1376264 | tf_op jit(solution)/shard_map/ppermute | solution.py:227
  26.1 30.6 %collective-permute-start.8 = (bf16[8,224,128]{2,1,0:T(8,128)(2,1)S(1)}, bf16[8,224,128]{2,1,0:T(8,128)(2,1)}, u32[]{:S(2)}, u32[]{:S(2)}) collective-permute-start(bf16[8,224,128]{2,1,0:T(8,128)(2,1)S(1)} %pad_maximum_fusion.tokens_ref), channel_id=1, source_target_pairs={{0,16},{8,24},{16,0},{24,8},{1,17},{9,25},{17,1},{25,9},{2,18},{10... | collective-permute-start | bytes 1376264 | tf_op jit(solution)/shard_map/ppermute | solution.py:227
  26.1 30.6 %collective-permute-start.7 = (bf16[8,224,128]{2,1,0:T(8,128)(2,1)S(1)}, bf16[8,224,128]{2,1,0:T(8,128)(2,1)}, u32[]{:S(2)}, u32[]{:S(2)}) collective-permute-start(bf16[8,224,128]{2,1,0:T(8,128)(2,1)S(1)} %pad_maximum_fusion.tokens_ref), channel_id=1, source_target_pairs={{0,8},{8,16},{16,24},{24,0},{1,9},{9,17},{17,25},{25,1},{2,10},{10... | collective-permute-start | bytes 1376264 | tf_op jit(solution)/shard_map/ppermute | solution.py:227
  26.7 29.9 %collective-permute-start.6 = (bf16[224,768]{1,0:T(8,128)(2,1)S(1)}, bf16[224,768]{1,0:T(8,128)(2,1)}, u32[]{:S(2)}, u32[]{:S(2)}) collective-permute-start(bf16[224,768]{1,0:T(8,128)(2,1)S(1)} %get-tuple-element.24), channel_id=1, source_target_pairs={{0,16},{8,24},{16,0},{24,8},{1,17},{9,25},{17,1},{25,9},{2,18},{10... | collective-permute-start | bytes 1032200 | tf_op jit(solution)/shard_map/ppermute | solution.py:227
  56.7 0.8 copy-start.1
  63.8 8.6 %collective-permute-start.12 = (bf16[304,128]{1,0:T(8,128)(2,1)S(1)}, bf16[304,128]{1,0:T(8,128)(2,1)S(1)}, u32[]{:S(2)}, u32[]{:S(2)}) collective-permute-start(bf16[304,128]{1,0:T(8,128)(2,1)S(1)} %get-tuple-element.32), channel_id=1, source_target_pairs={{0,6},{2,0},{4,2},{6,4},{1,7},{3,1},{5,3},{7,5},{8,14},{10,8},{12,... | collective-permute-start | bytes 233480 | tf_op jit(solution)/shard_map/ppermute | solution.py:227
  69.2 7.4 %collective-permute-start.11 = (bf16[304,128]{1,0:T(8,128)(2,1)S(1)}, bf16[304,128]{1,0:T(8,128)(2,1)S(1)}, u32[]{:S(2)}, u32[]{:S(2)}) collective-permute-start(bf16[304,128]{1,0:T(8,128)(2,1)S(1)} %get-tuple-element.33), channel_id=1, source_target_pairs={{0,4},{2,6},{4,0},{6,2},{1,5},{3,7},{5,1},{7,3},{8,12},{10,14},{12... | collective-permute-start | bytes 233480 | tf_op jit(solution)/shard_map/ppermute | solution.py:227
  70.4 7.3 %collective-permute-start.10 = (bf16[304,128]{1,0:T(8,128)(2,1)S(1)}, bf16[304,128]{1,0:T(8,128)(2,1)S(1)}, u32[]{:S(2)}, u32[]{:S(2)}) collective-permute-start(bf16[304,128]{1,0:T(8,128)(2,1)S(1)} %get-tuple-element.34), channel_id=1, source_target_pairs={{0,2},{2,4},{4,6},{6,0},{1,3},{3,5},{5,7},{7,1},{8,10},{10,12},{12... | collective-permute-start | bytes 233480 | tf_op jit(solution)/shard_map/ppermute | solution.py:227
  77.8 3.3 %collective-permute-start.13 = (bf16[304,128]{1,0:T(8,128)(2,1)S(1)}, bf16[304,128]{1,0:T(8,128)(2,1)S(1)}, u32[]{:S(2)}, u32[]{:S(2)}) collective-permute-start(bf16[304,128]{1,0:T(8,128)(2,1)S(1)} %sum.2.refs_0_), channel_id=1, source_target_pairs={{0,1},{1,0},{2,3},{3,2},{4,5},{5,4},{6,7},{7,6},{8,9},{9,8},{10,11... | collective-permute-start | bytes 233480 | tf_op jit(solution)/shard_map/ppermute | solution.py:227
  81.2 7.2 %collective-permute-start.16 = (bf16[304,128]{1,0:T(8,128)(2,1)S(1)}, bf16[304,128]{1,0:T(8,128)(2,1)S(1)}, u32[]{:S(2)}, u32[]{:S(2)}) collective-permute-start(bf16[304,128]{1,0:T(8,128)(2,1)S(1)} %sum.3), channel_id=1, source_target_pairs={{0,6},{2,0},{4,2},{6,4},{1,7},{3,1},{5,3},{7,5},{8,14},{10,8},{12,... | collective-permute-start | bytes 233480 | tf_op jit(solution)/shard_map/ppermute | solution.py:227
  84.0 7.3 %collective-permute-start.15 = (bf16[304,128]{1,0:T(8,128)(2,1)S(1)}, bf16[304,128]{1,0:T(8,128)(2,1)S(1)}, u32[]{:S(2)}, u32[]{:S(2)}) collective-permute-start(bf16[304,128]{1,0:T(8,128)(2,1)S(1)} %sum.3), channel_id=1, source_target_pairs={{0,4},{2,6},{4,0},{6,2},{1,5},{3,7},{5,1},{7,3},{8,12},{10,14},{12... | collective-permute-start | bytes 233480 | tf_op jit(solution)/shard_map/ppermute | solution.py:227
  86.2 6.0 %collective-permute-start.14 = (bf16[304,128]{1,0:T(8,128)(2,1)S(1)}, bf16[304,128]{1,0:T(8,128)(2,1)S(1)}, u32[]{:S(2)}, u32[]{:S(2)}) collective-permute-start(bf16[304,128]{1,0:T(8,128)(2,1)S(1)} %sum.3), channel_id=1, source_target_pairs={{0,2},{2,4},{4,6},{6,0},{1,3},{3,5},{5,7},{7,1},{8,10},{10,12},{12... | collective-permute-start | bytes 233480 | tf_op jit(solution)/shard_map/ppermute | solution.py:227
  92.2 5.8 %collective-permute-start.19 = (bf16[4,304,128]{2,1,0:T(8,128)(2,1)S(1)}, bf16[4,304,128]{2,1,0:T(8,128)(2,1)S(1)}, u32[]{:S(2)}, u32[]{:S(2)}) collective-permute-start(bf16[4,304,128]{2,1,0:T(8,128)(2,1)S(1)} %pad_maximum_fusion.1.refs_0_), channel_id=1, source_target_pairs={{0,24},{8,0},{16,8},{24,16},{1,25},{9,1},{17,9},{25,17},{2,26},{10... | collective-permute-start | bytes 933896 | tf_op jit(solution)/shard_map/ppermute | solution.py:227
  92.3 7.4 %collective-permute-start.18 = (bf16[4,304,128]{2,1,0:T(8,128)(2,1)S(1)}, bf16[4,304,128]{2,1,0:T(8,128)(2,1)S(1)}, u32[]{:S(2)}, u32[]{:S(2)}) collective-permute-start(bf16[4,304,128]{2,1,0:T(8,128)(2,1)S(1)} %pad_maximum_fusion.1.refs_0_), channel_id=1, source_target_pairs={{0,16},{8,24},{16,0},{24,8},{1,17},{9,25},{17,1},{25,9},{2,18},{10... | collective-permute-start | bytes 933896 | tf_op jit(solution)/shard_map/ppermute | solution.py:227
  92.7 14.6 %collective-permute-start.17 = (bf16[4,304,128]{2,1,0:T(8,128)(2,1)S(1)}, bf16[4,304,128]{2,1,0:T(8,128)(2,1)S(1)}, u32[]{:S(2)}, u32[]{:S(2)}) collective-permute-start(bf16[4,304,128]{2,1,0:T(8,128)(2,1)S(1)} %pad_maximum_fusion.1.refs_0_), channel_id=1, source_target_pairs={{0,8},{8,16},{16,24},{24,0},{1,9},{9,17},{17,25},{25,1},{2,10},{10... | collective-permute-start | bytes 933896 | tf_op jit(solution)/shard_map/ppermute | solution.py:227

commit v11 on v7

--- a/solution.py
+++ b/solution.py
@@ -82,7 +82,8 @@
 
 
 def gram_kernel(place_ref, group_ref, counts_ref, hidden_ref, tokens_ref, *refs):
-    count = (len(refs) - 4) // 2
+    count = (len(refs) - 3) // 3
+    other_tokens, refs = refs[: count - 1], refs[count - 1 :]
     away_refs, moment_ref, cut_ref, needed_ref = refs[:count], *refs[count : count + 3]
     here_refs, semaphores = refs[count + 3 : -1], refs[-1]
     copies = fetched(away_refs, here_refs, semaphores)
@@ -115,9 +116,8 @@
     values = [jnp.concatenate([moment_ref[:, column(place, block)] for block in range(NEEDED)], axis=1)]
     for copy in copies[1:]:
         copy.wait()
-    others = len(other_refs) // 2
-    for momentum_columns, other_tokens in zip(other_refs[:others], other_refs[others:]):
-        gradient = jnp.dot(tokens_of(other_tokens), needed_ref[...], preferred_element_type=F32)
+    for momentum_columns, tokens in zip(other_refs, other_tokens):
+        gradient = jnp.dot(tokens_of(tokens), needed_ref[...], preferred_element_type=F32)
         values.append(MOMENTUM_DECAY * momentum_columns[...].astype(F32) + gradient)
     high, low = split_two(jnp.concatenate(values, axis=0))
     left = jnp.concatenate([high[:, : 2 * BLOCK], low[:, : 2 * BLOCK], high[:, : 2 * BLOCK]], axis=0).T
@@ -256,7 +256,7 @@
     other_tokens = [shifted(tokens, "x", k) for k in distances]
     fetch = [
         pltpu.with_memory_space_constraint(value, pltpu.HBM)
-        for value in [momentum[0]] + other_columns + other_tokens
+        for value in [momentum[0]] + other_columns
     ]
     moment, parts = call(
         gram_kernel,
@@ -264,11 +264,11 @@
             jax.ShapeDtypeStruct((rows, FF), F32),
             jax.ShapeDtypeStruct((pairs, piece + UNIT, BLOCK), BF16),
         ),
-        [place, group, counts, hidden, tokens] + fetch,
+        [place, group, counts, hidden, tokens] + other_tokens + fetch,
         scratch=[pltpu.VMEM((hidden.shape[0] * hidden.shape[1], NEEDED * BLOCK), BF16)]
         + [pltpu.VMEM(value.shape, value.dtype) for value in fetch]
         + [pltpu.SemaphoreType.DMA((len(fetch),))],
-        away=range(5, 5 + len(fetch)),
+        away=range(5 + len(other_tokens), 5 + len(other_tokens) + len(fetch)),
         scalars=3,
         mib=28,
     )

time: 147 us -> 147 us (level)
  no operation moved by 1% of the time
where the time goes in v11:
time: 147 us
  waiting for transfers between devices  57.2 us (39%)
  starting transfers between devices  37.5 us (26%)
  Pallas kernels  22.9 us (16%)
  blocking collectives  22.7 us (15%)
  other arithmetic  4.37 us (3%)
  local copies, waits for them, and re-layouts  1.8 us (1%)
    ppermute x20, waiting for transfers between devices, shifted(): lax.ppermute(value, axis, [(i, (i + distance) % size) for i in range(size)])  57.2 us
    ppermute x20, starting transfers between devices, shifted(): lax.ppermute(value, axis, [(i, (i + distance) % size) for i in range(size)])  31.8 us
    pallas_call x5, Pallas kernels, call(): pl.pallas_call(kernel, out_shape=out_shape, in_specs=[whole(pltpu.SMEM if...  22.9 us
    all_gather x1, blocking collectives, body(): lax.all_gather((update * 256.0).astype(jnp.float16), DP, axis=0, tiled=Fa...  22.7 us
    all_to_all x1, starting transfers between devices, body(): hidden = lax.all_to_all(hidden_token_tiles, DP, 0, 0, tiled=True)  5.66 us
    mul x1, other arithmetic, body(): return (moment[None], gathered.astype(F32) * (1.0 / 256.0))  4.07 us
  transfers between devices with their start and end apart: 21, of which 12 were waited for; matrix products, arithmetic and copies ran while one was open for 0% of the time, Pallas kernels for 0%

profile of v11, /device:TPU:1, one launch (start us, length us, event | category | flops | bytes accessed | tf_op | source)
XLA Modules:
  0.0 147.2 jit_solution(11382486597886942749)
XLA Ops:
  0.7 2.1 %outgoing.1 = (bf16[224,768]{1,0:T(8,128)(2,1)S(1)}, bf16[224,768]{1,0:T(8,128)(2,1)S(1)}, bf16[224,768]{1,0:T(8,128)(2,1)S(1)}, bf16[4,224,128]{2,1,0:T(8,128)(2,1)S(1)}, bf16[4,224,128]{2,1,0:T(8,128)(2,1)S(1)}) custom-call(s32[2]{0:T(128)S(1)} %pad_add_fusion.place_ref, s32[1]{0:T(128)} %bitcast.2.group_ref, f32[224,1024]{1,0:T(8,128)} %bitcast.31, ...), custom_call_target="tpu_custom_call" | custom-call | tf_op jit(solution)/shard_map/outgoing/pallas_call | solution.py:208
  3.5 3.2 %collective-permute-start = (bf16[4,224,128]{2,1,0:T(8,128)(2,1)S(1)}, bf16[4,224,128]{2,1,0:T(8,128)(2,1)S(1)}, u32[]{:S(2)}, u32[]{:S(2)}) collective-permute-start(bf16[4,224,128]{2,1,0:T(8,128)(2,1)S(1)} %get-tuple-element.16), channel_id=1, source_target_pairs={{0,32},{32,0},{1,33},{33,1},{2,34},{34,2},{3,35},{35,3},{4,36},{36... | collective-permute-start | bytes 688136 | tf_op jit(solution)/shard_map/ppermute | solution.py:224
  6.8 2.7 %collective-permute-start.5 = (bf16[224,768]{1,0:T(8,128)(2,1)S(1)}, bf16[224,768]{1,0:T(8,128)(2,1)S(1)}, u32[]{:S(2)}, u32[]{:S(2)}) collective-permute-start(bf16[224,768]{1,0:T(8,128)(2,1)S(1)} %get-tuple-element.18), channel_id=1, source_target_pairs={{0,24},{8,0},{16,8},{24,16},{1,25},{9,1},{17,9},{25,17},{2,26},{10... | collective-permute-start | bytes 1032200 | tf_op jit(solution)/shard_map/ppermute | solution.py:224
  9.6 2.2 %collective-permute-start.2 = (bf16[2,224,128]{2,1,0:T(8,128)(2,1)S(1)}, bf16[2,224,128]{2,1,0:T(8,128)(2,1)S(1)}, u32[]{:S(2)}, u32[]{:S(2)}) collective-permute-start(bf16[2,224,128]{2,1,0:T(8,128)(2,1)S(1)} %get-tuple-element.30), channel_id=1, source_target_pairs={{0,128},{64,192},{128,0},{192,64},{1,129},{65,193},{129,1},{193,65... | collective-permute-start | bytes 344072 | tf_op jit(solution)/shard_map/ppermute | solution.py:224
  11.8 1.1 collective-permute-start.3
  12.8 2.7 %collective-permute-done.1 = bf16[2,224,128]{2,1,0:T(8,128)(2,1)S(1)} collective-permute-done((bf16[2,224,128]{2,1,0:T(8,128)(2,1)S(1)}, bf16[2,224,128]{2,1,0:T(8,128)(2,1)S(1)}, u32[]{:S(2)}, u32[]{:S(2)}) %collective-permute-start.1) | collective-permute-done | bytes 114720 | tf_op jit(solution)/shard_map/ppermute | solution.py:224
  15.5 1.4 collective-permute-done.2
  16.9 0.8 collective-permute-done.3
  17.7 0.7 copy-done.2
  18.6 5.7 %all-to-all-start = ((bf16[8,128,1024]{2,1,0:T(8,128)(2,1)}), bf16[8,128,1024]{2,1,0:T(8,128)(2,1)S(1)}, u32[]{:S(2)}, u32[]{:S(2)}) async-start(bf16[8,128,1024]{2,1,0:T(8,128)(2,1)} %param.4), calls=%async_computation | async-start | bytes 4194304 | tf_op jit(solution)/shard_map/all_to_all | solution.py:254
  24.3 1.3 collective-permute-start.8
  26.3 3.1 %collective-permute-start.9 = (bf16[224,768]{1,0:T(8,128)(2,1)}, bf16[224,768]{1,0:T(8,128)(2,1)}, u32[]{:S(2)}, u32[]{:S(2)}) collective-permute-start(bf16[224,768]{1,0:T(8,128)(2,1)} %copy-done.1), channel_id=1, source_target_pairs={{0,16},{8,24},{16,0},{24,8},{1,17},{9,25},{17,1},{25,9},{2,18},{10... | collective-permute-start | bytes 1032200 | tf_op jit(solution)/shard_map/ppermute | solution.py:224
  29.6 26.6 %collective-permute-done.9.refs_5_ = bf16[224,768]{1,0:T(8,128)(2,1)} collective-permute-done((bf16[224,768]{1,0:T(8,128)(2,1)}, bf16[224,768]{1,0:T(8,128)(2,1)}, u32[]{:S(2)}, u32[]{:S(2)}) %collective-permute-start.9) | collective-permute-done | bytes 344096 | tf_op jit(solution)/shard_map/ppermute | solution.py:224
  56.2 6.7 %gram.1 = (f32[224,1024]{1,0:T(8,128)}, bf16[4,304,128]{2,1,0:T(8,128)(2,1)S(1)}) custom-call(s32[2]{0:T(128)S(1)} %pad_add_fusion.place_ref, s32[1]{0:T(128)} %bitcast.2.group_ref, s32[8]{0:T(128)S(1)} %dynamic-slice_reduce_fusion.counts_ref, bf16[8,128,1024]{2,1,0:T(8,128)(2,1)S(1)} %all-to-all-done.hidden_ref, ...), custom_call_target="tpu_custom_call" | custom-call | tf_op jit(solution)/shard_map/gram/pallas_call | solution.py:208
  63.0 5.4 %collective-permute-start.12 = (bf16[304,128]{1,0:T(8,128)(2,1)S(1)}, bf16[304,128]{1,0:T(8,128)(2,1)S(1)}, u32[]{:S(2)}, u32[]{:S(2)}) collective-permute-start(bf16[304,128]{1,0:T(8,128)(2,1)S(1)} %get-tuple-element.32), channel_id=1, source_target_pairs={{0,6},{2,0},{4,2},{6,4},{1,7},{3,1},{5,3},{7,5},{8,14},{10,8},{12,... | collective-permute-start | bytes 233480 | tf_op jit(solution)/shard_map/ppermute | solution.py:224
  68.4 1.2 collective-permute-start.11
  69.5 2.1 %collective-permute-start.10 = (bf16[304,128]{1,0:T(8,128)(2,1)S(1)}, bf16[304,128]{1,0:T(8,128)(2,1)S(1)}, u32[]{:S(2)}, u32[]{:S(2)}) collective-permute-start(bf16[304,128]{1,0:T(8,128)(2,1)S(1)} %get-tuple-element.34), channel_id=1, source_target_pairs={{0,2},{2,4},{4,6},{6,0},{1,3},{3,5},{5,7},{7,1},{8,10},{10,12},{12... | collective-permute-start | bytes 233480 | tf_op jit(solution)/shard_map/ppermute | solution.py:224
  71.6 4.1 %collective-permute-done.11.refs_2_ = bf16[304,128]{1,0:T(8,128)(2,1)S(1)} collective-permute-done((bf16[304,128]{1,0:T(8,128)(2,1)S(1)}, bf16[304,128]{1,0:T(8,128)(2,1)S(1)}, u32[]{:S(2)}, u32[]{:S(2)}) %collective-permute-start.11) | collective-permute-done | bytes 77856 | tf_op jit(solution)/shard_map/ppermute | solution.py:224
  75.7 1.2 collective-permute-done.10.refs_1_
  77.0 3.2 %collective-permute-done.13.refs_1_ = bf16[304,128]{1,0:T(8,128)(2,1)S(1)} collective-permute-done((bf16[304,128]{1,0:T(8,128)(2,1)S(1)}, bf16[304,128]{1,0:T(8,128)(2,1)S(1)}, u32[]{:S(2)}, u32[]{:S(2)}) %collective-permute-start.13) | collective-permute-done | bytes 77856 | tf_op jit(solution)/shard_map/ppermute | solution.py:224
  80.4 2.8 %collective-permute-start.16 = (bf16[304,128]{1,0:T(8,128)(2,1)S(1)}, bf16[304,128]{1,0:T(8,128)(2,1)S(1)}, u32[]{:S(2)}, u32[]{:S(2)}) collective-permute-start(bf16[304,128]{1,0:T(8,128)(2,1)S(1)} %sum.3), channel_id=1, source_target_pairs={{0,6},{2,0},{4,2},{6,4},{1,7},{3,1},{5,3},{7,5},{8,14},{10,8},{12,... | collective-permute-start | bytes 233480 | tf_op jit(solution)/shard_map/ppermute | solution.py:224
  83.2 2.1 %collective-permute-start.15 = (bf16[304,128]{1,0:T(8,128)(2,1)S(1)}, bf16[304,128]{1,0:T(8,128)(2,1)S(1)}, u32[]{:S(2)}, u32[]{:S(2)}) collective-permute-start(bf16[304,128]{1,0:T(8,128)(2,1)S(1)} %sum.3), channel_id=1, source_target_pairs={{0,4},{2,6},{4,0},{6,2},{1,5},{3,7},{5,1},{7,3},{8,12},{10,14},{12... | collective-permute-start | bytes 233480 | tf_op jit(solution)/shard_map/ppermute | solution.py:224
  85.3 2.3 %collective-permute-start.14 = (bf16[304,128]{1,0:T(8,128)(2,1)S(1)}, bf16[304,128]{1,0:T(8,128)(2,1)S(1)}, u32[]{:S(2)}, u32[]{:S(2)}) collective-permute-start(bf16[304,128]{1,0:T(8,128)(2,1)S(1)} %sum.3), channel_id=1, source_target_pairs={{0,2},{2,4},{4,6},{6,0},{1,3},{3,5},{5,7},{7,1},{8,10},{10,12},{12... | collective-permute-start | bytes 233480 | tf_op jit(solution)/shard_map/ppermute | solution.py:224
  87.6 2.9 %collective-permute-done.15 = bf16[304,128]{1,0:T(8,128)(2,1)S(1)} collective-permute-done((bf16[304,128]{1,0:T(8,128)(2,1)S(1)}, bf16[304,128]{1,0:T(8,128)(2,1)S(1)}, u32[]{:S(2)}, u32[]{:S(2)}) %collective-permute-start.15) | collective-permute-done | bytes 77856 | tf_op jit(solution)/shard_map/ppermute | solution.py:224
  90.5 0.8 collective-permute-done.14
  91.8 1.1 collective-permute-start.17
  92.9 4.3 %collective-permute-done.19.refs_3_ = bf16[4,304,128]{2,1,0:T(8,128)(2,1)S(1)} collective-permute-done((bf16[4,304,128]{2,1,0:T(8,128)(2,1)S(1)}, bf16[4,304,128]{2,1,0:T(8,128)(2,1)S(1)}, u32[]{:S(2)}, u32[]{:S(2)}) %collective-permute-start.19) | collective-permute-done | bytes 311328 | tf_op jit(solution)/shard_map/ppermute | solution.py:224
  97.2 1.7 %collective-permute-done.18.refs_2_ = bf16[4,304,128]{2,1,0:T(8,128)(2,1)S(1)} collective-permute-done((bf16[4,304,128]{2,1,0:T(8,128)(2,1)S(1)}, bf16[4,304,128]{2,1,0:T(8,128)(2,1)S(1)}, u32[]{:S(2)}, u32[]{:S(2)}) %collective-permute-start.18) | collective-permute-done | bytes 311328 | tf_op jit(solution)/shard_map/ppermute | solution.py:224
  98.9 7.6 %collective-permute-done.17.refs_1_ = bf16[4,304,128]{2,1,0:T(8,128)(2,1)S(1)} collective-permute-done((bf16[4,304,128]{2,1,0:T(8,128)(2,1)S(1)}, bf16[4,304,128]{2,1,0:T(8,128)(2,1)S(1)}, u32[]{:S(2)}, u32[]{:S(2)}) %collective-permute-start.17) | collective-permute-done | bytes 311328 | tf_op jit(solution)/shard_map/ppermute | solution.py:224
  106.5 13.9 %polynomial.1 = f32[224,1024]{1,0:T(8,128)S(1)} custom-call(s32[2]{0:T(128)S(1)} %pad_add_fusion.place_ref, f32[224,1024]{1,0:T(8,128)} %get-tuple-element.26.moment_away_ref, bf16[4,304,128]{2,1,0:T(8,128)(2,1)S(1)} %pad_maximum_fusion.1.refs_0_, bf16[4,304,128]{2,1,0:T(8,128)(2,1)S(1)} %collective-permute-done.17.refs_1_, ...), custom_call_target="tpu_custom_call" | custom-call | tf_op jit(solution)/shard_map/polynomial/pallas_call | solution.py:208
  120.5 22.7 %all-gather.2 = f16[1792,1024]{1,0:T(8,128)(2,1)S(1)} all-gather(f16[224,1024]{1,0:T(8,128)(2,1)S(1)} %multiply_convert_fusion), channel_id=2, replica_groups=mesh['y'=4,'core'=2,'x'=4,'z_pair'=4,'z_low'=2] {'y','core'}, dimensions={0}, use_global_device_ids=true | all-gather | bytes 4128768 | tf_op jit(solution)/shard_map/all_gather | solution.py:293
  143.1 4.1 %convert_multiply_fusion = f32[1792,1024]{1,0:T(8,128)} fusion(f16[1792,1024]{1,0:T(8,128)(2,1)S(1)} %all-gather.2), kind=kLoop, calls=%fused_computation | loop fusion | flops 3670016 | bytes 11010048 | tf_op jit(solution)/shard_map/mul | solution.py:294
  (32 shorter events, 2.9 us)
Async XLA Ops:
  0.6 28.8 %copy-start = (s32[8,8]{1,0:T(8,128)S(1)}, s32[8,8]{1,0:T(8,128)}, u32[]{:S(2)}) copy-start(s32[8,8]{1,0:T(8,128)} %param.7) | copy-start | bytes 772
  2.8 0.7 copy-start.1
  3.5 5.9 %collective-permute-start = (bf16[4,224,128]{2,1,0:T(8,128)(2,1)S(1)}, bf16[4,224,128]{2,1,0:T(8,128)(2,1)S(1)}, u32[]{:S(2)}, u32[]{:S(2)}) collective-permute-start(bf16[4,224,128]{2,1,0:T(8,128)(2,1)S(1)} %get-tuple-element.16), channel_id=1, source_target_pairs={{0,32},{32,0},{1,33},{33,1},{2,34},{34,2},{3,35},{35,3},{4,36},{36... | collective-permute-start | bytes 688136 | tf_op jit(solution)/shard_map/ppermute | solution.py:224
  6.8 10.9 %collective-permute-start.4 = (bf16[224,768]{1,0:T(8,128)(2,1)S(1)}, bf16[224,768]{1,0:T(8,128)(2,1)S(1)}, u32[]{:S(2)}, u32[]{:S(2)}) collective-permute-start(bf16[224,768]{1,0:T(8,128)(2,1)S(1)} %get-tuple-element.17), channel_id=1, source_target_pairs={{0,8},{8,16},{16,24},{24,0},{1,9},{9,17},{17,25},{25,1},{2,10},{10... | collective-permute-start | bytes 1032200 | tf_op jit(solution)/shard_map/ppermute | solution.py:224
  6.8 10.9 %collective-permute-start.5 = (bf16[224,768]{1,0:T(8,128)(2,1)S(1)}, bf16[224,768]{1,0:T(8,128)(2,1)S(1)}, u32[]{:S(2)}, u32[]{:S(2)}) collective-permute-start(bf16[224,768]{1,0:T(8,128)(2,1)S(1)} %get-tuple-element.18), channel_id=1, source_target_pairs={{0,24},{8,0},{16,8},{24,16},{1,25},{9,1},{17,9},{25,17},{2,26},{10... | collective-permute-start | bytes 1032200 | tf_op jit(solution)/shard_map/ppermute | solution.py:224
  9.5 6.0 %collective-permute-start.1 = (bf16[2,224,128]{2,1,0:T(8,128)(2,1)S(1)}, bf16[2,224,128]{2,1,0:T(8,128)(2,1)S(1)}, u32[]{:S(2)}, u32[]{:S(2)}) collective-permute-start(bf16[2,224,128]{2,1,0:T(8,128)(2,1)S(1)} %get-tuple-element.29), channel_id=1, source_target_pairs={{0,64},{64,128},{128,192},{192,0},{1,65},{65,129},{129,193},{193,1... | collective-permute-start | bytes 344072 | tf_op jit(solution)/shard_map/ppermute | solution.py:224
  9.6 7.3 %collective-permute-start.2 = (bf16[2,224,128]{2,1,0:T(8,128)(2,1)S(1)}, bf16[2,224,128]{2,1,0:T(8,128)(2,1)S(1)}, u32[]{:S(2)}, u32[]{:S(2)}) collective-permute-start(bf16[2,224,128]{2,1,0:T(8,128)(2,1)S(1)} %get-tuple-element.30), channel_id=1, source_target_pairs={{0,128},{64,192},{128,0},{192,64},{1,129},{65,193},{129,1},{193,65... | collective-permute-start | bytes 344072 | tf_op jit(solution)/shard_map/ppermute | solution.py:224
  11.8 5.9 %collective-permute-start.3 = (bf16[2,224,128]{2,1,0:T(8,128)(2,1)S(1)}, bf16[2,224,128]{2,1,0:T(8,128)(2,1)S(1)}, u32[]{:S(2)}, u32[]{:S(2)}) collective-permute-start(bf16[2,224,128]{2,1,0:T(8,128)(2,1)S(1)} %get-tuple-element.31), channel_id=1, source_target_pairs={{0,192},{64,0},{128,64},{192,128},{1,193},{65,1},{129,65},{193,129... | collective-permute-start | bytes 344072 | tf_op jit(solution)/shard_map/ppermute | solution.py:224
  17.7 0.7 copy-start.2
  17.7 0.9 copy-start.3
  18.6 37.6 %all-to-all-start = ((bf16[8,128,1024]{2,1,0:T(8,128)(2,1)}), bf16[8,128,1024]{2,1,0:T(8,128)(2,1)S(1)}, u32[]{:S(2)}, u32[]{:S(2)}) async-start(bf16[8,128,1024]{2,1,0:T(8,128)(2,1)} %param.4), calls=%async_computation | async-start | bytes 4194304 | tf_op jit(solution)/shard_map/all_to_all | solution.py:254
  24.3 31.9 %collective-permute-start.8 = (bf16[8,224,128]{2,1,0:T(8,128)(2,1)S(1)}, bf16[8,224,128]{2,1,0:T(8,128)(2,1)S(1)}, u32[]{:S(2)}, u32[]{:S(2)}) collective-permute-start(bf16[8,224,128]{2,1,0:T(8,128)(2,1)S(1)} %pad_maximum_fusion.tokens_ref), channel_id=1, source_target_pairs={{0,24},{8,0},{16,8},{24,16},{1,25},{9,1},{17,9},{25,17},{2,26},{10... | collective-permute-start | bytes 1376264 | tf_op jit(solution)/shard_map/ppermute | solution.py:224
  25.6 30.6 %collective-permute-start.7 = (bf16[8,224,128]{2,1,0:T(8,128)(2,1)S(1)}, bf16[8,224,128]{2,1,0:T(8,128)(2,1)S(1)}, u32[]{:S(2)}, u32[]{:S(2)}) collective-permute-start(bf16[8,224,128]{2,1,0:T(8,128)(2,1)S(1)} %pad_maximum_fusion.tokens_ref), channel_id=1, source_target_pairs={{0,16},{8,24},{16,0},{24,8},{1,17},{9,25},{17,1},{25,9},{2,18},{10... | collective-permute-start | bytes 1376264 | tf_op jit(solution)/shard_map/ppermute | solution.py:224
  25.6 30.6 %collective-permute-start.6 = (bf16[8,224,128]{2,1,0:T(8,128)(2,1)S(1)}, bf16[8,224,128]{2,1,0:T(8,128)(2,1)}, u32[]{:S(2)}, u32[]{:S(2)}) collective-permute-start(bf16[8,224,128]{2,1,0:T(8,128)(2,1)S(1)} %pad_maximum_fusion.tokens_ref), channel_id=1, source_target_pairs={{0,8},{8,16},{16,24},{24,0},{1,9},{9,17},{17,25},{25,1},{2,10},{10... | collective-permute-start | bytes 1376264 | tf_op jit(solution)/shard_map/ppermute | solution.py:224
  26.3 29.9 %collective-permute-start.9 = (bf16[224,768]{1,0:T(8,128)(2,1)}, bf16[224,768]{1,0:T(8,128)(2,1)}, u32[]{:S(2)}, u32[]{:S(2)}) collective-permute-start(bf16[224,768]{1,0:T(8,128)(2,1)} %copy-done.1), channel_id=1, source_target_pairs={{0,16},{8,24},{16,0},{24,8},{1,17},{9,25},{17,1},{25,9},{2,18},{10... | collective-permute-start | bytes 1032200 | tf_op jit(solution)/shard_map/ppermute | solution.py:224
  63.0 8.6 %collective-permute-start.12 = (bf16[304,128]{1,0:T(8,128)(2,1)S(1)}, bf16[304,128]{1,0:T(8,128)(2,1)S(1)}, u32[]{:S(2)}, u32[]{:S(2)}) collective-permute-start(bf16[304,128]{1,0:T(8,128)(2,1)S(1)} %get-tuple-element.32), channel_id=1, source_target_pairs={{0,6},{2,0},{4,2},{6,4},{1,7},{3,1},{5,3},{7,5},{8,14},{10,8},{12,... | collective-permute-start | bytes 233480 | tf_op jit(solution)/shard_map/ppermute | solution.py:224
  68.4 7.4 %collective-permute-start.11 = (bf16[304,128]{1,0:T(8,128)(2,1)S(1)}, bf16[304,128]{1,0:T(8,128)(2,1)S(1)}, u32[]{:S(2)}, u32[]{:S(2)}) collective-permute-start(bf16[304,128]{1,0:T(8,128)(2,1)S(1)} %get-tuple-element.33), channel_id=1, source_target_pairs={{0,4},{2,6},{4,0},{6,2},{1,5},{3,7},{5,1},{7,3},{8,12},{10,14},{12... | collective-permute-start | bytes 233480 | tf_op jit(solution)/shard_map/ppermute | solution.py:224
  69.5 7.3 %collective-permute-start.10 = (bf16[304,128]{1,0:T(8,128)(2,1)S(1)}, bf16[304,128]{1,0:T(8,128)(2,1)S(1)}, u32[]{:S(2)}, u32[]{:S(2)}) collective-permute-start(bf16[304,128]{1,0:T(8,128)(2,1)S(1)} %get-tuple-element.34), channel_id=1, source_target_pairs={{0,2},{2,4},{4,6},{6,0},{1,3},{3,5},{5,7},{7,1},{8,10},{10,12},{12... | collective-permute-start | bytes 233480 | tf_op jit(solution)/shard_map/ppermute | solution.py:224
  77.0 3.3 %collective-permute-start.13 = (bf16[304,128]{1,0:T(8,128)(2,1)S(1)}, bf16[304,128]{1,0:T(8,128)(2,1)S(1)}, u32[]{:S(2)}, u32[]{:S(2)}) collective-permute-start(bf16[304,128]{1,0:T(8,128)(2,1)S(1)} %sum.2.refs_0_), channel_id=1, source_target_pairs={{0,1},{1,0},{2,3},{3,2},{4,5},{5,4},{6,7},{7,6},{8,9},{9,8},{10,11... | collective-permute-start | bytes 233480 | tf_op jit(solution)/shard_map/ppermute | solution.py:224
  80.4 7.2 %collective-permute-start.16 = (bf16[304,128]{1,0:T(8,128)(2,1)S(1)}, bf16[304,128]{1,0:T(8,128)(2,1)S(1)}, u32[]{:S(2)}, u32[]{:S(2)}) collective-permute-start(bf16[304,128]{1,0:T(8,128)(2,1)S(1)} %sum.3), channel_id=1, source_target_pairs={{0,6},{2,0},{4,2},{6,4},{1,7},{3,1},{5,3},{7,5},{8,14},{10,8},{12,... | collective-permute-start | bytes 233480 | tf_op jit(solution)/shard_map/ppermute | solution.py:224
  83.2 7.3 %collective-permute-start.15 = (bf16[304,128]{1,0:T(8,128)(2,1)S(1)}, bf16[304,128]{1,0:T(8,128)(2,1)S(1)}, u32[]{:S(2)}, u32[]{:S(2)}) collective-permute-start(bf16[304,128]{1,0:T(8,128)(2,1)S(1)} %sum.3), channel_id=1, source_target_pairs={{0,4},{2,6},{4,0},{6,2},{1,5},{3,7},{5,1},{7,3},{8,12},{10,14},{12... | collective-permute-start | bytes 233480 | tf_op jit(solution)/shard_map/ppermute | solution.py:224
  85.3 6.0 %collective-permute-start.14 = (bf16[304,128]{1,0:T(8,128)(2,1)S(1)}, bf16[304,128]{1,0:T(8,128)(2,1)S(1)}, u32[]{:S(2)}, u32[]{:S(2)}) collective-permute-start(bf16[304,128]{1,0:T(8,128)(2,1)S(1)} %sum.3), channel_id=1, source_target_pairs={{0,2},{2,4},{4,6},{6,0},{1,3},{3,5},{5,7},{7,1},{8,10},{10,12},{12... | collective-permute-start | bytes 233480 | tf_op jit(solution)/shard_map/ppermute | solution.py:224
  91.4 5.8 %collective-permute-start.19 = (bf16[4,304,128]{2,1,0:T(8,128)(2,1)S(1)}, bf16[4,304,128]{2,1,0:T(8,128)(2,1)S(1)}, u32[]{:S(2)}, u32[]{:S(2)}) collective-permute-start(bf16[4,304,128]{2,1,0:T(8,128)(2,1)S(1)} %pad_maximum_fusion.1.refs_0_), channel_id=1, source_target_pairs={{0,24},{8,0},{16,8},{24,16},{1,25},{9,1},{17,9},{25,17},{2,26},{10... | collective-permute-start | bytes 933896 | tf_op jit(solution)/shard_map/ppermute | solution.py:224
  91.4 7.4 %collective-permute-start.18 = (bf16[4,304,128]{2,1,0:T(8,128)(2,1)S(1)}, bf16[4,304,128]{2,1,0:T(8,128)(2,1)S(1)}, u32[]{:S(2)}, u32[]{:S(2)}) collective-permute-start(bf16[4,304,128]{2,1,0:T(8,128)(2,1)S(1)} %pad_maximum_fusion.1.refs_0_), channel_id=1, source_target_pairs={{0,16},{8,24},{16,0},{24,8},{1,17},{9,25},{17,1},{25,9},{2,18},{10... | collective-permute-start | bytes 933896 | tf_op jit(solution)/shard_map/ppermute | solution.py:224
  91.8 14.7 %collective-permute-start.17 = (bf16[4,304,128]{2,1,0:T(8,128)(2,1)S(1)}, bf16[4,304,128]{2,1,0:T(8,128)(2,1)S(1)}, u32[]{:S(2)}, u32[]{:S(2)}) collective-permute-start(bf16[4,304,128]{2,1,0:T(8,128)(2,1)S(1)} %pad_maximum_fusion.1.refs_0_), channel_id=1, source_target_pairs={{0,8},{8,16},{16,24},{24,0},{1,9},{9,17},{17,25},{25,1},{2,10},{10... | collective-permute-start | bytes 933896 | tf_op jit(solution)/shard_map/ppermute | solution.py:224
